TPU v7x, 256 devices: a whole 4x4x8 slice. The times are simulated.
256 devices in a mesh: req: 64 (over y, z_hi, x, core), dec: 4 (over z_lo).
Axes of the slice: x: 4, y: 4, z: 8 (z_hi: 2, z_lo: 4; z = z_hi * 4 + z_lo), core: 2. Of those that a mesh axis runs over, the one named last changes fastest.
Arguments:
- queries: bfloat16 [32768, 2048], P('req', 'dec')
- keys: bfloat16 [32768, 2048], P('req', 'dec'), may hold values from -6 to 6
- values: bfloat16 [32768, 2048], P('req', 'dec'), may hold values from -6 to 6
- resid: bfloat16 [32768, 2048], P('req', 'dec'), may hold values from -6 to 6
- seg_ids: int32 [32768], P('req'), may hold values from -1 to 7, as said below
- out_weight: bfloat16 [2048, 2048], P('dec'), may hold values from -0.125 to 0.125
- norm_gain: float32 [2048], replicated, may hold values from 0.1 to 1.9
- adapter_down: bfloat16 [2048, 128], replicated, may hold values from -0.125 to 0.125
- adapter_up: bfloat16 [128, 4096], P(None, ('req', 'dec')), may hold values from -0.5 to 0.5
- gate_weight: bfloat16 [2048, 4096], P(None, ('req', 'dec')), may hold values from -0.125 to 0.125
- up_weight: bfloat16 [2048, 4096], P(None, ('req', 'dec')), may hold values from -0.125 to 0.125
- down_weight: bfloat16 [4096, 2048], P(('req', 'dec')), may hold values from -0.09375 to 0.09375
- row_order: int32 [64, 512], P('req'), may hold values from 0 to 511, each once within a row
- block_table: int32 [64, 8], P('req'), may hold values from 0 to 7, each once within a row
Outputs:
- block_out: bfloat16 [32768, 2048], P('req', 'dec')
- kv_cache: bfloat16 [512, 64, 4096], P(('req', 'dec'))
Inputs may be any that keep to these rules, and one draw needn't show every extreme that they name: `seg_ids`: within each index of req the live slots come first, grouped into requests whose numbers start at 0, rise by one from request to request and never fall, then come padding slots marked -1; some index of req holds one request that fills all its 512 slots, and when there is more than one index of req, some other index holds request numbers up to the stated most.
All inputs are finite; a program needn't handle non-finite values.
Results may differ from a plain program's by a relative error of at most 0.017.
Values may be sent and summed in bfloat16 or wider, within the bound.
A program may use at most 128 MiB of HBM per device.

v0:
```python
import jax
import jax.numpy as jnp
from jax import lax
from jax.sharding import PartitionSpec as P

HD = 128


def attend(query_rows, key_rows, value_rows, segment):
    row_count = query_rows.shape[0]
    head_count = query_rows.shape[1] // HD
    query_heads = query_rows.reshape(row_count, head_count, HD)
    key_heads = key_rows.reshape(row_count, head_count, HD)
    value_heads = value_rows.reshape(row_count, head_count, HD)
    scores = jnp.einsum(
        "qhd,khd->hqk", query_heads, key_heads, preferred_element_type=jnp.float32
    ) * HD ** (-0.5)
    position = jnp.arange(row_count)
    allowed = (
        (segment[:, None] == segment[None, :])
        & (position[None, :] <= position[:, None])
        & (segment[:, None] >= 0)
    )
    masked = jnp.where(allowed[None], scores, -1e30)
    highest = jnp.max(masked, axis=-1, keepdims=True)
    exponent = jnp.where(allowed[None], jnp.exp(masked - highest), 0.0)
    denominator = jnp.sum(exponent, axis=-1, keepdims=True)
    denominator = jnp.where(denominator > 0, denominator, 1.0)
    weights = (exponent / denominator).astype(jnp.bfloat16)
    result = jnp.einsum("hqk,khd->qhd", weights, value_heads, preferred_element_type=jnp.float32)
    return result.astype(jnp.bfloat16).reshape(row_count, head_count * HD)


def body(
    queries,
    keys,
    values,
    resid,
    seg_ids,
    out_weight,
    norm_gain,
    adapter_down,
    adapter_up,
    gate_weight,
    up_weight,
    down_weight,
    row_order,
    block_table,
):
    slot_count = queries.shape[0]
    features = keys.shape[1]
    block_count = block_table.shape[1]
    block_slots = slot_count // block_count
    table_row = block_table[0]
    placement = (jnp.arange(block_count)[:, None] == table_row[None, :]).astype(jnp.bfloat16)
    key_blocks = keys.reshape(block_count, block_slots, features)
    value_blocks = values.reshape(block_count, block_slots, features)
    ordered_keys = jnp.einsum(
        "tj,jbw->tbw", placement, key_blocks, preferred_element_type=jnp.float32
    ).astype(jnp.bfloat16)
    ordered_values = jnp.einsum(
        "tj,jbw->tbw", placement, value_blocks, preferred_element_type=jnp.float32
    ).astype(jnp.bfloat16)
    moved_keys, moved_values = (
        lax.all_to_all(ordered_keys, "dec", split_axis=0, concat_axis=2, tiled=True),
        lax.all_to_all(ordered_values, "dec", split_axis=0, concat_axis=2, tiled=True),
    )
    kv_cache = jnp.concatenate([moved_keys, moved_values], axis=2)
    attn = attend(queries, keys, values, seg_ids)
    partial_value = jnp.dot(attn, out_weight, preferred_element_type=jnp.float32).astype(
        jnp.bfloat16
    )
    head_total = lax.psum_scatter(partial_value, "dec", scatter_dimension=1, tiled=True).astype(
        jnp.float32
    )
    hidden = (resid.astype(jnp.float32) + head_total).astype(jnp.bfloat16)
    permuted = jnp.take(hidden, row_order[0], axis=0)
    whole_rows = lax.all_gather(permuted, "dec", axis=1, tiled=True)
    mixed_rows = lax.all_to_all(whole_rows, "req", split_axis=0, concat_axis=0, tiled=True)
    quarter = resid.shape[1]
    column = lax.dynamic_slice_in_dim(mixed_rows, lax.axis_index("dec") * quarter, quarter, 1)
    values_f = mixed_rows.astype(jnp.float32)
    scale = lax.rsqrt(jnp.mean(values_f * values_f, axis=-1, keepdims=True) + 1e-05)
    normed = (values_f * scale * norm_gain).astype(jnp.bfloat16)
    low_rank = jnp.dot(normed, adapter_down, preferred_element_type=jnp.float32).astype(
        jnp.bfloat16
    )
    operand = jnp.concatenate([normed, low_rank], axis=1)
    rank_width = adapter_down.shape[1]
    piece_width = gate_weight.shape[1]
    padding = jnp.zeros((rank_width, piece_width), jnp.bfloat16)
    stacked = jnp.stack(
        [
            jnp.concatenate([gate_weight, adapter_up], axis=0),
            jnp.concatenate([up_weight, padding], axis=0),
        ]
    )
    projected = jnp.einsum(
        "md,gdc->gmc",
        operand,
        lax.all_gather(stacked, "req", axis=2, tiled=True),
        preferred_element_type=jnp.float32,
    )
    hidden_units = (jax.nn.gelu(projected[0]) * projected[1]).astype(jnp.bfloat16)
    down_full = lax.all_gather(down_weight, "req", axis=0, tiled=True)
    down_part = jnp.dot(hidden_units, down_full, preferred_element_type=jnp.float32).astype(
        jnp.bfloat16
    )
    mlp_total = lax.psum_scatter(down_part, "dec", scatter_dimension=1, tiled=True).astype(
        jnp.float32
    )
    block_out = (column.astype(jnp.float32) + mlp_total).astype(jnp.bfloat16)
    return (block_out, kv_cache)


def solution(mesh):
    placed = (
        P("req", "dec"),
        P("req", "dec"),
        P("req", "dec"),
        P("req", "dec"),
        P("req"),
        P("dec", None),
        P(),
        P(),
        P(None, ("req", "dec")),
        P(None, ("req", "dec")),
        P(None, ("req", "dec")),
        P(("req", "dec"), None),
        P("req", None),
        P("req", None),
    )
    return jax.shard_map(
        body,
        mesh=mesh,
        in_specs=placed,
        out_specs=(P("req", "dec"), P(("req", "dec"), None, None)),
        check_vma=False,
    )
```

profile of v0, /device:TPU:33, one launch (start us, length us, event | category | flops | bytes accessed | tf_op | source)
XLA Modules:
  0.0 433.8 jit_solution(6591187465169870902)
XLA Ops:
  8.1 1.0 fusion.26
  9.0 1.9 fusion.27
  11.0 4.1 fusion.46
  15.3 2.6 fusion.19
  18.0 2.6 convolution_convert_fusion.1
  20.8 49.4 %reduce-scatter.3.cloned.1.call-done = bf16[512,512]{1,0:T(8,128)(2,1)} async-done(((bf16[512,2048]{1,0:T(8,128)(2,1)}), bf16[512,512]{1,0:T(8,128)(2,1)}) %reduce-scatter.3.cloned.1.call-update) | async-done | bytes 524304 | tf_op jit(solution)/shard_map/reduce_scatter | solution.py:73
  70.2 1.2 add_convert_fusion.1
  71.4 2.0 gather_fusion
  75.8 49.4 %all-gather.4.cloned.1.call-done = bf16[512,2048]{1,0:T(8,128)(2,1)} async-done(((bf16[512,512]{1,0:T(8,128)(2,1)}), bf16[512,2048]{1,0:T(8,128)(2,1)}) %all-gather.4.cloned.1.call-update) | async-done | bytes 2097168 | tf_op jit(solution)/shard_map/all_gather | solution.py:78
  125.1 67.0 %all_to_all.48 = bf16[64,8,2048]{2,1,0:T(8,128)(2,1)S(1)} all-to-all(bf16[64,8,2048]{2,1,0:T(8,128)(2,1)} %bitcast.72), channel_id=1, replica_groups=mesh['req'=64,'dec'=4] {'req'}, dimensions={0} | all-to-all | bytes 4194304 | tf_op jit(solution)/shard_map/all_to_all | solution.py:79
  192.1 1.3 copy-done.1
  194.0 2.1 multiply_convert_fusion
  196.2 1.3 copy-done.2
  198.5 64.6 %all-gather.6.cloned.1.call-done = bf16[2,2176,1024]{1,2,0:T(8,128)(2,1)} async-done(((bf16[2,2176,16]{1,2,0:T(8,128)(2,1)}), bf16[2,2176,1024]{1,2,0:T(8,128)(2,1)}) %all-gather.6.cloned.1.call-update) | async-done | bytes 8912912 | tf_op jit(solution)/shard_map/all_gather | solution.py:101
  263.0 10.6 %fusion.5 = f32[2,512,1024]{1,2,0:T(8,128)} fusion(bf16[2,2176,1024]{1,2,0:T(8,128)(2,1)} %all-gather.6.cloned.1.call-done, bf16[512,128]{1,0:T(8,128)(2,1)S(1)} %copy.36, bf16[512,2048]{1,0:T(8,128)(2,1)} %copy-done.2), kind=kOutput, calls=%fused_computation.15 | convolution fusion | flops 4567859200 | bytes 15335424 | tf_op jit(solution)/shard_map/md,gdc->gmc/dot_general | solution.py:98
  273.6 79.4 %all-gather.8.cloned.1.call-done = bf16[1024,2048]{1,0:T(8,128)(2,1)} async-done(((bf16[16,2048]{1,0:T(8,128)(2,1)}), bf16[1024,2048]{1,0:T(8,128)(2,1)}) %all-gather.8.cloned.1.call-update) | async-done | bytes 4194320 | tf_op jit(solution)/shard_map/all_gather | solution.py:105
  353.0 7.4 %convolution_convert_fusion = bf16[512,2048]{1,0:T(8,128)(2,1)} fusion(bf16[1024,2048]{1,0:T(8,128)(2,1)} %all-gather.8.cloned.1.call-done, f32[2,512,1024]{1,2,0:T(8,128)} %fusion.5), kind=kOutput, calls=%fused_computation.9 | convolution fusion | flops 2153775104 | bytes 10485760 | tf_op jit(solution)/shard_map/dot_general | solution.py:106
  361.8 4.4 %all-to-all-start.1 = ((bf16[8,64,512]{2,1,0:T(8,128)(2,1)}), bf16[8,64,512]{2,1,0:T(8,128)(2,1)S(1)}, u32[]{:S(2)}, u32[]{:S(2)}) async-start(bf16[8,64,512]{2,1,0:T(8,128)(2,1)} %copy.38), calls=%async_computation.3 | async-start | bytes 1048576 | tf_op jit(solution)/shard_map/all_to_all | solution.py:65
  367.5 22.7 %all-to-all-done.1 = bf16[8,64,512]{2,1,0:T(8,128)(2,1)S(1)} async-done(((bf16[8,64,512]{2,1,0:T(8,128)(2,1)}), bf16[8,64,512]{2,1,0:T(8,128)(2,1)S(1)}, u32[]{:S(2)}, u32[]{:S(2)}) %all-to-all-start.1) | async-done | bytes 524320 | tf_op jit(solution)/shard_map/all_to_all | solution.py:65
  390.3 8.0 %all-to-all-start.2 = ((bf16[8,64,512]{2,1,0:T(8,128)(2,1)}), bf16[8,64,512]{2,1,0:T(8,128)(2,1)S(1)}, u32[]{:S(2)}, u32[]{:S(2)}) async-start(bf16[8,64,512]{2,1,0:T(8,128)(2,1)} %copy.41), calls=%async_computation.4 | async-start | bytes 1048576 | tf_op jit(solution)/shard_map/all_to_all | solution.py:66
  399.1 21.5 %all-to-all-done.2 = bf16[8,64,512]{2,1,0:T(8,128)(2,1)S(1)} async-done(((bf16[8,64,512]{2,1,0:T(8,128)(2,1)}), bf16[8,64,512]{2,1,0:T(8,128)(2,1)S(1)}, u32[]{:S(2)}, u32[]{:S(2)}) %all-to-all-start.2) | async-done | bytes 524320 | tf_op jit(solution)/shard_map/all_to_all | solution.py:66
  420.7 2.1 pad_maximum_fusion
  422.8 2.4 reduce-scatter.5.cloned.1.call-done
  425.2 2.1 add_convert_fusion
  (56 shorter events, 8.7 us)
Async XLA Ops:
  7.2 10.8 %copy-start = (bf16[512,2048]{1,0:T(8,128)(2,1)S(1)}, bf16[512,2048]{1,0:T(8,128)(2,1)}, u32[]{:S(2)}) copy-start(bf16[512,2048]{1,0:T(8,128)(2,1)} %param.19) | copy-start | bytes 6291460
  7.2 63.0 %reduce-scatter.3.cloned.1.call-start = ((), (), s32[]{:S(2)}) async-start(), calls=%async_computation.5 | async-start | bytes 2621440 | tf_op jit(solution)/shard_map/reduce_scatter | solution.py:73
  10.9 4.1 copy-start.4
  18.0 2.8 copy-start.11
  18.0 52.3 %copy-start.6 = (bf16[512,512]{1,0:T(8,128)(2,1)S(1)}, bf16[512,512]{1,0:T(8,128)(2,1)}, u32[]{:S(2)}) copy-start(bf16[512,512]{1,0:T(8,128)(2,1)} %param.17) | copy-start | bytes 1572868
  20.6 53.8 %copy-start.8 = (bf16[2048,16]{0,1:T(8,128)(2,1)S(1)}, bf16[2048,16]{0,1:T(8,128)(2,1)}, u32[]{:S(2)}) copy-start(bf16[2048,16]{0,1:T(8,128)(2,1)} %param.23) | copy-start | bytes 196612
  20.7 53.8 %copy-start.9 = (bf16[2048,16]{0,1:T(8,128)(2,1)S(1)}, bf16[2048,16]{0,1:T(8,128)(2,1)}, u32[]{:S(2)}) copy-start(bf16[2048,16]{0,1:T(8,128)(2,1)} %param.24) | copy-start | bytes 196612
  20.7 53.8 %copy-start.12 = (bf16[128,16]{0,1:T(8,128)(2,1)S(1)}, bf16[128,16]{0,1:T(8,128)(2,1)}, u32[]{:S(2)}) copy-start(bf16[128,16]{0,1:T(8,128)(2,1)} %param.22) | copy-start | bytes 12292
  20.7 104.5 %all-gather.4.cloned.1.call-start = ((), (), s32[]{:S(2)}) async-start(), calls=%async_computation.6 | async-start | bytes 2621440 | tf_op jit(solution)/shard_map/all_gather | solution.py:78
  73.4 120.7 %copy-start.10 = (f32[2048]{0:T(1024)S(1)}, f32[2048]{0:T(1024)}, u32[]{:S(2)}) copy-start(f32[2048]{0:T(1024)} %param.20) | copy-start | bytes 24580
  74.4 188.7 %all-gather.6.cloned.1.call-start = ((), (), s32[]{:S(2)}) async-start(), calls=%async_computation.7 | async-start | bytes 9052160 | tf_op jit(solution)/shard_map/all_gather | solution.py:101
  75.2 277.8 %all-gather.8.cloned.1.call-start = ((), (), s32[]{:S(2)}) async-start(), calls=%async_computation.8 | async-start | bytes 4259840 | tf_op jit(solution)/shard_map/all_gather | solution.py:105
  75.7 349.4 %reduce-scatter.5.cloned.1.call-start = ((), (), s32[]{:S(2)}) async-start(), calls=%async_computation.9 | async-start | bytes 2621440 | tf_op jit(solution)/shard_map/reduce_scatter | solution.py:109
  192.1 1.3 copy-start.1
  193.4 4.1 copy-start.7
  196.2 1.3 copy-start.2
  273.6 86.8 %copy-start.3 = (bf16[512,512]{1,0:T(8,128)(2,1)S(1)}, bf16[512,512]{1,0:T(8,128)(2,1)}, u32[]{:S(2)}) copy-start(bf16[512,512]{1,0:T(8,128)(2,1)} %param.15) | copy-start | bytes 1572868
  273.6 86.8 %copy-start.13 = (s32[1,8]{1,0:T(1,128)S(1)}, s32[1,8]{1,0:T(1,128)}, u32[]{:S(2)}) copy-start(s32[1,8]{1,0:T(1,128)} %param.27) | copy-start | bytes 100
  360.4 5.8 %copy-start.5 = (bf16[512,512]{1,0:T(8,128)(2,1)S(1)}, bf16[512,512]{1,0:T(8,128)(2,1)}, u32[]{:S(2)}) copy-start(bf16[512,512]{1,0:T(8,128)(2,1)} %param.16) | copy-start | bytes 1572868
  361.8 28.5 %all-to-all-start.1 = ((bf16[8,64,512]{2,1,0:T(8,128)(2,1)}), bf16[8,64,512]{2,1,0:T(8,128)(2,1)S(1)}, u32[]{:S(2)}, u32[]{:S(2)}) async-start(bf16[8,64,512]{2,1,0:T(8,128)(2,1)} %copy.38), calls=%async_computation.3 | async-start | bytes 1048576 | tf_op jit(solution)/shard_map/all_to_all | solution.py:65
  390.3 30.4 %all-to-all-start.2 = ((bf16[8,64,512]{2,1,0:T(8,128)(2,1)}), bf16[8,64,512]{2,1,0:T(8,128)(2,1)S(1)}, u32[]{:S(2)}, u32[]{:S(2)}) async-start(bf16[8,64,512]{2,1,0:T(8,128)(2,1)} %copy.41), calls=%async_computation.4 | async-start | bytes 1048576 | tf_op jit(solution)/shard_map/all_to_all | solution.py:66
Sparse Core Ops, SparseCore 0:
  20.8 49.4 reduce-scatter.2
  74.5 50.6 all-gather.3
  129.5 133.5 all-gather.5
  266.5 86.4 all-gather.7
  360.5 64.5 reduce-scatter.4
where the time goes:
time: 436 us; the launch traced here: 434 us
  waiting for transfers between devices  290 us (67%)
  blocking collectives  67 us (15%)
  matrix products  26.7 us (6%)
  other arithmetic  15.6 us (4%)
  between operations  14 us (3%)
  starting transfers between devices  12.6 us (3%)
  local copies, waits for them, and re-layouts  7.92 us (2%)
    all_gather x1, waiting for transfers between devices, body(): down_full = lax.all_gather(down_weight, 'req', axis=0, tiled=True)  79.4 us
    all_to_all x1, blocking collectives, body(): lax.all_to_all(whole_rows, 'req', split_axis=0, concat_axis=0, tiled=True)  67 us
    all_gather x1, waiting for transfers between devices, body(): lax.all_gather(stacked, 'req', axis=2, tiled=True)  64.6 us
    reduce_scatter x1, waiting for transfers between devices, body(): lax.psum_scatter(partial_value, 'dec', scatter_dimension=1, tiled=True)  49.4 us
    all_gather x1, waiting for transfers between devices, body(): whole_rows = lax.all_gather(permuted, 'dec', axis=1, tiled=True)  49.4 us
    all_to_all x1, waiting for transfers between devices, body(): lax.all_to_all(ordered_keys, 'dec', split_axis=0, concat_axis=2, tiled=True)  22.7 us
    all_to_all x1, waiting for transfers between devices, body(): lax.all_to_all(ordered_values, 'dec', split_axis=0, concat_axis=2, tiled=...  21.5 us
    dot_general x1, matrix products, body(): jnp.einsum('md,gdc->gmc', operand, lax.all_gather(stacked, 'req', axis=2,...  10.6 us
  transfers between devices with their start and end apart: 7, of which 7 were waited for; matrix products, arithmetic and copies ran while one was open for 5% of the time, Pallas kernels for 0%

commit v1 on v0

v1 whole, which is shorter than its diff:
```python
import jax
import jax.numpy as jnp
from jax import lax
from jax.sharding import PartitionSpec as P

HD = 128


def attend(query_rows, key_rows, value_rows, segment):
    row_count = query_rows.shape[0]
    head_count = query_rows.shape[1] // HD
    query_heads = query_rows.reshape(row_count, head_count, HD)
    key_heads = key_rows.reshape(row_count, head_count, HD)
    value_heads = value_rows.reshape(row_count, head_count, HD)
    scores = jnp.einsum(
        "qhd,khd->hqk", query_heads, key_heads, preferred_element_type=jnp.float32
    ) * HD ** (-0.5)
    position = jnp.arange(row_count)
    allowed = (
        (segment[:, None] == segment[None, :])
        & (position[None, :] <= position[:, None])
        & (segment[:, None] >= 0)
    )
    masked = jnp.where(allowed[None], scores, -1e30)
    highest = jnp.max(masked, axis=-1, keepdims=True)
    exponent = jnp.where(allowed[None], jnp.exp(masked - highest), 0.0)
    denominator = jnp.sum(exponent, axis=-1, keepdims=True)
    denominator = jnp.where(denominator > 0, denominator, 1.0)
    weights = (exponent / denominator).astype(jnp.bfloat16)
    result = jnp.einsum("hqk,khd->qhd", weights, value_heads, preferred_element_type=jnp.float32)
    return result.astype(jnp.bfloat16).reshape(row_count, head_count * HD)


def reduce_over_dec(part, dec_count):
    rows = part.shape[0]
    quarter = part.shape[1] // dec_count
    pieces = part.reshape(rows, dec_count, quarter).transpose(1, 0, 2)
    got = lax.all_to_all(pieces, "dec", split_axis=0, concat_axis=0, tiled=True)
    return jnp.sum(got.astype(jnp.float32), axis=0)


def body(
    queries,
    keys,
    values,
    resid,
    seg_ids,
    out_weight,
    norm_gain,
    adapter_down,
    adapter_up,
    gate_weight,
    up_weight,
    down_weight,
    row_order,
    block_table,
):
    dec_count = out_weight.shape[1] // out_weight.shape[0]
    features = keys.shape[1]
    quarter = resid.shape[1]
    model_width = down_weight.shape[1]

    gate_up_local = jnp.stack([gate_weight.T, up_weight.T])
    gate_up = lax.all_gather(gate_up_local, "req", axis=1, tiled=True)
    down_adapter_local = jnp.concatenate([down_weight, adapter_up.T], axis=1)
    down_adapter = lax.all_gather(down_adapter_local, "req", axis=0, tiled=True)

    slot_count = keys.shape[0]
    block_count = block_table.shape[1]
    block_slots = slot_count // block_count
    table_row = block_table[0]
    placement = (jnp.arange(block_count)[:, None] == table_row[None, :]).astype(jnp.bfloat16)
    both = jnp.stack(
        [
            keys.reshape(block_count, block_slots, features),
            values.reshape(block_count, block_slots, features),
        ],
        axis=2,
    )
    ordered = jnp.einsum(
        "tj,jbkw->tbkw", placement, both, preferred_element_type=jnp.float32
    ).astype(jnp.bfloat16)
    per_dev = block_count // dec_count
    ordered = ordered.reshape(dec_count, per_dev, block_slots, 2, features)
    moved = lax.all_to_all(ordered, "dec", split_axis=0, concat_axis=0, tiled=True)
    kv_cache = moved.transpose(1, 2, 3, 0, 4).reshape(per_dev, block_slots, 2 * dec_count * features)

    attn = attend(queries, keys, values, seg_ids)
    partial_value = jnp.dot(attn, out_weight, preferred_element_type=jnp.float32).astype(
        jnp.bfloat16
    )
    head_total = reduce_over_dec(partial_value, dec_count)
    hidden = (resid.astype(jnp.float32) + head_total).astype(jnp.bfloat16)

    permuted = jnp.take(hidden, row_order[0], axis=0)
    cap = permuted.shape[0]
    req_n = gate_up.shape[1] // gate_weight.shape[1]
    per_group = cap // req_n
    column = lax.all_to_all(
        permuted.reshape(req_n, per_group, quarter), "req", split_axis=0, concat_axis=0, tiled=True
    ).reshape(cap, quarter)
    spread = jnp.broadcast_to(column[None], (dec_count, cap, quarter))
    quarters = lax.all_to_all(spread, "dec", split_axis=0, concat_axis=0, tiled=True)
    mixed_rows = quarters.transpose(1, 0, 2).reshape(cap, dec_count * quarter)

    values_f = mixed_rows.astype(jnp.float32)
    scale = lax.rsqrt(jnp.mean(values_f * values_f, axis=-1, keepdims=True) + 1e-05)
    normed = (values_f * scale * norm_gain).astype(jnp.bfloat16)
    low_rank = jnp.dot(normed, adapter_down, preferred_element_type=jnp.float32).astype(
        jnp.bfloat16
    )
    contract = (((1,), (1,)), ((), ()))
    gate = lax.dot_general(
        normed, gate_up[0], contract, preferred_element_type=jnp.float32
    ) + lax.dot_general(
        low_rank, down_adapter[:, model_width:], contract, preferred_element_type=jnp.float32
    )
    up = lax.dot_general(normed, gate_up[1], contract, preferred_element_type=jnp.float32)
    hidden_units = (jax.nn.gelu(gate) * up).astype(jnp.bfloat16)
    down_part = jnp.dot(
        hidden_units, down_adapter[:, :model_width], preferred_element_type=jnp.float32
    ).astype(jnp.bfloat16)
    mlp_total = reduce_over_dec(down_part, dec_count)
    block_out = (column.astype(jnp.float32) + mlp_total).astype(jnp.bfloat16)
    return (block_out, kv_cache)


def solution(mesh):
    placed = (
        P("req", "dec"),
        P("req", "dec"),
        P("req", "dec"),
        P("req", "dec"),
        P("req"),
        P("dec", None),
        P(),
        P(),
        P(None, ("req", "dec")),
        P(None, ("req", "dec")),
        P(None, ("req", "dec")),
        P(("req", "dec"), None),
        P("req", None),
        P("req", None),
    )
    return jax.shard_map(
        body,
        mesh=mesh,
        in_specs=placed,
        out_specs=(P("req", "dec"), P(("req", "dec"), None, None)),
        check_vma=False,
    )
```

time: 436 us -> 336 us (0.77)
  waiting for transfers between devices: 290 us -> 166 us
  blocking collectives: 67 us -> 33.2 us
  starting transfers between devices: 12.6 us -> 40.6 us
  local copies, waits for them, and re-layouts: 7.92 us -> 25.9 us
  other arithmetic: 15.6 us -> 24.4 us
    all_gather x3 -> x2, waiting for transfers between devices: 193 us -> 32.4 us  [the longest x1 32.4 us: body(): gate_up = lax.all_gather(gate_up_local, 'req', axis=1, tiled=True)]
    all_to_all x2 -> x4, waiting for transfers between devices: 44.2 us -> 133 us  [the longest x2 87.2 us: reduce_over_dec(): got = lax.all_to_all(pieces, 'dec', split_axis=0, concat_axis=0, tiled=True)]
    reduce_scatter x2 -> x0, waiting for transfers between devices: 51.8 us -> none  [the longest x1 49.4 us: body(): lax.psum_scatter(partial_value, 'dec', scatter_dimension=1, tiled=True)]
    all_to_all x1, blocking collectives: 67 us -> 33.2 us  [body(): lax.all_to_all(permuted.reshape(req_n, per_group, quarter), 'req', split_...]
    all_to_all x2 -> x4, starting transfers between devices: 12.4 us -> 40.6 us  [the longest x2 25.7 us: reduce_over_dec(): got = lax.all_to_all(pieces, 'dec', split_axis=0, concat_axis=0, tiled=True)]
    reshape x0 -> x6, local copies, waits for them, and re-layouts: none -> 13.4 us  [the longest x2 5.15 us: body(): ordered = ordered.reshape(dec_count, per_dev, block_slots, 2, features)]
    dot_general x5 -> x4, matrix products: 19.6 us -> 24.2 us  [the longest x1 11.6 us: body(): jnp.dot(hidden_units, down_adapter[:, :model_width], preferred_element_ty...]
  transfers between devices with their start and end apart: 7 -> 6, of which waited for: 7 -> 4; matrix products, arithmetic and copies ran while one was open for 5% -> 22% of each run, Pallas kernels for 0% -> 0%
where the time goes in v1:
time: 336 us; the launch traced here: 331 us
  waiting for transfers between devices  166 us (49%)
  starting transfers between devices  40.6 us (12%)
  blocking collectives  33.2 us (10%)
  matrix products  26.7 us (8%)
  local copies, waits for them, and re-layouts  25.9 us (8%)
  other arithmetic  24.4 us (7%)
  between operations  14.2 us (4%)
    all_to_all x2, waiting for transfers between devices, reduce_over_dec(): got = lax.all_to_all(pieces, 'dec', split_axis=0, concat_axis=0, tiled=True)  87.2 us
    all_to_all x1, waiting for transfers between devices, body(): lax.all_to_all(spread, 'dec', split_axis=0, concat_axis=0, tiled=True)  46.1 us
    all_to_all x1, blocking collectives, body(): lax.all_to_all(permuted.reshape(req_n, per_group, quarter), 'req', split_...  33.2 us
    all_gather x1, waiting for transfers between devices, body(): gate_up = lax.all_gather(gate_up_local, 'req', axis=1, tiled=True)  32.4 us
    all_to_all x2, starting transfers between devices, reduce_over_dec(): got = lax.all_to_all(pieces, 'dec', split_axis=0, concat_axis=0, tiled=True)  25.7 us
    dot_general x1, matrix products, body(): jnp.dot(hidden_units, down_adapter[:, :model_width], preferred_element_ty...  11.6 us
    all_to_all x1, starting transfers between devices, body(): lax.all_to_all(spread, 'dec', split_axis=0, concat_axis=0, tiled=True)  7.78 us
    all_to_all x1, starting transfers between devices, body(): lax.all_to_all(ordered, 'dec', split_axis=0, concat_axis=0, tiled=True)  7.12 us
  transfers between devices with their start and end apart: 6, of which 4 were waited for; matrix products, arithmetic and copies ran while one was open for 22% of the time, Pallas kernels for 0%

profile of v1, /device:TPU:33, one launch (start us, length us, event | category | flops | bytes accessed | tf_op | source)
XLA Modules:
  0.0 330.7 jit_solution(6583664212031384983)
XLA Ops:
  10.5 2.0 copy.52
  15.0 2.4 fusion.47
  20.6 5.6 %all-to-all-start = ((bf16[4,512,512]{2,1,0:T(8,128)(2,1)}), bf16[4,512,512]{2,1,0:T(8,128)(2,1)}, u32[]{:S(2)}, u32[]{:S(2)}) async-start(bf16[4,512,512]{2,1,0:T(8,128)(2,1)} %bitcast.87), calls=%async_computation | async-start | bytes 4194304 | tf_op jit(solution)/shard_map/all_to_all | solution.py:38
  27.5 48.0 %all-to-all-done = bf16[4,512,512]{2,1,0:T(8,128)(2,1)} async-done(((bf16[4,512,512]{2,1,0:T(8,128)(2,1)}), bf16[4,512,512]{2,1,0:T(8,128)(2,1)}, u32[]{:S(2)}, u32[]{:S(2)}) %all-to-all-start) | async-done | bytes 2097184 | tf_op jit(solution)/shard_map/all_to_all | solution.py:38
  78.7 2.6 gather_fusion
  82.5 33.2 %all_to_all.25 = bf16[64,8,512]{2,1,0:T(8,128)(2,1)S(1)} all-to-all(bf16[64,8,512]{2,1,0:T(8,128)(2,1)S(1)} %bitcast_select_fusion), channel_id=1, replica_groups=mesh['req'=64,'dec'=4] {'req'}, dimensions={0} | all-to-all | bytes 1048576 | tf_op jit(solution)/shard_map/all_to_all | solution.py:99
  116.7 2.5 broadcast_in_dim.55
  119.3 7.8 %all-to-all-start.2 = ((bf16[4,512,512]{1,2,0:T(8,128)(2,1)}), bf16[4,512,512]{1,2,0:T(8,128)(2,1)}, u32[]{:S(2)}, u32[]{:S(2)}) async-start(bf16[4,512,512]{1,2,0:T(8,128)(2,1)} %broadcast_in_dim.55), calls=%async_computation.2 | async-start | bytes 4194304 | tf_op jit(solution)/shard_map/all_to_all | solution.py:103
  130.1 2.2 reshape.173
  132.3 2.9 copy.48
  135.3 46.1 %all-to-all-done.2 = bf16[4,512,512]{1,2,0:T(8,128)(2,1)} async-done(((bf16[4,512,512]{1,2,0:T(8,128)(2,1)}), bf16[4,512,512]{1,2,0:T(8,128)(2,1)}, u32[]{:S(2)}, u32[]{:S(2)}) %all-to-all-start.2) | async-done | bytes 2097184 | tf_op jit(solution)/shard_map/all_to_all | solution.py:103
  181.4 7.1 %all-to-all-start.4 = ((bf16[4,2,64,2,512]{4,1,3,2,0:T(2,128)(2,1)}), bf16[4,2,64,2,512]{4,1,3,2,0:T(2,128)(2,1)}, u32[]{:S(2)}, u32[]{:S(2)}) async-start(bf16[4,2,64,2,512]{4,1,3,2,0:T(2,128)(2,1)} %copy.48), calls=%async_computation.4 | async-start | bytes 2097152 | tf_op jit(solution)/shard_map/all_to_all | solution.py:85
  188.5 2.1 multiply_reduce_fusion
  190.6 3.5 %multiply_convert_fusion = bf16[4,512,512]{1,2,0:T(8,128)(2,1)} fusion(f32[4,512]{1,0:T(4,128)S(1)} %mul.74, f32[512]{0:T(512)S(1)} %add_rsqrt_fusion, bf16[4,512,512]{1,2,0:T(8,128)(2,1)} %all-to-all-done.2), kind=kLoop, calls=%fused_computation.12 | loop fusion | flops 4194304 | bytes 4204544 | tf_op jit(solution)/shard_map/convert.2
  194.1 3.5 %fusion.6 = bf16[512,2048]{0,1:T(8,128)(2,1)} fusion(f32[2048]{0:T(1024)S(1)} %copy-done.5, f32[512]{0:T(512)S(1)} %add_rsqrt_fusion, bf16[4,512,512]{1,2,0:T(8,128)(2,1)} %all-to-all-done.2), kind=kLoop, calls=%fused_computation.10 | loop fusion | flops 4194304 | bytes 4204544 | tf_op jit(solution)/shard_map/convert_element_type | solution.py:108
  197.6 4.7 %fusion.25 = f32[512,1024]{1,0:T(8,128)} fusion(bf16[512,2048]{0,1:T(8,128)(2,1)} %fusion.6, bf16[2048,128]{1,0:T(8,128)(2,1)S(1)} %copy-done.3, bf16[1024,2176]{1,0:T(8,128)(2,1)} %all-gather.5.cloned.1.call-done), kind=kOutput, calls=%fused_computation.40 | convolution fusion | flops 402718720 | bytes 4980736 | tf_op jit(solution)/shard_map/dot_general | solution.py:115
  202.3 32.4 %all-gather.3.cloned.1.call-done = bf16[2,1024,2048]{2,1,0:T(8,128)(2,1)} async-done(((bf16[2,16,2048]{2,1,0:T(8,128)(2,1)}), bf16[2,1024,2048]{2,1,0:T(8,128)(2,1)}) %all-gather.3.cloned.1.call-update) | async-done | bytes 8388624 | tf_op jit(solution)/shard_map/all_gather | solution.py:64
  234.7 6.5 %fusion.4 = f32[512,1024]{1,0:T(8,128)} fusion(bf16[512,2048]{0,1:T(8,128)(2,1)} %bitcast.94, bf16[2,1024,2048]{2,1,0:T(8,128)(2,1)} %all-gather.3.cloned.1.call-done), kind=kOutput, calls=%fused_computation.7 | convolution fusion | flops 2147483648 | bytes 8388608 | tf_op jit(solution)/shard_map/dot_general | solution.py:113
  241.3 11.6 %fusion.8 = bf16[512,2048]{1,0:T(8,128)(2,1)} fusion(bf16[1024,2176]{1,0:T(8,128)(2,1)} %all-gather.5.cloned.1.call-done, f32[512,1024]{1,0:T(8,128)} %fusion.4, f32[512,1024]{1,0:T(8,128)} %fusion.25, bf16[512,2048]{0,1:T(8,128)(2,1)} %bitcast.95, bf16[2,1024,2048]{2,1,0:T(8,128)(2,1)} %all-gather.3.cloned.1.call-done), kind=kOutput, calls=%fused_computation.20 | convolution fusion | flops 4301783040 | bytes 16777216 | tf_op jit(solution)/shard_map/dot_general | solution.py:120
  252.8 3.1 copy.67
  256.0 20.1 %all-to-all-start.3 = ((bf16[4,512,512]{2,1,0:T(8,128)(2,1)}), bf16[4,512,512]{2,1,0:T(8,128)(2,1)}, u32[]{:S(2)}, u32[]{:S(2)}) async-start(bf16[4,512,512]{2,1,0:T(8,128)(2,1)} %bitcast.88), calls=%async_computation.3 | async-start | bytes 4194304 | tf_op jit(solution)/shard_map/all_to_all | solution.py:38
  276.1 3.0 copy.49
  279.1 2.6 reshape.174
  281.7 39.3 %all-to-all-done.3 = bf16[4,512,512]{2,1,0:T(8,128)(2,1)} async-done(((bf16[4,512,512]{2,1,0:T(8,128)(2,1)}), bf16[4,512,512]{2,1,0:T(8,128)(2,1)}, u32[]{:S(2)}, u32[]{:S(2)}) %all-to-all-start.3) | async-done | bytes 2097184 | tf_op jit(solution)/shard_map/all_to_all | solution.py:38
  (48 shorter events, 21.6 us)
Async XLA Ops:
  7.2 10.7 %copy-start = (bf16[512,2048]{1,0:T(8,128)(2,1)S(1)}, bf16[512,2048]{1,0:T(8,128)(2,1)}, u32[]{:S(2)}) copy-start(bf16[512,2048]{1,0:T(8,128)(2,1)} %param.19) | copy-start | bytes 6291460
  7.2 7.0 %copy-start.2 = (bf16[512,512]{1,0:T(8,128)(2,1)S(1)}, bf16[512,512]{1,0:T(8,128)(2,1)}, u32[]{:S(2)}) copy-start(bf16[512,512]{1,0:T(8,128)(2,1)} %param.14) | copy-start | bytes 1572868
  7.2 7.0 %copy-start.1 = (bf16[512,512]{1,0:T(8,128)(2,1)S(1)}, bf16[512,512]{1,0:T(8,128)(2,1)}, u32[]{:S(2)}) copy-start(bf16[512,512]{1,0:T(8,128)(2,1)} %param.15) | copy-start | bytes 1572868
  7.2 190.4 %all-gather.5.cloned.1.call-start = ((), (), s32[]{:S(2)}) async-start(), calls=%async_computation.6 | async-start | bytes 4526080 | tf_op jit(solution)/shard_map/all_gather | solution.py:66
  8.9 225.8 %all-gather.3.cloned.1.call-start = ((), (), s32[]{:S(2)}) async-start(), calls=%async_computation.5 | async-start | bytes 8519680 | tf_op jit(solution)/shard_map/all_gather | solution.py:64
  15.0 2.4 copy-start.4
  20.6 6.1 %copy-start.6 = (s32[1,512]{1,0:T(1,128)S(1)}, s32[1,512]{1,0:T(1,128)}, u32[]{:S(2)}) copy-start(s32[1,512]{1,0:T(1,128)} %param.26) | copy-start | bytes 6148
  20.6 54.8 %all-to-all-start = ((bf16[4,512,512]{2,1,0:T(8,128)(2,1)}), bf16[4,512,512]{2,1,0:T(8,128)(2,1)}, u32[]{:S(2)}, u32[]{:S(2)}) async-start(bf16[4,512,512]{2,1,0:T(8,128)(2,1)} %bitcast.87), calls=%async_computation | async-start | bytes 4194304 | tf_op jit(solution)/shard_map/all_to_all | solution.py:38
  119.3 7.8 %copy-start.5 = (f32[2048]{0:T(1024)S(1)}, f32[2048]{0:T(1024)}, u32[]{:S(2)}) copy-start(f32[2048]{0:T(1024)} %param.20) | copy-start | bytes 24580
  119.3 62.1 %all-to-all-start.2 = ((bf16[4,512,512]{1,2,0:T(8,128)(2,1)}), bf16[4,512,512]{1,2,0:T(8,128)(2,1)}, u32[]{:S(2)}, u32[]{:S(2)}) async-start(bf16[4,512,512]{1,2,0:T(8,128)(2,1)} %broadcast_in_dim.55), calls=%async_computation.2 | async-start | bytes 4194304 | tf_op jit(solution)/shard_map/all_to_all | solution.py:103
  127.0 1.7 copy-start.7
  181.4 74.6 %all-to-all-start.4 = ((bf16[4,2,64,2,512]{4,1,3,2,0:T(2,128)(2,1)}), bf16[4,2,64,2,512]{4,1,3,2,0:T(2,128)(2,1)}, u32[]{:S(2)}, u32[]{:S(2)}) async-start(bf16[4,2,64,2,512]{4,1,3,2,0:T(2,128)(2,1)} %copy.48), calls=%async_computation.4 | async-start | bytes 2097152 | tf_op jit(solution)/shard_map/all_to_all | solution.py:85
  194.1 3.5 %copy-start.3 = (bf16[2048,128]{1,0:T(8,128)(2,1)S(1)}, bf16[2048,128]{1,0:T(8,128)(2,1)}, u32[]{:S(2)}) copy-start(bf16[2048,128]{1,0:T(8,128)(2,1)} %param.21) | copy-start | bytes 1572868
  256.0 65.0 %all-to-all-start.3 = ((bf16[4,512,512]{2,1,0:T(8,128)(2,1)}), bf16[4,512,512]{2,1,0:T(8,128)(2,1)}, u32[]{:S(2)}, u32[]{:S(2)}) async-start(bf16[4,512,512]{2,1,0:T(8,128)(2,1)} %bitcast.88), calls=%async_computation.3 | async-start | bytes 4194304 | tf_op jit(solution)/shard_map/all_to_all | solution.py:38
Sparse Core Ops, SparseCore 0:
  11.6 102.2 all-gather.4
  117.5 117.2 all-gather.2

commit v2 on v1

--- a/solution.py
+++ b/solution.py
@@ -60,10 +60,15 @@
     quarter = resid.shape[1]
     model_width = down_weight.shape[1]
 
-    gate_up_local = jnp.stack([gate_weight.T, up_weight.T])
-    gate_up = lax.all_gather(gate_up_local, "req", axis=1, tiled=True)
-    down_adapter_local = jnp.concatenate([down_weight, adapter_up.T], axis=1)
-    down_adapter = lax.all_gather(down_adapter_local, "req", axis=0, tiled=True)
+    hidden_width = gate_weight.shape[0]
+    unit_rows_local = jnp.concatenate(
+        [gate_weight.T, up_weight.T, down_weight, adapter_up.T], axis=1
+    )
+    unit_rows = lax.all_gather(unit_rows_local, "req", axis=0, tiled=True)
+    gate_rows = unit_rows[:, :hidden_width]
+    up_rows = unit_rows[:, hidden_width : 2 * hidden_width]
+    down_rows = unit_rows[:, 2 * hidden_width : 2 * hidden_width + model_width]
+    adapter_rows = unit_rows[:, 2 * hidden_width + model_width :]
 
     slot_count = keys.shape[0]
     block_count = block_table.shape[1]
@@ -94,7 +99,7 @@
 
     permuted = jnp.take(hidden, row_order[0], axis=0)
     cap = permuted.shape[0]
-    req_n = gate_up.shape[1] // gate_weight.shape[1]
+    req_n = unit_rows.shape[0] // gate_weight.shape[1]
     per_group = cap // req_n
     column = lax.all_to_all(
         permuted.reshape(req_n, per_group, quarter), "req", split_axis=0, concat_axis=0, tiled=True
@@ -111,14 +116,14 @@
     )
     contract = (((1,), (1,)), ((), ()))
     gate = lax.dot_general(
-        normed, gate_up[0], contract, preferred_element_type=jnp.float32
+        normed, gate_rows, contract, preferred_element_type=jnp.float32
     ) + lax.dot_general(
-        low_rank, down_adapter[:, model_width:], contract, preferred_element_type=jnp.float32
+        low_rank, adapter_rows, contract, preferred_element_type=jnp.float32
     )
-    up = lax.dot_general(normed, gate_up[1], contract, preferred_element_type=jnp.float32)
+    up = lax.dot_general(normed, up_rows, contract, preferred_element_type=jnp.float32)
     hidden_units = (jax.nn.gelu(gate) * up).astype(jnp.bfloat16)
     down_part = jnp.dot(
-        hidden_units, down_adapter[:, :model_width], preferred_element_type=jnp.float32
+        hidden_units, down_rows, preferred_element_type=jnp.float32
     ).astype(jnp.bfloat16)
     mlp_total = reduce_over_dec(down_part, dec_count)
     block_out = (column.astype(jnp.float32) + mlp_total).astype(jnp.bfloat16)

time: 336 us -> 313 us (0.932)
  waiting for transfers between devices: 166 us -> 140 us
  blocking collectives: 33.2 us -> 50.3 us
  starting transfers between devices: 40.6 us -> 31.1 us
  other arithmetic: 24.4 us -> 19.5 us
    all_gather x2 -> x1, waiting for transfers between devices: 32.4 us -> 0.01 us  [body(): unit_rows = lax.all_gather(unit_rows_local, 'req', axis=0, tiled=True)]
    all_to_all x1, blocking collectives: 33.2 us -> 50.3 us  [body(): lax.all_to_all(permuted.reshape(req_n, per_group, quarter), 'req', split_...]
    all_to_all x2, starting transfers between devices: 25.7 us -> 10.2 us  [reduce_over_dec(): got = lax.all_to_all(pieces, 'dec', split_axis=0, concat_axis=0, tiled=True)]
    all_to_all x1, starting transfers between devices: 7.78 us -> 13.2 us  [body(): lax.all_to_all(spread, 'dec', split_axis=0, concat_axis=0, tiled=True)]
    all_to_all x2, waiting for transfers between devices: 87.2 us -> 92.7 us  [reduce_over_dec(): got = lax.all_to_all(pieces, 'dec', split_axis=0, concat_axis=0, tiled=True)]
    another operation x2 -> x0, other arithmetic: 5.01 us -> none
  transfers between devices with their start and end apart: 6 -> 5, of which waited for: 4 -> 3; matrix products, arithmetic and copies ran while one was open for 22% -> 22% of each run, Pallas kernels for 0% -> 0%
where the time goes in v2:
time: 313 us; the launch traced here: 307 us
  waiting for transfers between devices  140 us (45%)
  blocking collectives  50.3 us (16%)
  starting transfers between devices  31.1 us (10%)
  matrix products  26.4 us (8%)
  local copies, waits for them, and re-layouts  25.9 us (8%)
  other arithmetic  19.5 us (6%)
  between operations  14.2 us (5%)
    all_to_all x2, waiting for transfers between devices, reduce_over_dec(): got = lax.all_to_all(pieces, 'dec', split_axis=0, concat_axis=0, tiled=True)  92.7 us
    all_to_all x1, blocking collectives, body(): lax.all_to_all(permuted.reshape(req_n, per_group, quarter), 'req', split_...  50.3 us
    all_to_all x1, waiting for transfers between devices, body(): lax.all_to_all(spread, 'dec', split_axis=0, concat_axis=0, tiled=True)  47.1 us
    all_to_all x1, starting transfers between devices, body(): lax.all_to_all(spread, 'dec', split_axis=0, concat_axis=0, tiled=True)  13.2 us
    dot_general x1, matrix products, body(): jnp.dot(hidden_units, down_rows, preferred_element_type=jnp.float32)  11.5 us
    all_to_all x2, starting transfers between devices, reduce_over_dec(): got = lax.all_to_all(pieces, 'dec', split_axis=0, concat_axis=0, tiled=True)  10.2 us
    all_to_all x1, starting transfers between devices, body(): lax.all_to_all(ordered, 'dec', split_axis=0, concat_axis=0, tiled=True)  7.62 us
    dot_general x1, matrix products, body(): lax.dot_general(normed, gate_rows, contract, preferred_element_type=jnp.f...  6.59 us
  transfers between devices with their start and end apart: 5, of which 3 were waited for; matrix products, arithmetic and copies ran while one was open for 22% of the time, Pallas kernels for 0%

profile of v2, /device:TPU:33, one launch (start us, length us, event | category | flops | bytes accessed | tf_op | source)
XLA Modules:
  0.0 307.2 jit_solution(4106815651385532545)
XLA Ops:
  9.0 2.0 copy.52
  13.5 2.4 fusion.57
  19.2 5.6 %all-to-all-start = ((bf16[4,512,512]{2,1,0:T(8,128)(2,1)}), bf16[4,512,512]{2,1,0:T(8,128)(2,1)}, u32[]{:S(2)}, u32[]{:S(2)}) async-start(bf16[4,512,512]{2,1,0:T(8,128)(2,1)} %bitcast.70), calls=%async_computation | async-start | bytes 4194304 | tf_op jit(solution)/shard_map/all_to_all | solution.py:38
  26.1 53.9 %all-to-all-done = bf16[4,512,512]{2,1,0:T(8,128)(2,1)} async-done(((bf16[4,512,512]{2,1,0:T(8,128)(2,1)}), bf16[4,512,512]{2,1,0:T(8,128)(2,1)}, u32[]{:S(2)}, u32[]{:S(2)}) %all-to-all-start) | async-done | bytes 2097184 | tf_op jit(solution)/shard_map/all_to_all | solution.py:38
  79.9 2.0 convert_reduce_fusion.1
  83.2 2.6 gather_fusion
  87.0 50.3 %all_to_all.25 = bf16[64,8,512]{2,1,0:T(8,128)(2,1)S(1)} all-to-all(bf16[64,8,512]{2,1,0:T(8,128)(2,1)S(1)} %bitcast_select_fusion), channel_id=1, replica_groups=mesh['req'=64,'dec'=4] {'req'}, dimensions={0} | all-to-all | bytes 1048576 | tf_op jit(solution)/shard_map/all_to_all | solution.py:104
  138.3 2.5 broadcast_in_dim.55
  140.8 13.2 %all-to-all-start.2 = ((bf16[4,512,512]{1,2,0:T(8,128)(2,1)}), bf16[4,512,512]{1,2,0:T(8,128)(2,1)}, u32[]{:S(2)}, u32[]{:S(2)}) async-start(bf16[4,512,512]{1,2,0:T(8,128)(2,1)} %broadcast_in_dim.55), calls=%async_computation.2 | async-start | bytes 4194304 | tf_op jit(solution)/shard_map/all_to_all | solution.py:108
  157.1 2.3 reshape.152
  159.4 2.9 copy.48
  162.3 47.1 %all-to-all-done.2 = bf16[4,512,512]{1,2,0:T(8,128)(2,1)} async-done(((bf16[4,512,512]{1,2,0:T(8,128)(2,1)}), bf16[4,512,512]{1,2,0:T(8,128)(2,1)}, u32[]{:S(2)}, u32[]{:S(2)}) %all-to-all-start.2) | async-done | bytes 2097184 | tf_op jit(solution)/shard_map/all_to_all | solution.py:108
  209.4 7.6 %all-to-all-start.4 = ((bf16[4,2,64,2,512]{4,1,3,2,0:T(2,128)(2,1)}), bf16[4,2,64,2,512]{4,1,3,2,0:T(2,128)(2,1)}, u32[]{:S(2)}, u32[]{:S(2)}) async-start(bf16[4,2,64,2,512]{4,1,3,2,0:T(2,128)(2,1)} %copy.48), calls=%async_computation.4 | async-start | bytes 2097152 | tf_op jit(solution)/shard_map/all_to_all | solution.py:90
  217.0 2.1 multiply_reduce_fusion
  219.1 3.5 %fusion.8 = bf16[512,2048]{0,1:T(8,128)(2,1)} fusion(f32[2048]{0:T(1024)S(1)} %copy-done.5, f32[512]{0:T(512)S(1)} %add_rsqrt_fusion, bf16[4,512,512]{1,2,0:T(8,128)(2,1)} %all-to-all-done.2), kind=kLoop, calls=%fused_computation.10 | loop fusion | flops 4194304 | bytes 4204544 | tf_op jit(solution)/shard_map/convert_element_type | solution.py:113
  222.6 6.6 %fusion.5 = f32[512,1024]{1,0:T(8,128)} fusion(bf16[512,2048]{0,1:T(8,128)(2,1)} %fusion.8, bf16[1024,6272]{1,0:T(8,128)(2,1)} %all-gather.2.cloned.1.call-done), kind=kOutput, calls=%fused_computation.6 | convolution fusion | flops 2147483648 | bytes 8388608 | tf_op jit(solution)/shard_map/dot_general | solution.py:118
  229.2 4.4 %fusion.31 = f32[512,1024]{1,0:T(8,128)} fusion(bf16[512,2048]{0,1:T(8,128)(2,1)} %fusion.8, bf16[2048,128]{1,0:T(8,128)(2,1)S(1)} %copy-done.3, bf16[1024,6272]{1,0:T(8,128)(2,1)} %all-gather.2.cloned.1.call-done), kind=kOutput, calls=%fused_computation.39 | convolution fusion | flops 402718720 | bytes 4980736 | tf_op jit(solution)/shard_map/dot_general | solution.py:120
  233.6 11.5 %fusion.10 = bf16[512,2048]{1,0:T(8,128)(2,1)} fusion(bf16[1024,6272]{1,0:T(8,128)(2,1)} %all-gather.2.cloned.1.call-done, f32[512,1024]{1,0:T(8,128)} %fusion.5, f32[512,1024]{1,0:T(8,128)} %fusion.31, bf16[512,2048]{0,1:T(8,128)(2,1)} %fusion.8), kind=kOutput, calls=%fused_computation.19 | convolution fusion | flops 4301783040 | bytes 16777216 | tf_op jit(solution)/shard_map/dot_general | solution.py:125
  245.2 3.1 %copy.67 = bf16[64,4,8,512]{3,2,0,1:T(8,128)(2,1)} copy(bf16[64,4,8,512]{3,2,1,0:T(8,128)(2,1)} %bitcast.74) | data formatting | bytes 4194304 | tf_op jit(solution)/shard_map/reshape | solution.py:37
  248.3 4.6 %all-to-all-start.3 = ((bf16[4,512,512]{2,1,0:T(8,128)(2,1)}), bf16[4,512,512]{2,1,0:T(8,128)(2,1)}, u32[]{:S(2)}, u32[]{:S(2)}) async-start(bf16[4,512,512]{2,1,0:T(8,128)(2,1)} %bitcast.71), calls=%async_computation.3 | async-start | bytes 4194304 | tf_op jit(solution)/shard_map/all_to_all | solution.py:38
  252.9 3.0 copy.49
  256.0 2.6 reshape.153
  258.5 38.8 %all-to-all-done.3 = bf16[4,512,512]{2,1,0:T(8,128)(2,1)} async-done(((bf16[4,512,512]{2,1,0:T(8,128)(2,1)}), bf16[4,512,512]{2,1,0:T(8,128)(2,1)}, u32[]{:S(2)}, u32[]{:S(2)}) %all-to-all-start.3) | async-done | bytes 2097184 | tf_op jit(solution)/shard_map/all_to_all | solution.py:38
  297.4 2.0 convert_reduce_fusion
  (42 shorter events, 16.2 us)
Async XLA Ops:
  7.2 9.2 %copy-start = (bf16[512,2048]{1,0:T(8,128)(2,1)S(1)}, bf16[512,2048]{1,0:T(8,128)(2,1)}, u32[]{:S(2)}) copy-start(bf16[512,2048]{1,0:T(8,128)(2,1)} %param.19) | copy-start | bytes 6291460
  7.2 5.6 %copy-start.2 = (bf16[512,512]{1,0:T(8,128)(2,1)S(1)}, bf16[512,512]{1,0:T(8,128)(2,1)}, u32[]{:S(2)}) copy-start(bf16[512,512]{1,0:T(8,128)(2,1)} %param.14) | copy-start | bytes 1572868
  7.2 5.6 %copy-start.1 = (bf16[512,512]{1,0:T(8,128)(2,1)S(1)}, bf16[512,512]{1,0:T(8,128)(2,1)}, u32[]{:S(2)}) copy-start(bf16[512,512]{1,0:T(8,128)(2,1)} %param.15) | copy-start | bytes 1572868
  7.2 215.4 %all-gather.2.cloned.1.call-start = ((), (), s32[]{:S(2)}) async-start(), calls=%async_computation.5 | async-start | bytes 13045760 | tf_op jit(solution)/shard_map/all_gather | solution.py:67
  13.5 2.4 copy-start.4
  19.2 6.1 %copy-start.6 = (s32[1,512]{1,0:T(1,128)S(1)}, s32[1,512]{1,0:T(1,128)}, u32[]{:S(2)}) copy-start(s32[1,512]{1,0:T(1,128)} %param.26) | copy-start | bytes 6148
  19.2 60.8 %all-to-all-start = ((bf16[4,512,512]{2,1,0:T(8,128)(2,1)}), bf16[4,512,512]{2,1,0:T(8,128)(2,1)}, u32[]{:S(2)}, u32[]{:S(2)}) async-start(bf16[4,512,512]{2,1,0:T(8,128)(2,1)} %bitcast.70), calls=%async_computation | async-start | bytes 4194304 | tf_op jit(solution)/shard_map/all_to_all | solution.py:38
  140.8 68.5 %all-to-all-start.2 = ((bf16[4,512,512]{1,2,0:T(8,128)(2,1)}), bf16[4,512,512]{1,2,0:T(8,128)(2,1)}, u32[]{:S(2)}, u32[]{:S(2)}) async-start(bf16[4,512,512]{1,2,0:T(8,128)(2,1)} %broadcast_in_dim.55), calls=%async_computation.2 | async-start | bytes 4194304 | tf_op jit(solution)/shard_map/all_to_all | solution.py:108
  154.1 1.6 copy-start.7
  162.3 56.8 %copy-start.5 = (f32[2048]{0:T(1024)S(1)}, f32[2048]{0:T(1024)}, u32[]{:S(2)}) copy-start(f32[2048]{0:T(1024)} %param.20) | copy-start | bytes 24580
  209.4 38.9 %all-to-all-start.4 = ((bf16[4,2,64,2,512]{4,1,3,2,0:T(2,128)(2,1)}), bf16[4,2,64,2,512]{4,1,3,2,0:T(2,128)(2,1)}, u32[]{:S(2)}, u32[]{:S(2)}) async-start(bf16[4,2,64,2,512]{4,1,3,2,0:T(2,128)(2,1)} %copy.48), calls=%async_computation.4 | async-start | bytes 2097152 | tf_op jit(solution)/shard_map/all_to_all | solution.py:90
  222.6 6.6 %copy-start.3 = (bf16[2048,128]{1,0:T(8,128)(2,1)S(1)}, bf16[2048,128]{1,0:T(8,128)(2,1)}, u32[]{:S(2)}) copy-start(bf16[2048,128]{1,0:T(8,128)(2,1)} %param.21) | copy-start | bytes 1572868
  248.3 49.0 %all-to-all-start.3 = ((bf16[4,512,512]{2,1,0:T(8,128)(2,1)}), bf16[4,512,512]{2,1,0:T(8,128)(2,1)}, u32[]{:S(2)}, u32[]{:S(2)}) async-start(bf16[4,512,512]{2,1,0:T(8,128)(2,1)} %bitcast.71), calls=%async_computation.3 | async-start | bytes 4194304 | tf_op jit(solution)/shard_map/all_to_all | solution.py:38
Sparse Core Ops, SparseCore 0:
  11.7 189.5 all-gather.1

commit v3 on v2

--- a/solution.py
+++ b/solution.py
@@ -94,39 +94,49 @@
     partial_value = jnp.dot(attn, out_weight, preferred_element_type=jnp.float32).astype(
         jnp.bfloat16
     )
-    head_total = reduce_over_dec(partial_value, dec_count)
-    hidden = (resid.astype(jnp.float32) + head_total).astype(jnp.bfloat16)
-
-    permuted = jnp.take(hidden, row_order[0], axis=0)
-    cap = permuted.shape[0]
+    order = row_order[0]
+    cap = resid.shape[0]
     req_n = unit_rows.shape[0] // gate_weight.shape[1]
     per_group = cap // req_n
-    column = lax.all_to_all(
-        permuted.reshape(req_n, per_group, quarter), "req", split_axis=0, concat_axis=0, tiled=True
-    ).reshape(cap, quarter)
-    spread = jnp.broadcast_to(column[None], (dec_count, cap, quarter))
-    quarters = lax.all_to_all(spread, "dec", split_axis=0, concat_axis=0, tiled=True)
-    mixed_rows = quarters.transpose(1, 0, 2).reshape(cap, dec_count * quarter)
+    chunks = 2
+    per_chunk = per_group // chunks
+    partial_sorted = jnp.take(partial_value, order, axis=0).reshape(
+        req_n, chunks, per_chunk, dec_count * quarter
+    )
+    resid_sorted = jnp.take(resid, order, axis=0).reshape(req_n, chunks, per_chunk, quarter)
+    contract = (((1,), (1,)), ((), ()))
+    outs = []
+    for c in range(chunks):
+        rows_c = req_n * per_chunk
+        head_total = reduce_over_dec(partial_sorted[:, c].reshape(rows_c, dec_count * quarter), dec_count)
+        hidden = (resid_sorted[:, c].reshape(rows_c, quarter).astype(jnp.float32) + head_total).astype(
+            jnp.bfloat16
+        )
+        column = lax.all_to_all(
+            hidden.reshape(req_n, per_chunk, quarter), "req", split_axis=0, concat_axis=0, tiled=True
+        ).reshape(rows_c, quarter)
+        spread = jnp.broadcast_to(column[None], (dec_count, rows_c, quarter))
+        quarters = lax.all_to_all(spread, "dec", split_axis=0, concat_axis=0, tiled=True)
+        mixed_rows = quarters.transpose(1, 0, 2).reshape(rows_c, dec_count * quarter)
 
-    values_f = mixed_rows.astype(jnp.float32)
-    scale = lax.rsqrt(jnp.mean(values_f * values_f, axis=-1, keepdims=True) + 1e-05)
-    normed = (values_f * scale * norm_gain).astype(jnp.bfloat16)
-    low_rank = jnp.dot(normed, adapter_down, preferred_element_type=jnp.float32).astype(
-        jnp.bfloat16
-    )
-    contract = (((1,), (1,)), ((), ()))
-    gate = lax.dot_general(
-        normed, gate_rows, contract, preferred_element_type=jnp.float32
-    ) + lax.dot_general(
-        low_rank, adapter_rows, contract, preferred_element_type=jnp.float32
-    )
-    up = lax.dot_general(normed, up_rows, contract, preferred_element_type=jnp.float32)
-    hidden_units = (jax.nn.gelu(gate) * up).astype(jnp.bfloat16)
-    down_part = jnp.dot(
-        hidden_units, down_rows, preferred_element_type=jnp.float32
-    ).astype(jnp.bfloat16)
-    mlp_total = reduce_over_dec(down_part, dec_count)
-    block_out = (column.astype(jnp.float32) + mlp_total).astype(jnp.bfloat16)
+        values_f = mixed_rows.astype(jnp.float32)
+        scale = lax.rsqrt(jnp.mean(values_f * values_f, axis=-1, keepdims=True) + 1e-05)
+        normed = (values_f * scale * norm_gain).astype(jnp.bfloat16)
+        low_rank = jnp.dot(normed, adapter_down, preferred_element_type=jnp.float32).astype(
+            jnp.bfloat16
+        )
+        gate = lax.dot_general(
+            normed, gate_rows, contract, preferred_element_type=jnp.float32
+        ) + lax.dot_general(low_rank, adapter_rows, contract, preferred_element_type=jnp.float32)
+        up = lax.dot_general(normed, up_rows, contract, preferred_element_type=jnp.float32)
+        hidden_units = (jax.nn.gelu(gate) * up).astype(jnp.bfloat16)
+        down_part = jnp.dot(hidden_units, down_rows, preferred_element_type=jnp.float32).astype(
+            jnp.bfloat16
+        )
+        mlp_total = reduce_over_dec(down_part, dec_count)
+        out_c = (column.astype(jnp.float32) + mlp_total).astype(jnp.bfloat16)
+        outs.append(out_c.reshape(req_n, per_chunk, quarter))
+    block_out = jnp.stack(outs, axis=1).reshape(cap, quarter)
     return (block_out, kv_cache)
 
 

time: 313 us -> 363 us (1.16)
  waiting for transfers between devices: 140 us -> 170 us
  starting transfers between devices: 31.1 us -> 54.5 us
  blocking collectives: 50.3 us -> 27.7 us
  local copies, waits for them, and re-layouts: 25.9 us -> 39.4 us
  matrix products: 26.4 us -> 34.1 us
    all_to_all x1, blocking collectives: 50.3 us -> 27.7 us  [body(): lax.all_to_all(hidden.reshape(req_n, per_chunk, quarter), 'req', split_ax...]
    all_to_all x2 -> x4, waiting for transfers between devices: 92.7 us -> 115 us  [reduce_over_dec(): got = lax.all_to_all(pieces, 'dec', split_axis=0, concat_axis=0, tiled=True)]
    all_to_all x2 -> x4, starting transfers between devices: 10.2 us -> 27.1 us  [reduce_over_dec(): got = lax.all_to_all(pieces, 'dec', split_axis=0, concat_axis=0, tiled=True)]
    all_to_all x0 -> x1, waiting for transfers between devices: none -> 13.6 us  [body(): lax.all_to_all(hidden.reshape(req_n, per_chunk, quarter), 'req', split_ax...]
    all_to_all x1 -> x2, waiting for transfers between devices: 47.1 us -> 37.1 us  [body(): lax.all_to_all(spread, 'dec', split_axis=0, concat_axis=0, tiled=True)]
    gather x1 -> x4, local copies, waits for them, and re-layouts: 2.63 us -> 10.6 us  [the longest x2 8.54 us: body(): jnp.take(partial_value, order, axis=0)]
    all_to_all x0 -> x1, starting transfers between devices: none -> 4.65 us  [body(): lax.all_to_all(hidden.reshape(req_n, per_chunk, quarter), 'req', split_ax...]
    all_to_all x1, waiting for transfers between devices: 0.01 us -> 3.83 us  [body(): lax.all_to_all(ordered, 'dec', split_axis=0, concat_axis=0, tiled=True)]
  transfers between devices with their start and end apart: 5 -> 9, of which waited for: 3 -> 8; matrix products, arithmetic and copies ran while one was open for 22% -> 24% of each run, Pallas kernels for 0% -> 0%
where the time goes in v3:
time: 363 us; the launch traced here: 357 us
  waiting for transfers between devices  170 us (47%)
  starting transfers between devices  54.5 us (15%)
  local copies, waits for them, and re-layouts  39.4 us (11%)
  matrix products  34.1 us (9%)
  blocking collectives  27.7 us (8%)
  other arithmetic  17.3 us (5%)
  between operations  14.4 us (4%)
    all_to_all x4, waiting for transfers between devices, reduce_over_dec(): got = lax.all_to_all(pieces, 'dec', split_axis=0, concat_axis=0, tiled=True)  115 us
    all_to_all x2, waiting for transfers between devices, body(): lax.all_to_all(spread, 'dec', split_axis=0, concat_axis=0, tiled=True)  37.1 us
    all_to_all x1, blocking collectives, body(): lax.all_to_all(hidden.reshape(req_n, per_chunk, quarter), 'req', split_ax...  27.7 us
    all_to_all x4, starting transfers between devices, reduce_over_dec(): got = lax.all_to_all(pieces, 'dec', split_axis=0, concat_axis=0, tiled=True)  27.1 us
    all_to_all x2, starting transfers between devices, body(): lax.all_to_all(spread, 'dec', split_axis=0, concat_axis=0, tiled=True)  15.4 us
    all_to_all x1, waiting for transfers between devices, body(): lax.all_to_all(hidden.reshape(req_n, per_chunk, quarter), 'req', split_ax...  13.6 us
    dot_general x2, matrix products, body(): jnp.dot(hidden_units, down_rows, preferred_element_type=jnp.float32)  12.6 us
    dot_general x2, matrix products, body(): lax.dot_general(normed, gate_rows, contract, preferred_element_type=jnp.f...  9.44 us
  transfers between devices with their start and end apart: 9, of which 8 were waited for; matrix products, arithmetic and copies ran while one was open for 24% of the time, Pallas kernels for 0%

profile of v3, /device:TPU:33, one launch (start us, length us, event | category | flops | bytes accessed | tf_op | source)
XLA Modules:
  0.0 357.2 jit_solution(2582587203872842380)
XLA Ops:
  20.0 6.3 %gather_fusion.1 = bf16[512,2048]{1,0:T(8,128)(2,1)S(1)} fusion(bf16[512,2048]{1,0:T(8,128)(2,1)} %convolution_convert_fusion, s32[1024]{0:T(1024)S(1)} %pad_clamp_fusion), kind=kCustom, calls=%fused_computation.1 | custom fusion | bytes 4196352 | tf_op jit(solution)/shard_map/jit(_take)/gather | solution.py:103
  36.7 5.6 %all-to-all-start = ((bf16[4,256,512]{2,1,0:T(8,128)(2,1)}), bf16[4,256,512]{2,1,0:T(8,128)(2,1)S(1)}, u32[]{:S(2)}, u32[]{:S(2)}) async-start(bf16[4,256,512]{2,1,0:T(8,128)(2,1)} %copy.54), calls=%async_computation | async-start | bytes 2097152 | tf_op jit(solution)/shard_map/all_to_all | solution.py:38
  45.2 30.4 %all-to-all-done = bf16[4,256,512]{2,1,0:T(8,128)(2,1)S(1)} async-done(((bf16[4,256,512]{2,1,0:T(8,128)(2,1)}), bf16[4,256,512]{2,1,0:T(8,128)(2,1)S(1)}, u32[]{:S(2)}, u32[]{:S(2)}) %all-to-all-start) | async-done | bytes 1048608 | tf_op jit(solution)/shard_map/all_to_all | solution.py:38
  75.6 6.9 %all-to-all-start.4 = ((bf16[4,256,512]{2,1,0:T(8,128)(2,1)}), bf16[4,256,512]{2,1,0:T(8,128)(2,1)S(1)}, u32[]{:S(2)}, u32[]{:S(2)}) async-start(bf16[4,256,512]{2,1,0:T(8,128)(2,1)} %copy.57), calls=%async_computation.4 | async-start | bytes 2097152 | tf_op jit(solution)/shard_map/all_to_all | solution.py:38
  85.2 65.0 %all-to-all-done.4 = bf16[4,256,512]{2,1,0:T(8,128)(2,1)S(1)} async-done(((bf16[4,256,512]{2,1,0:T(8,128)(2,1)}), bf16[4,256,512]{2,1,0:T(8,128)(2,1)S(1)}, u32[]{:S(2)}, u32[]{:S(2)}) %all-to-all-start.4) | async-done | bytes 1048608 | tf_op jit(solution)/shard_map/all_to_all | solution.py:38
  151.5 27.7 %all_to_all.45 = bf16[64,4,512]{2,1,0:T(4,128)(2,1)S(1)} all-to-all(bf16[64,4,512]{2,1,0:T(4,128)(2,1)S(1)} %get-tuple-element.5), channel_id=1, replica_groups=mesh['req'=64,'dec'=4] {'req'}, dimensions={0} | all-to-all | bytes 524288 | tf_op jit(solution)/shard_map/all_to_all | solution.py:115
  179.2 4.7 %all-to-all-start.1 = ((bf16[64,4,512]{2,1,0:T(4,128)(2,1)}), bf16[64,4,512]{2,1,0:T(4,128)(2,1)S(1)}, u32[]{:S(2)}, u32[]{:S(2)}) async-start(bf16[64,4,512]{2,1,0:T(4,128)(2,1)} %get-tuple-element.4), calls=%async_computation.1 | async-start | bytes 524288 | tf_op jit(solution)/shard_map/all_to_all | solution.py:115
  184.1 13.6 %all-to-all-done.1 = bf16[64,4,512]{2,1,0:T(4,128)(2,1)S(1)} async-done(((bf16[64,4,512]{2,1,0:T(4,128)(2,1)}), bf16[64,4,512]{2,1,0:T(4,128)(2,1)S(1)}, u32[]{:S(2)}, u32[]{:S(2)}) %all-to-all-start.1) | async-done | bytes 262176 | tf_op jit(solution)/shard_map/all_to_all | solution.py:115
  198.7 9.0 %all-to-all-start.6 = ((bf16[4,256,512]{1,2,0:T(8,128)(2,1)}), bf16[4,256,512]{1,2,0:T(8,128)(2,1)S(1)}, u32[]{:S(2)}, u32[]{:S(2)}) async-start(bf16[4,256,512]{1,2,0:T(8,128)(2,1)} %broadcast_in_dim.81), calls=%async_computation.6 | async-start | bytes 2097152 | tf_op jit(solution)/shard_map/all_to_all | solution.py:119
  207.9 22.2 %all-to-all-done.6 = bf16[4,256,512]{1,2,0:T(8,128)(2,1)S(1)} async-done(((bf16[4,256,512]{1,2,0:T(8,128)(2,1)}), bf16[4,256,512]{1,2,0:T(8,128)(2,1)S(1)}, u32[]{:S(2)}, u32[]{:S(2)}) %all-to-all-start.6) | async-done | bytes 1048608 | tf_op jit(solution)/shard_map/all_to_all | solution.py:119
  231.1 6.5 %all-to-all-start.2 = ((bf16[4,256,512]{1,2,0:T(8,128)(2,1)}), bf16[4,256,512]{1,2,0:T(8,128)(2,1)S(1)}, u32[]{:S(2)}, u32[]{:S(2)}) async-start(bf16[4,256,512]{1,2,0:T(8,128)(2,1)} %broadcast_in_dim.79), calls=%async_computation.2 | async-start | bytes 2097152 | tf_op jit(solution)/shard_map/all_to_all | solution.py:119
  244.3 14.9 %all-to-all-done.2 = bf16[4,256,512]{1,2,0:T(8,128)(2,1)S(1)} async-done(((bf16[4,256,512]{1,2,0:T(8,128)(2,1)}), bf16[4,256,512]{1,2,0:T(8,128)(2,1)S(1)}, u32[]{:S(2)}, u32[]{:S(2)}) %all-to-all-start.2) | async-done | bytes 1048608 | tf_op jit(solution)/shard_map/all_to_all | solution.py:119
  259.2 7.2 %all-to-all-start.8 = ((bf16[4,2,64,2,512]{4,1,3,2,0:T(2,128)(2,1)}), bf16[4,2,64,2,512]{4,1,3,2,0:T(2,128)(2,1)S(1)}, u32[]{:S(2)}, u32[]{:S(2)}) async-start(bf16[4,2,64,2,512]{4,1,3,2,0:T(2,128)(2,1)} %copy.63), calls=%async_computation.8 | async-start | bytes 2097152 | tf_op jit(solution)/shard_map/all_to_all | solution.py:90
  268.6 4.9 %fusion.9 = f32[256,1024]{1,0:T(8,128)} fusion(bf16[256,2048]{0,1:T(8,128)(2,1)} %get-tuple-element.7, bf16[1024,6272]{1,0:T(8,128)(2,1)} %all-gather.2.cloned.1.call-done), kind=kOutput, calls=%fused_computation.14 | convolution fusion | flops 1073741824 | bytes 6291456 | tf_op jit(solution)/shard_map/dot_general | solution.py:128
  273.5 3.2 fusion.58
  276.7 6.2 %fusion.17 = bf16[256,2048]{1,0:T(8,128)(2,1)S(1)} fusion(bf16[1024,6272]{1,0:T(8,128)(2,1)} %all-gather.2.cloned.1.call-done, f32[256,1024]{1,0:T(8,128)} %fusion.58, bf16[256,2048]{0,1:T(8,128)(2,1)S(1)} %copy-done.6), kind=kOutput, calls=%fused_computation.21 | convolution fusion | flops 2148532224 | bytes 11534336 | tf_op jit(solution)/shard_map/dot_general | solution.py:133
  284.0 3.8 %all-to-all-done.8 = bf16[4,2,64,2,512]{4,1,3,2,0:T(2,128)(2,1)S(1)} async-done(((bf16[4,2,64,2,512]{4,1,3,2,0:T(2,128)(2,1)}), bf16[4,2,64,2,512]{4,1,3,2,0:T(2,128)(2,1)S(1)}, u32[]{:S(2)}, u32[]{:S(2)}) %all-to-all-start.8) | async-done | bytes 1048608 | tf_op jit(solution)/shard_map/all_to_all | solution.py:90
  287.8 7.3 %all-to-all-start.7 = ((bf16[4,256,512]{2,1,0:T(8,128)(2,1)}), bf16[4,256,512]{2,1,0:T(8,128)(2,1)S(1)}, u32[]{:S(2)}, u32[]{:S(2)}) async-start(bf16[4,256,512]{2,1,0:T(8,128)(2,1)} %bitcast.97), calls=%async_computation.7 | async-start | bytes 2097152 | tf_op jit(solution)/shard_map/all_to_all | solution.py:38
  295.2 4.5 %fusion.11 = f32[256,1024]{1,0:T(8,128)} fusion(bf16[256,2048]{0,1:T(8,128)(2,1)S(1)} %copy-done.5, bf16[1024,6272]{1,0:T(8,128)(2,1)} %all-gather.2.cloned.1.call-done), kind=kOutput, calls=%fused_computation.16 | convolution fusion | flops 1073741824 | bytes 6291456 | tf_op jit(solution)/shard_map/dot_general | solution.py:128
  299.7 3.4 fusion.51
  303.1 6.5 %fusion.14 = bf16[256,2048]{1,0:T(8,128)(2,1)S(1)} fusion(bf16[1024,6272]{1,0:T(8,128)(2,1)} %all-gather.2.cloned.1.call-done, f32[256,1024]{1,0:T(8,128)} %fusion.51, bf16[256,2048]{0,1:T(8,128)(2,1)} %get-tuple-element.6), kind=kOutput, calls=%fused_computation.20 | convolution fusion | flops 2148532224 | bytes 11534336 | tf_op jit(solution)/shard_map/dot_general | solution.py:133
  310.7 5.9 %all-to-all-done.7 = bf16[4,256,512]{2,1,0:T(8,128)(2,1)S(1)} async-done(((bf16[4,256,512]{2,1,0:T(8,128)(2,1)}), bf16[4,256,512]{2,1,0:T(8,128)(2,1)S(1)}, u32[]{:S(2)}, u32[]{:S(2)}) %all-to-all-start.7) | async-done | bytes 1048608 | tf_op jit(solution)/shard_map/all_to_all | solution.py:38
  316.6 7.3 %all-to-all-start.3 = ((bf16[4,256,512]{2,1,0:T(8,128)(2,1)}), bf16[4,256,512]{2,1,0:T(8,128)(2,1)S(1)}, u32[]{:S(2)}, u32[]{:S(2)}) async-start(bf16[4,256,512]{2,1,0:T(8,128)(2,1)} %bitcast.99), calls=%async_computation.3 | async-start | bytes 2097152 | tf_op jit(solution)/shard_map/all_to_all | solution.py:38
  331.4 13.9 %all-to-all-done.3 = bf16[4,256,512]{2,1,0:T(8,128)(2,1)S(1)} async-done(((bf16[4,256,512]{2,1,0:T(8,128)(2,1)}), bf16[4,256,512]{2,1,0:T(8,128)(2,1)S(1)}, u32[]{:S(2)}, u32[]{:S(2)}) %all-to-all-start.3) | async-done | bytes 1048608 | tf_op jit(solution)/shard_map/all_to_all | solution.py:38
  (84 shorter events, 56.0 us)
Async XLA Ops:
  7.2 10.3 %copy-start = (bf16[512,2048]{1,0:T(8,128)(2,1)S(1)}, bf16[512,2048]{1,0:T(8,128)(2,1)}, u32[]{:S(2)}) copy-start(bf16[512,2048]{1,0:T(8,128)(2,1)} %param.19) | copy-start | bytes 6291460
  7.2 261.4 %all-gather.2.cloned.1.call-start = ((), (), s32[]{:S(2)}) async-start(), calls=%async_computation.9 | async-start | bytes 13045760 | tf_op jit(solution)/shard_map/all_gather | solution.py:67
  26.3 2.8 copy-start.8
  36.7 45.8 %copy-start.2 = (bf16[512,512]{1,0:T(8,128)(2,1)S(1)}, bf16[512,512]{1,0:T(8,128)(2,1)}, u32[]{:S(2)}) copy-start(bf16[512,512]{1,0:T(8,128)(2,1)} %param.17) | copy-start | bytes 1572868
  36.7 38.8 %all-to-all-start = ((bf16[4,256,512]{2,1,0:T(8,128)(2,1)}), bf16[4,256,512]{2,1,0:T(8,128)(2,1)S(1)}, u32[]{:S(2)}, u32[]{:S(2)}) async-start(bf16[4,256,512]{2,1,0:T(8,128)(2,1)} %copy.54), calls=%async_computation | async-start | bytes 2097152 | tf_op jit(solution)/shard_map/all_to_all | solution.py:38
  75.6 74.7 %all-to-all-start.4 = ((bf16[4,256,512]{2,1,0:T(8,128)(2,1)}), bf16[4,256,512]{2,1,0:T(8,128)(2,1)S(1)}, u32[]{:S(2)}, u32[]{:S(2)}) async-start(bf16[4,256,512]{2,1,0:T(8,128)(2,1)} %copy.57), calls=%async_computation.4 | async-start | bytes 2097152 | tf_op jit(solution)/shard_map/all_to_all | solution.py:38
  179.2 18.4 %all-to-all-start.1 = ((bf16[64,4,512]{2,1,0:T(4,128)(2,1)}), bf16[64,4,512]{2,1,0:T(4,128)(2,1)S(1)}, u32[]{:S(2)}, u32[]{:S(2)}) async-start(bf16[64,4,512]{2,1,0:T(4,128)(2,1)} %get-tuple-element.4), calls=%async_computation.1 | async-start | bytes 524288 | tf_op jit(solution)/shard_map/all_to_all | solution.py:115
  184.0 53.7 %copy-start.4 = (bf16[512,512]{1,0:T(8,128)(2,1)S(1)}, bf16[512,512]{1,0:T(8,128)(2,1)}, u32[]{:S(2)}) copy-start(bf16[512,512]{1,0:T(8,128)(2,1)} %param.15) | copy-start | bytes 1572868
  197.7 40.3 %copy-start.3 = (bf16[64,4,512]{2,1,0:T(4,128)(2,1)}, bf16[64,4,512]{2,1,0:T(4,128)(2,1)S(1)}, u32[]{:S(2)}) copy-start(bf16[64,4,512]{2,1,0:T(4,128)(2,1)S(1)} %all-to-all-done.1) | copy-start | bytes 786436
  198.7 40.5 %copy-start.9 = (s32[1,8]{1,0:T(1,128)S(1)}, s32[1,8]{1,0:T(1,128)}, u32[]{:S(2)}) copy-start(s32[1,8]{1,0:T(1,128)} %param.27) | copy-start | bytes 100
  198.7 31.4 %all-to-all-start.6 = ((bf16[4,256,512]{1,2,0:T(8,128)(2,1)}), bf16[4,256,512]{1,2,0:T(8,128)(2,1)S(1)}, u32[]{:S(2)}, u32[]{:S(2)}) async-start(bf16[4,256,512]{1,2,0:T(8,128)(2,1)} %broadcast_in_dim.81), calls=%async_computation.6 | async-start | bytes 2097152 | tf_op jit(solution)/shard_map/all_to_all | solution.py:119
  231.1 28.0 %all-to-all-start.2 = ((bf16[4,256,512]{1,2,0:T(8,128)(2,1)}), bf16[4,256,512]{1,2,0:T(8,128)(2,1)S(1)}, u32[]{:S(2)}, u32[]{:S(2)}) async-start(bf16[4,256,512]{1,2,0:T(8,128)(2,1)} %broadcast_in_dim.79), calls=%async_computation.2 | async-start | bytes 2097152 | tf_op jit(solution)/shard_map/all_to_all | solution.py:119
  239.7 27.0 %copy-start.7 = (f32[2048]{0:T(1024)S(1)}, f32[2048]{0:T(1024)}, u32[]{:S(2)}) copy-start(f32[2048]{0:T(1024)} %param.20) | copy-start | bytes 24580
  259.2 28.6 %all-to-all-start.8 = ((bf16[4,2,64,2,512]{4,1,3,2,0:T(2,128)(2,1)}), bf16[4,2,64,2,512]{4,1,3,2,0:T(2,128)(2,1)S(1)}, u32[]{:S(2)}, u32[]{:S(2)}) async-start(bf16[4,2,64,2,512]{4,1,3,2,0:T(2,128)(2,1)} %copy.63), calls=%async_computation.8 | async-start | bytes 2097152 | tf_op jit(solution)/shard_map/all_to_all | solution.py:90
  268.6 4.9 %copy-start.6 = (bf16[256,2048]{0,1:T(8,128)(2,1)S(1)}, bf16[256,2048]{0,1:T(8,128)(2,1)}, u32[]{:S(2)}) copy-start(bf16[256,2048]{0,1:T(8,128)(2,1)} %get-tuple-element.7) | copy-start | bytes 3145732
  268.6 4.9 %copy-start.10 = (bf16[2048,128]{1,0:T(8,128)(2,1)S(1)}, bf16[2048,128]{1,0:T(8,128)(2,1)}, u32[]{:S(2)}) copy-start(bf16[2048,128]{1,0:T(8,128)(2,1)} %param.21) | copy-start | bytes 1572868
  282.9 12.3 %copy-start.5 = (bf16[256,2048]{0,1:T(8,128)(2,1)S(1)}, bf16[256,2048]{0,1:T(8,128)(2,1)}, u32[]{:S(2)}) copy-start(bf16[256,2048]{0,1:T(8,128)(2,1)} %get-tuple-element.6) | copy-start | bytes 3145732
  287.8 28.8 %all-to-all-start.7 = ((bf16[4,256,512]{2,1,0:T(8,128)(2,1)}), bf16[4,256,512]{2,1,0:T(8,128)(2,1)S(1)}, u32[]{:S(2)}, u32[]{:S(2)}) async-start(bf16[4,256,512]{2,1,0:T(8,128)(2,1)} %bitcast.97), calls=%async_computation.7 | async-start | bytes 2097152 | tf_op jit(solution)/shard_map/all_to_all | solution.py:38
  316.6 28.8 %all-to-all-start.3 = ((bf16[4,256,512]{2,1,0:T(8,128)(2,1)}), bf16[4,256,512]{2,1,0:T(8,128)(2,1)S(1)}, u32[]{:S(2)}, u32[]{:S(2)}) async-start(bf16[4,256,512]{2,1,0:T(8,128)(2,1)} %bitcast.99), calls=%async_computation.3 | async-start | bytes 2097152 | tf_op jit(solution)/shard_map/all_to_all | solution.py:38
  329.3 21.1 %copy-start.1 = (bf16[512,2048]{1,0:T(8,128)(2,1)S(1)}, bf16[512,2048]{1,0:T(8,128)(2,1)}, u32[]{:S(2)}) copy-start(bf16[512,2048]{1,0:T(8,128)(2,1)} %param.19) | copy-start | bytes 6291460
Sparse Core Ops, SparseCore 0:
  11.6 132.5 all-gather.1

commit v4 on v2

--- a/solution.py
+++ b/solution.py
@@ -4,6 +4,7 @@
 from jax.sharding import PartitionSpec as P
 
 HD = 128
+REQ = ("req_hi", "core")
 
 
 def attend(query_rows, key_rows, value_rows, segment):
@@ -64,7 +65,9 @@
     unit_rows_local = jnp.concatenate(
         [gate_weight.T, up_weight.T, down_weight, adapter_up.T], axis=1
     )
-    unit_rows = lax.all_gather(unit_rows_local, "req", axis=0, tiled=True)
+    same_core = lax.all_gather(unit_rows_local, "req_hi", axis=0, tiled=True)
+    other_core = lax.ppermute(same_core, "core", [(0, 1), (1, 0)])
+    unit_rows = jnp.concatenate([same_core, other_core], axis=0)
     gate_rows = unit_rows[:, :hidden_width]
     up_rows = unit_rows[:, hidden_width : 2 * hidden_width]
     down_rows = unit_rows[:, 2 * hidden_width : 2 * hidden_width + model_width]
@@ -102,7 +105,7 @@
     req_n = unit_rows.shape[0] // gate_weight.shape[1]
     per_group = cap // req_n
     column = lax.all_to_all(
-        permuted.reshape(req_n, per_group, quarter), "req", split_axis=0, concat_axis=0, tiled=True
+        permuted.reshape(req_n, per_group, quarter), REQ, split_axis=0, concat_axis=0, tiled=True
     ).reshape(cap, quarter)
     spread = jnp.broadcast_to(column[None], (dec_count, cap, quarter))
     quarters = lax.all_to_all(spread, "dec", split_axis=0, concat_axis=0, tiled=True)
@@ -131,26 +134,30 @@
 
 
 def solution(mesh):
+    req_size = mesh.shape["req"]
+    split = jax.sharding.Mesh(
+        mesh.devices.reshape(req_size // 2, 2, mesh.shape["dec"]), ("req_hi", "core", "dec")
+    )
     placed = (
-        P("req", "dec"),
-        P("req", "dec"),
-        P("req", "dec"),
-        P("req", "dec"),
-        P("req"),
+        P(REQ, "dec"),
+        P(REQ, "dec"),
+        P(REQ, "dec"),
+        P(REQ, "dec"),
+        P(REQ),
         P("dec", None),
         P(),
         P(),
-        P(None, ("req", "dec")),
-        P(None, ("req", "dec")),
-        P(None, ("req", "dec")),
-        P(("req", "dec"), None),
-        P("req", None),
-        P("req", None),
+        P(None, (*REQ, "dec")),
+        P(None, (*REQ, "dec")),
+        P(None, (*REQ, "dec")),
+        P((*REQ, "dec"), None),
+        P(REQ, None),
+        P(REQ, None),
     )
     return jax.shard_map(
         body,
-        mesh=mesh,
+        mesh=split,
         in_specs=placed,
-        out_specs=(P("req", "dec"), P(("req", "dec"), None, None)),
+        out_specs=(P(REQ, "dec"), P((*REQ, "dec"), None, None)),
         check_vma=False,
     )

time: 313 us -> 361 us (1.15)
  waiting for transfers between devices: 140 us -> 216 us
  blocking collectives: 50.3 us -> 25 us
  local copies, waits for them, and re-layouts: 25.9 us -> 36.2 us
  other arithmetic: 19.5 us -> 12.2 us
  starting transfers between devices: 31.1 us -> 25.9 us
    all_gather x1, waiting for transfers between devices: 0.01 us -> 87.7 us  [body(): same_core = lax.all_gather(unit_rows_local, 'req_hi', axis=0, tiled=True)]
    all_to_all x1, blocking collectives: 50.3 us -> 25 us  [body(): lax.all_to_all(permuted.reshape(req_n, per_group, quarter), REQ, split_ax...]
    all_to_all x1, waiting for transfers between devices: 47.1 us -> 36.4 us  [body(): lax.all_to_all(spread, 'dec', split_axis=0, concat_axis=0, tiled=True)]
    unnamed x17 -> x26, local copies, waits for them, and re-layouts: 0.55 us -> 7.27 us
    all_to_all x1, starting transfers between devices: 13.2 us -> 6.81 us  [body(): lax.all_to_all(spread, 'dec', split_axis=0, concat_axis=0, tiled=True)]
    concatenate x0 -> x1, local copies, waits for them, and re-layouts: none -> 5.89 us  [body(): unit_rows = jnp.concatenate([same_core, other_core], axis=0)]
  transfers between devices with their start and end apart: 5 -> 6, of which waited for: 3 -> 4; matrix products, arithmetic and copies ran while one was open for 22% -> 19% of each run, Pallas kernels for 0% -> 0%
where the time goes in v4:
time: 361 us; the launch traced here: 355 us
  waiting for transfers between devices  216 us (60%)
  local copies, waits for them, and re-layouts  36.2 us (10%)
  starting transfers between devices  25.9 us (7%)
  matrix products  25.5 us (7%)
  blocking collectives  25 us (7%)
  between operations  14.3 us (4%)
  other arithmetic  12.2 us (3%)
    all_to_all x2, waiting for transfers between devices, reduce_over_dec(): got = lax.all_to_all(pieces, 'dec', split_axis=0, concat_axis=0, tiled=True)  91.6 us
    all_gather x1, waiting for transfers between devices, body(): same_core = lax.all_gather(unit_rows_local, 'req_hi', axis=0, tiled=True)  87.7 us
    all_to_all x1, waiting for transfers between devices, body(): lax.all_to_all(spread, 'dec', split_axis=0, concat_axis=0, tiled=True)  36.4 us
    all_to_all x1, blocking collectives, body(): lax.all_to_all(permuted.reshape(req_n, per_group, quarter), REQ, split_ax...  25 us
    dot_general x1, matrix products, body(): jnp.dot(hidden_units, down_rows, preferred_element_type=jnp.float32)  11.1 us
    all_to_all x2, starting transfers between devices, reduce_over_dec(): got = lax.all_to_all(pieces, 'dec', split_axis=0, concat_axis=0, tiled=True)  10.2 us
    all_to_all x1, starting transfers between devices, body(): lax.all_to_all(ordered, 'dec', split_axis=0, concat_axis=0, tiled=True)  7.37 us
    unnamed x26, local copies, waits for them, and re-layouts  7.27 us
  transfers between devices with their start and end apart: 6, of which 4 were waited for; matrix products, arithmetic and copies ran while one was open for 19% of the time, Pallas kernels for 0%

profile of v4, /device:TPU:33, one launch (start us, length us, event | category | flops | bytes accessed | tf_op | source)
XLA Modules:
  0.0 354.8 jit_solution(14737727770543198385)
XLA Ops:
  7.2 1.8 pad_maximum_fusion
  9.0 2.0 copy.52
  13.5 2.4 fusion.58
  19.2 5.6 %all-to-all-start = ((bf16[4,512,512]{2,1,0:T(8,128)(2,1)}), bf16[4,512,512]{2,1,0:T(8,128)(2,1)S(1)}, u32[]{:S(2)}, u32[]{:S(2)}) async-start(bf16[4,512,512]{2,1,0:T(8,128)(2,1)} %bitcast.70), calls=%async_computation | async-start | bytes 4194304 | tf_op jit(solution)/shard_map/all_to_all | solution.py:39
  26.1 53.9 %all-to-all-done = bf16[4,512,512]{2,1,0:T(8,128)(2,1)S(1)} async-done(((bf16[4,512,512]{2,1,0:T(8,128)(2,1)}), bf16[4,512,512]{2,1,0:T(8,128)(2,1)S(1)}, u32[]{:S(2)}, u32[]{:S(2)}) %all-to-all-start) | async-done | bytes 2097184 | tf_op jit(solution)/shard_map/all_to_all | solution.py:39
  80.3 87.7 %all-gather.2.cloned.1.call-done = bf16[512,6272]{1,0:T(8,128)(2,1)} async-done(((bf16[16,6272]{1,0:T(8,128)(2,1)}), bf16[512,6272]{1,0:T(8,128)(2,1)}) %all-gather.2.cloned.1.call-update) | async-done | bytes 6422544 | tf_op jit(solution)/shard_map/all_gather | solution.py:68
  170.8 2.0 gather_fusion
  172.9 25.0 %all_to_all.25 = bf16[64,8,512]{2,1,0:T(8,128)(2,1)S(1)} all-to-all(bf16[64,8,512]{2,1,0:T(8,128)(2,1)S(1)} %bitcast_select_fusion), channel_id=1, replica_groups=mesh['req_hi'=32,'core'=2,'dec'=4] {'req_hi','core'}, dimensions={0} | all-to-all | bytes 1048576 | tf_op jit(solution)/shard_map/all_to_all | solution.py:107
  199.6 6.8 %all-to-all-start.2 = ((bf16[4,512,512]{1,2,0:T(8,128)(2,1)}), bf16[4,512,512]{1,2,0:T(8,128)(2,1)S(1)}, u32[]{:S(2)}, u32[]{:S(2)}) async-start(bf16[4,512,512]{1,2,0:T(8,128)(2,1)} %broadcast_in_dim.55), calls=%async_computation.2 | async-start | bytes 4194304 | tf_op jit(solution)/shard_map/all_to_all | solution.py:111
  209.5 2.3 reshape.152
  211.7 2.9 copy.48
  214.7 36.4 %all-to-all-done.2 = bf16[4,512,512]{1,2,0:T(8,128)(2,1)S(1)} async-done(((bf16[4,512,512]{1,2,0:T(8,128)(2,1)}), bf16[4,512,512]{1,2,0:T(8,128)(2,1)S(1)}, u32[]{:S(2)}, u32[]{:S(2)}) %all-to-all-start.2) | async-done | bytes 2097184 | tf_op jit(solution)/shard_map/all_to_all | solution.py:111
  251.0 7.4 %all-to-all-start.4 = ((bf16[4,2,64,2,512]{4,1,3,2,0:T(2,128)(2,1)}), bf16[4,2,64,2,512]{4,1,3,2,0:T(2,128)(2,1)}, u32[]{:S(2)}, u32[]{:S(2)}) async-start(bf16[4,2,64,2,512]{4,1,3,2,0:T(2,128)(2,1)} %copy.48), calls=%async_computation.4 | async-start | bytes 2097152 | tf_op jit(solution)/shard_map/all_to_all | solution.py:93
  259.5 6.7 %constant_dynamic-update-slice_fusion.1 = bf16[1024,6272]{1,0:T(8,128)(2,1)} fusion(bf16[512,6272]{1,0:T(8,128)(2,1)} %all-gather.2.cloned.1.call-done), kind=kLoop, calls=%fused_computation.66 | loop fusion | bytes 12845056
  266.2 5.9 %constant_dynamic-update-slice_fusion = bf16[1024,6272]{1,0:T(8,128)(2,1)} fusion(bf16[1024,6272]{1,0:T(8,128)(2,1)} %constant_dynamic-update-slice_fusion.1, bf16[512,6272]{1,0:T(8,128)(2,1)} %collective-permute-done), kind=kLoop, calls=%fused_computation.65 | loop fusion | bytes 12845056 | tf_op jit(solution)/shard_map/concatenate | solution.py:70
  272.1 6.0 %fusion.3 = f32[512,1024]{1,0:T(8,128)} fusion(bf16[512,2048]{0,1:T(8,128)(2,1)S(1)} %fusion.8, bf16[1024,6272]{1,0:T(8,128)(2,1)} %constant_dynamic-update-slice_fusion), kind=kOutput, calls=%fused_computation.4 | convolution fusion | flops 2147483648 | bytes 8388608 | tf_op jit(solution)/shard_map/dot_general | solution.py:126
  278.1 4.6 %fusion.27 = f32[512,1024]{1,0:T(8,128)} fusion(bf16[512,2048]{0,1:T(8,128)(2,1)} %copy-done.2, bf16[2048,128]{1,0:T(8,128)(2,1)S(1)} %copy-done.7, bf16[1024,6272]{1,0:T(8,128)(2,1)} %constant_dynamic-update-slice_fusion), kind=kOutput, calls=%fused_computation.39 | convolution fusion | flops 402718720 | bytes 4980736 | tf_op jit(solution)/shard_map/dot_general | solution.py:123
  282.7 11.1 %fusion.10 = bf16[512,2048]{1,0:T(8,128)(2,1)} fusion(bf16[1024,6272]{1,0:T(8,128)(2,1)} %constant_dynamic-update-slice_fusion, f32[512,1024]{1,0:T(8,128)} %fusion.3, f32[512,1024]{1,0:T(8,128)} %fusion.27, bf16[512,2048]{0,1:T(8,128)(2,1)S(1)} %copy-done.3), kind=kOutput, calls=%fused_computation.19 | convolution fusion | flops 4301783040 | bytes 16777216 | tf_op jit(solution)/shard_map/dot_general | solution.py:128
  293.8 3.1 copy.67
  296.9 4.6 %all-to-all-start.3 = ((bf16[4,512,512]{2,1,0:T(8,128)(2,1)}), bf16[4,512,512]{2,1,0:T(8,128)(2,1)}, u32[]{:S(2)}, u32[]{:S(2)}) async-start(bf16[4,512,512]{2,1,0:T(8,128)(2,1)} %bitcast.67), calls=%async_computation.3 | async-start | bytes 4194304 | tf_op jit(solution)/shard_map/all_to_all | solution.py:39
  301.5 3.0 copy.49
  304.5 2.7 reshape.153
  307.3 37.7 %all-to-all-done.3 = bf16[4,512,512]{2,1,0:T(8,128)(2,1)} async-done(((bf16[4,512,512]{2,1,0:T(8,128)(2,1)}), bf16[4,512,512]{2,1,0:T(8,128)(2,1)}, u32[]{:S(2)}, u32[]{:S(2)}) %all-to-all-start.3) | async-done | bytes 2097184 | tf_op jit(solution)/shard_map/all_to_all | solution.py:39
  345.0 2.0 convert_reduce_fusion
  (54 shorter events, 17.0 us)
Async XLA Ops:
  7.2 9.2 %copy-start = (bf16[512,2048]{1,0:T(8,128)(2,1)S(1)}, bf16[512,2048]{1,0:T(8,128)(2,1)}, u32[]{:S(2)}) copy-start(bf16[512,2048]{1,0:T(8,128)(2,1)} %param.19) | copy-start | bytes 6291460
  7.2 5.6 %copy-start.4 = (bf16[512,512]{1,0:T(8,128)(2,1)S(1)}, bf16[512,512]{1,0:T(8,128)(2,1)}, u32[]{:S(2)}) copy-start(bf16[512,512]{1,0:T(8,128)(2,1)} %param.15) | copy-start | bytes 1572868
  7.2 5.6 %copy-start.6 = (bf16[512,512]{1,0:T(8,128)(2,1)S(1)}, bf16[512,512]{1,0:T(8,128)(2,1)}, u32[]{:S(2)}) copy-start(bf16[512,512]{1,0:T(8,128)(2,1)} %param.14) | copy-start | bytes 1572868
  7.2 160.9 %all-gather.2.cloned.1.call-start = ((), (), s32[]{:S(2)}) async-start(), calls=%async_computation.5 | async-start | bytes 6623232 | tf_op jit(solution)/shard_map/all_gather | solution.py:68
  13.5 2.4 copy-start.8
  19.2 6.1 %copy-start.10 = (s32[1,512]{1,0:T(1,128)S(1)}, s32[1,512]{1,0:T(1,128)}, u32[]{:S(2)}) copy-start(s32[1,512]{1,0:T(1,128)} %param.26) | copy-start | bytes 6148
  19.2 60.8 %all-to-all-start = ((bf16[4,512,512]{2,1,0:T(8,128)(2,1)}), bf16[4,512,512]{2,1,0:T(8,128)(2,1)S(1)}, u32[]{:S(2)}, u32[]{:S(2)}) async-start(bf16[4,512,512]{2,1,0:T(8,128)(2,1)} %bitcast.70), calls=%async_computation | async-start | bytes 4194304 | tf_op jit(solution)/shard_map/all_to_all | solution.py:39
  168.1 98.1 %collective-permute-start = (bf16[512,6272]{1,0:T(8,128)(2,1)}, bf16[512,6272]{1,0:T(8,128)(2,1)}, u32[]{:S(2)}, u32[]{:S(2)}) collective-permute-start(bf16[512,6272]{1,0:T(8,128)(2,1)} %all-gather.2.cloned.1.call-done), channel_id=1, source_target_pairs={{0,4},{4,0},{1,5},{5,1},{2,6},{6,2},{3,7},{7,3},{8,12},{12,8},{9,1... | collective-permute-start | bytes 19267592 | tf_op jit(solution)/shard_map/ppermute | solution.py:69
  199.6 8.2 %copy-start.5 = (bf16[512,512]{1,0:T(8,128)(2,1)S(1)}, bf16[512,512]{1,0:T(8,128)(2,1)}, u32[]{:S(2)}) copy-start(bf16[512,512]{1,0:T(8,128)(2,1)} %param.15) | copy-start | bytes 1572868
  199.6 51.4 %all-to-all-start.2 = ((bf16[4,512,512]{1,2,0:T(8,128)(2,1)}), bf16[4,512,512]{1,2,0:T(8,128)(2,1)S(1)}, u32[]{:S(2)}, u32[]{:S(2)}) async-start(bf16[4,512,512]{1,2,0:T(8,128)(2,1)} %broadcast_in_dim.55), calls=%async_computation.2 | async-start | bytes 4194304 | tf_op jit(solution)/shard_map/all_to_all | solution.py:111
  206.4 1.7 copy-start.11
  214.7 44.3 %copy-start.9 = (f32[2048]{0:T(1024)S(1)}, f32[2048]{0:T(1024)}, u32[]{:S(2)}) copy-start(f32[2048]{0:T(1024)} %param.20) | copy-start | bytes 24580
  251.0 45.9 %all-to-all-start.4 = ((bf16[4,2,64,2,512]{4,1,3,2,0:T(2,128)(2,1)}), bf16[4,2,64,2,512]{4,1,3,2,0:T(2,128)(2,1)}, u32[]{:S(2)}, u32[]{:S(2)}) async-start(bf16[4,2,64,2,512]{4,1,3,2,0:T(2,128)(2,1)} %copy.48), calls=%async_computation.4 | async-start | bytes 2097152 | tf_op jit(solution)/shard_map/all_to_all | solution.py:93
  259.5 12.6 %copy-start.2 = (bf16[512,2048]{0,1:T(8,128)(2,1)}, bf16[512,2048]{0,1:T(8,128)(2,1)S(1)}, u32[]{:S(2)}) copy-start(bf16[512,2048]{0,1:T(8,128)(2,1)S(1)} %fusion.8) | copy-start | bytes 6291460
  272.1 6.0 %copy-start.7 = (bf16[2048,128]{1,0:T(8,128)(2,1)S(1)}, bf16[2048,128]{1,0:T(8,128)(2,1)}, u32[]{:S(2)}) copy-start(bf16[2048,128]{1,0:T(8,128)(2,1)} %param.21) | copy-start | bytes 1572868
  278.1 4.6 %copy-start.3 = (bf16[512,2048]{0,1:T(8,128)(2,1)S(1)}, bf16[512,2048]{0,1:T(8,128)(2,1)}, u32[]{:S(2)}) copy-start(bf16[512,2048]{0,1:T(8,128)(2,1)} %copy-done.2) | copy-start | bytes 6291460
  296.9 48.1 %all-to-all-start.3 = ((bf16[4,512,512]{2,1,0:T(8,128)(2,1)}), bf16[4,512,512]{2,1,0:T(8,128)(2,1)}, u32[]{:S(2)}, u32[]{:S(2)}) async-start(bf16[4,512,512]{2,1,0:T(8,128)(2,1)} %bitcast.67), calls=%async_computation.3 | async-start | bytes 4194304 | tf_op jit(solution)/shard_map/all_to_all | solution.py:39
  304.5 43.4 %copy-start.1 = (bf16[512,2048]{1,0:T(8,128)(2,1)S(1)}, bf16[512,2048]{1,0:T(8,128)(2,1)}, u32[]{:S(2)}) copy-start(bf16[512,2048]{1,0:T(8,128)(2,1)} %param.19) | copy-start | bytes 6291460
Sparse Core Ops, SparseCore 0:
  12.1 155.9 all-gather.1

commit v5 on v2

--- a/solution.py
+++ b/solution.py
@@ -32,11 +32,26 @@
 
 
 def reduce_over_dec(part, dec_count):
-    rows = part.shape[0]
     quarter = part.shape[1] // dec_count
-    pieces = part.reshape(rows, dec_count, quarter).transpose(1, 0, 2)
-    got = lax.all_to_all(pieces, "dec", split_axis=0, concat_axis=0, tiled=True)
-    return jnp.sum(got.astype(jnp.float32), axis=0)
+    here = lax.axis_index("dec")
+    total = lax.dynamic_slice_in_dim(part, here * quarter, quarter, 1).astype(jnp.float32)
+    for shift in range(1, dec_count):
+        piece = lax.dynamic_slice_in_dim(part, ((here + shift) % dec_count) * quarter, quarter, 1)
+        pairs = [(i, (i + shift) % dec_count) for i in range(dec_count)]
+        total = total + lax.ppermute(piece, "dec", pairs).astype(jnp.float32)
+    return total
+
+
+def gather_over_dec(column, dec_count):
+    here = lax.axis_index("dec")
+    arrived = [column]
+    for shift in range(1, dec_count):
+        pairs = [(i, (i + shift) % dec_count) for i in range(dec_count)]
+        arrived.append(lax.ppermute(column, "dec", pairs))
+    stacked = jnp.stack(arrived)
+    by_quarter = jnp.take(stacked, (here - jnp.arange(dec_count)) % dec_count, axis=0)
+    rows = column.shape[0]
+    return by_quarter.transpose(1, 0, 2).reshape(rows, dec_count * column.shape[1])
 
 
 def body(
@@ -104,9 +119,7 @@
     column = lax.all_to_all(
         permuted.reshape(req_n, per_group, quarter), "req", split_axis=0, concat_axis=0, tiled=True
     ).reshape(cap, quarter)
-    spread = jnp.broadcast_to(column[None], (dec_count, cap, quarter))
-    quarters = lax.all_to_all(spread, "dec", split_axis=0, concat_axis=0, tiled=True)
-    mixed_rows = quarters.transpose(1, 0, 2).reshape(cap, dec_count * quarter)
+    mixed_rows = gather_over_dec(column, dec_count)
 
     values_f = mixed_rows.astype(jnp.float32)
     scale = lax.rsqrt(jnp.mean(values_f * values_f, axis=-1, keepdims=True) + 1e-05)

time: 313 us -> 317 us (1.013)
  waiting for transfers between devices: 140 us -> 196 us
  blocking collectives: 50.3 us -> 0 us
  starting transfers between devices: 31.1 us -> 34.7 us
    ppermute x0 -> x9, waiting for transfers between devices: none -> 156 us  [the longest x6 96.6 us: reduce_over_dec(): total = total + lax.ppermute(piece, 'dec', pairs).astype(jnp.float32)]
    all_to_all x3 -> x1, waiting for transfers between devices: 140 us -> 39.8 us  [body(): lax.all_to_all(permuted.reshape(req_n, per_group, quarter), 'req', split_...]
    all_to_all x1 -> x0, blocking collectives: 50.3 us -> none  [body(): lax.all_to_all(permuted.reshape(req_n, per_group, quarter), 'req', split_...]
    ppermute x0 -> x9, starting transfers between devices: none -> 15.8 us  [the longest x6 14.4 us: reduce_over_dec(): total = total + lax.ppermute(piece, 'dec', pairs).astype(jnp.float32)]
    all_to_all x3 -> x1, starting transfers between devices: 23.5 us -> 13.4 us  [body(): lax.all_to_all(permuted.reshape(req_n, per_group, quarter), 'req', split_...]
    reshape x3 -> x0, local copies, waits for them, and re-layouts: 5.63 us -> none  [the longest x2 4.62 us: reduce_over_dec(): pieces = part.reshape(rows, dec_count, quarter).transpose(1, 0, 2)]
    convert_element_type x0 -> x1, local copies, waits for them, and re-layouts: none -> 5.23 us  [body(): values_f = mixed_rows.astype(jnp.float32)]
    reduce_sum x2 -> x0, other arithmetic: 4.05 us -> none  [reduce_over_dec(): return jnp.sum(got.astype(jnp.float32), axis=0)]
  transfers between devices with their start and end apart: 5 -> 12, of which waited for: 3 -> 9; matrix products, arithmetic and copies ran while one was open for 22% -> 20% of each run, Pallas kernels for 0% -> 0%
where the time goes in v5:
time: 317 us; the launch traced here: 313 us
  waiting for transfers between devices  196 us (62%)
  starting transfers between devices  34.7 us (11%)
  local copies, waits for them, and re-layouts  24.6 us (8%)
  matrix products  23.5 us (7%)
  other arithmetic  20.2 us (6%)
  between operations  14.4 us (5%)
    ppermute x6, waiting for transfers between devices, reduce_over_dec(): total = total + lax.ppermute(piece, 'dec', pairs).astype(jnp.float32)  96.6 us
    ppermute x3, waiting for transfers between devices, gather_over_dec(): arrived.append(lax.ppermute(column, 'dec', pairs))  59.7 us
    all_to_all x1, waiting for transfers between devices, body(): lax.all_to_all(permuted.reshape(req_n, per_group, quarter), 'req', split_...  39.8 us
    ppermute x6, starting transfers between devices, reduce_over_dec(): total = total + lax.ppermute(piece, 'dec', pairs).astype(jnp.float32)  14.4 us
    all_to_all x1, starting transfers between devices, body(): lax.all_to_all(permuted.reshape(req_n, per_group, quarter), 'req', split_...  13.4 us
    dot_general x1, matrix products, body(): jnp.dot(hidden_units, down_rows, preferred_element_type=jnp.float32)  10.9 us
  transfers between devices with their start and end apart: 12, of which 9 were waited for; matrix products, arithmetic and copies ran while one was open for 20% of the time, Pallas kernels for 0%

profile of v5, /device:TPU:33, one launch (start us, length us, event | category | flops | bytes accessed | tf_op | source)
XLA Modules:
  0.0 313.4 jit_solution(3881153383850298905)
XLA Ops:
  13.6 2.4 fusion.61
  25.0 8.9 %collective-permute-done = bf16[512,512]{1,0:T(8,128)(2,1)S(1)} collective-permute-done((bf16[512,512]{1,0:T(8,128)(2,1)S(1)}, bf16[512,512]{1,0:T(8,128)(2,1)S(1)}, u32[]{:S(2)}, u32[]{:S(2)}) %collective-permute-start) | collective-permute-done | bytes 524320 | tf_op jit(solution)/shard_map/ppermute | solution.py:41
  34.0 40.8 %collective-permute-done.1 = bf16[512,512]{1,0:T(8,128)(2,1)} collective-permute-done((bf16[512,512]{1,0:T(8,128)(2,1)S(1)}, bf16[512,512]{1,0:T(8,128)(2,1)}, u32[]{:S(2)}, u32[]{:S(2)}) %collective-permute-start.1) | collective-permute-done | bytes 524320 | tf_op jit(solution)/shard_map/ppermute | solution.py:41
  74.7 8.0 %collective-permute-done.2 = bf16[512,512]{1,0:T(8,128)(2,1)} collective-permute-done((bf16[512,512]{1,0:T(8,128)(2,1)S(1)}, bf16[512,512]{1,0:T(8,128)(2,1)}, u32[]{:S(2)}, u32[]{:S(2)}) %collective-permute-start.2) | collective-permute-done | bytes 524320 | tf_op jit(solution)/shard_map/ppermute | solution.py:41
  87.4 13.4 %all-to-all-start = ((bf16[64,8,512]{2,1,0:T(8,128)(2,1)}), bf16[64,8,512]{2,1,0:T(8,128)(2,1)S(1)}, u32[]{:S(2)}, u32[]{:S(2)}) async-start(bf16[64,8,512]{2,1,0:T(8,128)(2,1)} %bitcast_select_fusion), calls=%async_computation | async-start | bytes 1048576 | tf_op jit(solution)/shard_map/all_to_all | solution.py:119
  101.4 39.8 %all-to-all-done = bf16[64,8,512]{2,1,0:T(8,128)(2,1)S(1)} async-done(((bf16[64,8,512]{2,1,0:T(8,128)(2,1)}), bf16[64,8,512]{2,1,0:T(8,128)(2,1)S(1)}, u32[]{:S(2)}, u32[]{:S(2)}) %all-to-all-start) | async-done | bytes 524320 | tf_op jit(solution)/shard_map/all_to_all | solution.py:119
  145.3 5.4 %all-to-all-start.1 = ((bf16[4,2,64,2,512]{4,1,3,2,0:T(2,128)(2,1)}), bf16[4,2,64,2,512]{4,1,3,2,0:T(2,128)(2,1)}, u32[]{:S(2)}, u32[]{:S(2)}) async-start(bf16[4,2,64,2,512]{4,1,3,2,0:T(2,128)(2,1)} %copy.44), calls=%async_computation.1 | async-start | bytes 2097152 | tf_op jit(solution)/shard_map/all_to_all | solution.py:105
  150.7 49.3 %collective-permute-done.5 = bf16[512,512]{1,0:T(8,128)(2,1)S(1)} collective-permute-done((bf16[512,512]{1,0:T(8,128)(2,1)S(1)}, bf16[512,512]{1,0:T(8,128)(2,1)S(1)}, u32[]{:S(2)}, u32[]{:S(2)}) %collective-permute-start.5) | collective-permute-done | bytes 524320 | tf_op jit(solution)/shard_map/ppermute | solution.py:50
  200.0 10.4 %collective-permute-done.4 = bf16[512,512]{1,0:T(8,128)(2,1)} collective-permute-done((bf16[512,512]{1,0:T(8,128)(2,1)S(1)}, bf16[512,512]{1,0:T(8,128)(2,1)}, u32[]{:S(2)}, u32[]{:S(2)}) %collective-permute-start.4) | collective-permute-done | bytes 524320 | tf_op jit(solution)/shard_map/ppermute | solution.py:50
  210.4 2.8 pad_maximum_fusion
  217.7 5.2 %copy.41 = f32[512,4,512]{0,2,1:T(8,128)} copy(f32[512,4,512]{2,0,1:T(8,128)} %convert_bitcast_fusion) | data formatting | bytes 8388608 | tf_op jit(solution)/shard_map/convert_element_type | solution.py:124
  223.7 2.6 fusion.9
  226.3 5.9 %fusion.6 = f32[512,1024]{1,0:T(8,128)} fusion(bf16[512,2048]{0,1:T(8,128)(2,1)S(1)} %fusion.9, bf16[1024,6272]{1,0:T(8,128)(2,1)} %all-gather.2.cloned.1.call-done), kind=kOutput, calls=%fused_computation.10 | convolution fusion | flops 2147483648 | bytes 8388608 | tf_op jit(solution)/shard_map/dot_general | solution.py:131
  232.3 3.8 %fusion.32 = f32[512,1024]{1,0:T(8,128)} fusion(bf16[512,2048]{0,1:T(8,128)(2,1)S(1)} %fusion.9, bf16[2048,128]{1,0:T(8,128)(2,1)S(1)} %copy-done.6, bf16[1024,6272]{1,0:T(8,128)(2,1)} %all-gather.2.cloned.1.call-done), kind=kOutput, calls=%fused_computation.40 | convolution fusion | flops 402718720 | bytes 4980736 | tf_op jit(solution)/shard_map/dot_general | solution.py:133
  236.1 10.9 %fusion.11 = bf16[512,2048]{1,0:T(8,128)(2,1)} fusion(bf16[1024,6272]{1,0:T(8,128)(2,1)} %all-gather.2.cloned.1.call-done, f32[512,1024]{1,0:T(8,128)} %fusion.6, f32[512,1024]{1,0:T(8,128)} %fusion.32, bf16[512,2048]{0,1:T(8,128)(2,1)S(1)} %fusion.9), kind=kOutput, calls=%fused_computation.20 | convolution fusion | flops 4301783040 | bytes 16777216 | tf_op jit(solution)/shard_map/dot_general | solution.py:138
  247.0 2.5 constant_dynamic-slice_fusion.2
  249.5 5.7 %collective-permute-start.6 = (bf16[512,512]{1,0:T(8,128)(2,1)}, bf16[512,512]{1,0:T(8,128)(2,1)}, u32[]{:S(2)}, u32[]{:S(2)}) collective-permute-start(bf16[512,512]{1,0:T(8,128)(2,1)} %get-tuple-element.2), channel_id=1, source_target_pairs={{0,1},{1,2},{2,3},{3,0},{4,5},{5,6},{6,7},{7,4},{8,9},{9,10},{10,1... | collective-permute-start | bytes 1572872 | tf_op jit(solution)/shard_map/ppermute | solution.py:41
  255.2 4.1 %collective-permute-start.7 = (bf16[512,512]{1,0:T(8,128)(2,1)}, bf16[512,512]{1,0:T(8,128)(2,1)}, u32[]{:S(2)}, u32[]{:S(2)}) collective-permute-start(bf16[512,512]{1,0:T(8,128)(2,1)} %get-tuple-element.4), channel_id=1, source_target_pairs={{0,2},{1,3},{2,0},{3,1},{4,6},{5,7},{6,4},{7,5},{8,10},{9,11},{10,... | collective-permute-start | bytes 1572872 | tf_op jit(solution)/shard_map/ppermute | solution.py:41
  259.3 3.0 copy.45
  262.3 2.7 reshape.198
  265.0 4.2 %collective-permute-done.6 = bf16[512,512]{1,0:T(8,128)(2,1)} collective-permute-done((bf16[512,512]{1,0:T(8,128)(2,1)}, bf16[512,512]{1,0:T(8,128)(2,1)}, u32[]{:S(2)}, u32[]{:S(2)}) %collective-permute-start.6) | collective-permute-done | bytes 524320 | tf_op jit(solution)/shard_map/ppermute | solution.py:41
  269.3 30.7 %collective-permute-done.7 = bf16[512,512]{1,0:T(8,128)(2,1)} collective-permute-done((bf16[512,512]{1,0:T(8,128)(2,1)}, bf16[512,512]{1,0:T(8,128)(2,1)}, u32[]{:S(2)}, u32[]{:S(2)}) %collective-permute-start.7) | collective-permute-done | bytes 524320 | tf_op jit(solution)/shard_map/ppermute | solution.py:41
  299.9 4.0 %collective-permute-done.8 = bf16[512,512]{1,0:T(8,128)(2,1)} collective-permute-done((bf16[512,512]{1,0:T(8,128)(2,1)S(1)}, bf16[512,512]{1,0:T(8,128)(2,1)}, u32[]{:S(2)}, u32[]{:S(2)}) %collective-permute-start.8) | collective-permute-done | bytes 524320 | tf_op jit(solution)/shard_map/ppermute | solution.py:41
  303.9 2.6 add_convert_fusion
  (66 shorter events, 29.8 us)
Async XLA Ops:
  7.2 9.3 %copy-start = (bf16[512,2048]{1,0:T(8,128)(2,1)S(1)}, bf16[512,2048]{1,0:T(8,128)(2,1)}, u32[]{:S(2)}) copy-start(bf16[512,2048]{1,0:T(8,128)(2,1)} %param.19) | copy-start | bytes 6291460
  7.2 5.6 %copy-start.5 = (bf16[512,512]{1,0:T(8,128)(2,1)S(1)}, bf16[512,512]{1,0:T(8,128)(2,1)}, u32[]{:S(2)}) copy-start(bf16[512,512]{1,0:T(8,128)(2,1)} %param.14) | copy-start | bytes 1572868
  7.2 5.6 %copy-start.2 = (bf16[512,512]{1,0:T(8,128)(2,1)S(1)}, bf16[512,512]{1,0:T(8,128)(2,1)}, u32[]{:S(2)}) copy-start(bf16[512,512]{1,0:T(8,128)(2,1)} %param.15) | copy-start | bytes 1572868
  7.2 219.1 %all-gather.2.cloned.1.call-start = ((), (), s32[]{:S(2)}) async-start(), calls=%async_computation.2 | async-start | bytes 13045760 | tf_op jit(solution)/shard_map/all_gather | solution.py:82
  13.5 2.4 copy-start.7
  17.7 1.3 copy-start.3
  19.0 5.2 %copy-start.10 = (s32[1,512]{1,0:T(1,128)S(1)}, s32[1,512]{1,0:T(1,128)}, u32[]{:S(2)}) copy-start(s32[1,512]{1,0:T(1,128)} %param.26) | copy-start | bytes 6148
  19.0 63.8 %copy-start.8 = (bf16[512,512]{1,0:T(8,128)(2,1)S(1)}, bf16[512,512]{1,0:T(8,128)(2,1)}, u32[]{:S(2)}) copy-start(bf16[512,512]{1,0:T(8,128)(2,1)} %param.17) | copy-start | bytes 1572868
  19.2 14.8 %collective-permute-start = (bf16[512,512]{1,0:T(8,128)(2,1)S(1)}, bf16[512,512]{1,0:T(8,128)(2,1)S(1)}, u32[]{:S(2)}, u32[]{:S(2)}) collective-permute-start(bf16[512,512]{1,0:T(8,128)(2,1)S(1)} %get-tuple-element.5), channel_id=1, source_target_pairs={{0,1},{1,2},{2,3},{3,0},{4,5},{5,6},{6,7},{7,4},{8,9},{9,10},{10,1... | collective-permute-start | bytes 1572872 | tf_op jit(solution)/shard_map/ppermute | solution.py:41
  20.9 53.8 %collective-permute-start.1 = (bf16[512,512]{1,0:T(8,128)(2,1)S(1)}, bf16[512,512]{1,0:T(8,128)(2,1)}, u32[]{:S(2)}, u32[]{:S(2)}) collective-permute-start(bf16[512,512]{1,0:T(8,128)(2,1)S(1)} %get-tuple-element.7), channel_id=1, source_target_pairs={{0,2},{1,3},{2,0},{3,1},{4,6},{5,7},{6,4},{7,5},{8,10},{9,11},{10,... | collective-permute-start | bytes 1572872 | tf_op jit(solution)/shard_map/ppermute | solution.py:41
  22.4 60.4 %collective-permute-start.2 = (bf16[512,512]{1,0:T(8,128)(2,1)S(1)}, bf16[512,512]{1,0:T(8,128)(2,1)}, u32[]{:S(2)}, u32[]{:S(2)}) collective-permute-start(bf16[512,512]{1,0:T(8,128)(2,1)S(1)} %get-tuple-element.6), channel_id=1, source_target_pairs={{0,3},{1,0},{2,1},{3,2},{4,7},{5,4},{6,5},{7,6},{8,11},{9,8},{10,9... | collective-permute-start | bytes 1572872 | tf_op jit(solution)/shard_map/ppermute | solution.py:41
  86.4 14.7 %copy-start.4 = (bf16[512,512]{1,0:T(8,128)(2,1)S(1)}, bf16[512,512]{1,0:T(8,128)(2,1)}, u32[]{:S(2)}) copy-start(bf16[512,512]{1,0:T(8,128)(2,1)} %param.16) | copy-start | bytes 1572868
  86.5 56.2 %copy-start.11 = (s32[1,8]{1,0:T(1,128)S(1)}, s32[1,8]{1,0:T(1,128)}, u32[]{:S(2)}) copy-start(s32[1,8]{1,0:T(1,128)} %param.27) | copy-start | bytes 100
  87.4 53.8 %all-to-all-start = ((bf16[64,8,512]{2,1,0:T(8,128)(2,1)}), bf16[64,8,512]{2,1,0:T(8,128)(2,1)S(1)}, u32[]{:S(2)}, u32[]{:S(2)}) async-start(bf16[64,8,512]{2,1,0:T(8,128)(2,1)} %bitcast_select_fusion), calls=%async_computation | async-start | bytes 1048576 | tf_op jit(solution)/shard_map/all_to_all | solution.py:119
  141.2 58.8 %collective-permute-start.5 = (bf16[512,512]{1,0:T(8,128)(2,1)S(1)}, bf16[512,512]{1,0:T(8,128)(2,1)S(1)}, u32[]{:S(2)}, u32[]{:S(2)}) collective-permute-start(bf16[512,512]{1,0:T(8,128)(2,1)S(1)} %bitcast.62), channel_id=1, source_target_pairs={{0,3},{1,0},{2,1},{3,2},{4,7},{5,4},{6,5},{7,6},{8,11},{9,8},{10,9... | collective-permute-start | bytes 1572872 | tf_op jit(solution)/shard_map/ppermute | solution.py:50
  141.2 58.8 %collective-permute-start.3 = (bf16[512,512]{1,0:T(8,128)(2,1)S(1)}, bf16[512,512]{1,0:T(8,128)(2,1)}, u32[]{:S(2)}, u32[]{:S(2)}) collective-permute-start(bf16[512,512]{1,0:T(8,128)(2,1)S(1)} %bitcast.63), channel_id=1, source_target_pairs={{0,1},{1,2},{2,3},{3,0},{4,5},{5,6},{6,7},{7,4},{8,9},{9,10},{10,1... | collective-permute-start | bytes 1572872 | tf_op jit(solution)/shard_map/ppermute | solution.py:50
  142.7 67.7 %collective-permute-start.4 = (bf16[512,512]{1,0:T(8,128)(2,1)S(1)}, bf16[512,512]{1,0:T(8,128)(2,1)}, u32[]{:S(2)}, u32[]{:S(2)}) collective-permute-start(bf16[512,512]{1,0:T(8,128)(2,1)S(1)} %bitcast.64), channel_id=1, source_target_pairs={{0,2},{1,3},{2,0},{3,1},{4,6},{5,7},{6,4},{7,5},{8,10},{9,11},{10,... | collective-permute-start | bytes 1572872 | tf_op jit(solution)/shard_map/ppermute | solution.py:50
  145.3 114.0 %all-to-all-start.1 = ((bf16[4,2,64,2,512]{4,1,3,2,0:T(2,128)(2,1)}), bf16[4,2,64,2,512]{4,1,3,2,0:T(2,128)(2,1)}, u32[]{:S(2)}, u32[]{:S(2)}) async-start(bf16[4,2,64,2,512]{4,1,3,2,0:T(2,128)(2,1)} %copy.44), calls=%async_computation.1 | async-start | bytes 2097152 | tf_op jit(solution)/shard_map/all_to_all | solution.py:105
  223.0 0.7 copy-start.9
  226.3 6.0 %copy-start.6 = (bf16[2048,128]{1,0:T(8,128)(2,1)S(1)}, bf16[2048,128]{1,0:T(8,128)(2,1)}, u32[]{:S(2)}) copy-start(bf16[2048,128]{1,0:T(8,128)(2,1)} %param.21) | copy-start | bytes 1572868
  249.5 19.8 %collective-permute-start.6 = (bf16[512,512]{1,0:T(8,128)(2,1)}, bf16[512,512]{1,0:T(8,128)(2,1)}, u32[]{:S(2)}, u32[]{:S(2)}) collective-permute-start(bf16[512,512]{1,0:T(8,128)(2,1)} %get-tuple-element.2), channel_id=1, source_target_pairs={{0,1},{1,2},{2,3},{3,0},{4,5},{5,6},{6,7},{7,4},{8,9},{9,10},{10,1... | collective-permute-start | bytes 1572872 | tf_op jit(solution)/shard_map/ppermute | solution.py:41
  255.2 44.7 %collective-permute-start.7 = (bf16[512,512]{1,0:T(8,128)(2,1)}, bf16[512,512]{1,0:T(8,128)(2,1)}, u32[]{:S(2)}, u32[]{:S(2)}) collective-permute-start(bf16[512,512]{1,0:T(8,128)(2,1)} %get-tuple-element.4), channel_id=1, source_target_pairs={{0,2},{1,3},{2,0},{3,1},{4,6},{5,7},{6,4},{7,5},{8,10},{9,11},{10,... | collective-permute-start | bytes 1572872 | tf_op jit(solution)/shard_map/ppermute | solution.py:41
  259.3 44.6 %collective-permute-start.8 = (bf16[512,512]{1,0:T(8,128)(2,1)S(1)}, bf16[512,512]{1,0:T(8,128)(2,1)}, u32[]{:S(2)}, u32[]{:S(2)}) collective-permute-start(bf16[512,512]{1,0:T(8,128)(2,1)S(1)} %get-tuple-element.3), channel_id=1, source_target_pairs={{0,3},{1,0},{2,1},{3,2},{4,7},{5,4},{6,5},{7,6},{8,11},{9,8},{10,9... | collective-permute-start | bytes 1572872 | tf_op jit(solution)/shard_map/ppermute | solution.py:41
  262.3 44.3 %copy-start.1 = (bf16[512,2048]{1,0:T(8,128)(2,1)S(1)}, bf16[512,2048]{1,0:T(8,128)(2,1)}, u32[]{:S(2)}) copy-start(bf16[512,2048]{1,0:T(8,128)(2,1)} %param.19) | copy-start | bytes 6291460
Sparse Core Ops, SparseCore 0:
  11.7 188.1 all-gather.1

commit v6 on v2

--- a/solution.py
+++ b/solution.py
@@ -32,11 +32,14 @@
 
 
 def reduce_over_dec(part, dec_count):
-    rows = part.shape[0]
     quarter = part.shape[1] // dec_count
-    pieces = part.reshape(rows, dec_count, quarter).transpose(1, 0, 2)
-    got = lax.all_to_all(pieces, "dec", split_axis=0, concat_axis=0, tiled=True)
-    return jnp.sum(got.astype(jnp.float32), axis=0)
+    here = lax.axis_index("dec")
+    total = lax.dynamic_slice_in_dim(part, here * quarter, quarter, 1).astype(jnp.float32)
+    for shift in range(1, dec_count):
+        piece = lax.dynamic_slice_in_dim(part, ((here + shift) % dec_count) * quarter, quarter, 1)
+        pairs = [(i, (i + shift) % dec_count) for i in range(dec_count)]
+        total = total + lax.ppermute(piece, "dec", pairs).astype(jnp.float32)
+    return total
 
 
 def body(
@@ -87,8 +90,6 @@
     ).astype(jnp.bfloat16)
     per_dev = block_count // dec_count
     ordered = ordered.reshape(dec_count, per_dev, block_slots, 2, features)
-    moved = lax.all_to_all(ordered, "dec", split_axis=0, concat_axis=0, tiled=True)
-    kv_cache = moved.transpose(1, 2, 3, 0, 4).reshape(per_dev, block_slots, 2 * dec_count * features)
 
     attn = attend(queries, keys, values, seg_ids)
     partial_value = jnp.dot(attn, out_weight, preferred_element_type=jnp.float32).astype(
@@ -107,6 +108,9 @@
     spread = jnp.broadcast_to(column[None], (dec_count, cap, quarter))
     quarters = lax.all_to_all(spread, "dec", split_axis=0, concat_axis=0, tiled=True)
     mixed_rows = quarters.transpose(1, 0, 2).reshape(cap, dec_count * quarter)
+    mixed_rows, ordered = lax.optimization_barrier((mixed_rows, ordered))
+    moved = lax.all_to_all(ordered, "dec", split_axis=0, concat_axis=0, tiled=True)
+    kv_cache = moved.transpose(1, 2, 3, 0, 4).reshape(per_dev, block_slots, 2 * dec_count * features)
 
     values_f = mixed_rows.astype(jnp.float32)
     scale = lax.rsqrt(jnp.mean(values_f * values_f, axis=-1, keepdims=True) + 1e-05)

time: 313 us -> 307 us (0.981); the launches traced: 307 us -> 306 us
  blocking collectives: 50.3 us -> 63.6 us
  starting transfers between devices: 31.1 us -> 23.3 us
  other arithmetic: 19.5 us -> 14.4 us
    ppermute x0 -> x6, waiting for transfers between devices: none -> 97.5 us  [reduce_over_dec(): total = total + lax.ppermute(piece, 'dec', pairs).astype(jnp.float32)]
    all_to_all x2 -> x0, waiting for transfers between devices: 92.7 us -> none  [reduce_over_dec(): got = lax.all_to_all(pieces, 'dec', split_axis=0, concat_axis=0, tiled=True)]
    all_to_all x1, blocking collectives: 50.3 us -> 63.6 us  [body(): lax.all_to_all(permuted.reshape(req_n, per_group, quarter), 'req', split_...]
    all_to_all x2 -> x0, starting transfers between devices: 10.2 us -> none  [reduce_over_dec(): got = lax.all_to_all(pieces, 'dec', split_axis=0, concat_axis=0, tiled=True)]
    all_to_all x1, starting transfers between devices: 13.2 us -> 4.43 us  [body(): lax.all_to_all(spread, 'dec', split_axis=0, concat_axis=0, tiled=True)]
    ppermute x0 -> x6, starting transfers between devices: none -> 8.02 us  [reduce_over_dec(): total = total + lax.ppermute(piece, 'dec', pairs).astype(jnp.float32)]
    all_to_all x1, waiting for transfers between devices: 47.1 us -> 39.5 us  [body(): lax.all_to_all(spread, 'dec', split_axis=0, concat_axis=0, tiled=True)]
    reshape x2 -> x0, local copies, waits for them, and re-layouts: 4.62 us -> none  [reduce_over_dec(): pieces = part.reshape(rows, dec_count, quarter).transpose(1, 0, 2)]
  transfers between devices with their start and end apart: 5 -> 9, of which waited for: 3 -> 7; matrix products, arithmetic and copies ran while one was open for 22% -> 20% of each run, Pallas kernels for 0% -> 0%
where the time goes in v6:
time: 307 us; the launch traced here: 306 us
  waiting for transfers between devices  137 us (45%)
  blocking collectives  63.6 us (21%)
  matrix products  27.6 us (9%)
  local copies, waits for them, and re-layouts  26.2 us (9%)
  starting transfers between devices  23.3 us (8%)
  other arithmetic  14.4 us (5%)
  between operations  14.3 us (5%)
    ppermute x6, waiting for transfers between devices, reduce_over_dec(): total = total + lax.ppermute(piece, 'dec', pairs).astype(jnp.float32)  97.5 us
    all_to_all x1, blocking collectives, body(): lax.all_to_all(permuted.reshape(req_n, per_group, quarter), 'req', split_...  63.6 us
    all_to_all x1, waiting for transfers between devices, body(): lax.all_to_all(spread, 'dec', split_axis=0, concat_axis=0, tiled=True)  39.5 us
    dot_general x1, matrix products, body(): jnp.dot(hidden_units, down_rows, preferred_element_type=jnp.float32)  12 us
    all_to_all x1, starting transfers between devices, body(): lax.all_to_all(ordered, 'dec', split_axis=0, concat_axis=0, tiled=True)  10.8 us
    ppermute x6, starting transfers between devices, reduce_over_dec(): total = total + lax.ppermute(piece, 'dec', pairs).astype(jnp.float32)  8.02 us
    dot_general x1, matrix products, body(): lax.dot_general(normed, gate_rows, contract, preferred_element_type=jnp.f...  6.99 us
  transfers between devices with their start and end apart: 9, of which 7 were waited for; matrix products, arithmetic and copies ran while one was open for 20% of the time, Pallas kernels for 0%

profile of v6, /device:TPU:33, one launch (start us, length us, event | category | flops | bytes accessed | tf_op | source)
XLA Modules:
  0.0 306.4 jit_solution(12716044753304133485)
XLA Ops:
  9.1 2.0 copy.48
  13.5 2.4 fusion.63
  25.9 9.9 %collective-permute-done = bf16[512,512]{1,0:T(8,128)(2,1)} collective-permute-done((bf16[512,512]{1,0:T(8,128)(2,1)}, bf16[512,512]{1,0:T(8,128)(2,1)}, u32[]{:S(2)}, u32[]{:S(2)}) %collective-permute-start) | collective-permute-done | bytes 524320 | tf_op jit(solution)/shard_map/ppermute | solution.py:41
  35.8 40.1 %collective-permute-done.1 = bf16[512,512]{1,0:T(8,128)(2,1)} collective-permute-done((bf16[512,512]{1,0:T(8,128)(2,1)}, bf16[512,512]{1,0:T(8,128)(2,1)}, u32[]{:S(2)}, u32[]{:S(2)}) %collective-permute-start.1) | collective-permute-done | bytes 524320 | tf_op jit(solution)/shard_map/ppermute | solution.py:41
  75.9 7.9 %collective-permute-done.2 = bf16[512,512]{1,0:T(8,128)(2,1)} collective-permute-done((bf16[512,512]{1,0:T(8,128)(2,1)S(1)}, bf16[512,512]{1,0:T(8,128)(2,1)}, u32[]{:S(2)}, u32[]{:S(2)}) %collective-permute-start.2) | collective-permute-done | bytes 524320 | tf_op jit(solution)/shard_map/ppermute | solution.py:41
  85.9 2.6 gather_fusion
  89.7 63.6 %all_to_all.15 = bf16[64,8,512]{2,1,0:T(8,128)(2,1)S(1)} all-to-all(bf16[64,8,512]{2,1,0:T(8,128)(2,1)S(1)} %bitcast_select_fusion), channel_id=1, replica_groups=mesh['req'=64,'dec'=4] {'req'}, dimensions={0} | all-to-all | bytes 1048576 | tf_op jit(solution)/shard_map/all_to_all | solution.py:105
  154.2 2.5 broadcast_in_dim.55
  156.7 4.4 %all-to-all-start.1 = ((bf16[4,512,512]{1,2,0:T(8,128)(2,1)}), bf16[4,512,512]{1,2,0:T(8,128)(2,1)}, u32[]{:S(2)}, u32[]{:S(2)}) async-start(bf16[4,512,512]{1,2,0:T(8,128)(2,1)} %broadcast_in_dim.55), calls=%async_computation.1 | async-start | bytes 4194304 | tf_op jit(solution)/shard_map/all_to_all | solution.py:109
  164.2 2.3 reshape.145
  166.5 39.5 %all-to-all-done.1 = bf16[4,512,512]{1,2,0:T(8,128)(2,1)} async-done(((bf16[4,512,512]{1,2,0:T(8,128)(2,1)}), bf16[4,512,512]{1,2,0:T(8,128)(2,1)}, u32[]{:S(2)}, u32[]{:S(2)}) %all-to-all-start.1) | async-done | bytes 2097184 | tf_op jit(solution)/shard_map/all_to_all | solution.py:109
  206.0 2.9 copy.44
  208.9 10.8 %all-to-all-start.2 = ((bf16[4,2,64,2,512]{4,1,3,2,0:T(2,128)(2,1)}), bf16[4,2,64,2,512]{4,1,3,2,0:T(2,128)(2,1)}, u32[]{:S(2)}, u32[]{:S(2)}) async-start(bf16[4,2,64,2,512]{4,1,3,2,0:T(2,128)(2,1)} %copy.44), calls=%async_computation.2 | async-start | bytes 2097152 | tf_op jit(solution)/shard_map/all_to_all | solution.py:112
  219.8 2.1 fusion.1
  221.9 7.0 %fusion.8 = f32[512,1024]{1,0:T(8,128)} fusion(bf16[1024,6272]{1,0:T(8,128)(2,1)} %all-gather.2.cloned.1.call-done, bf16[512,2048]{0,1:T(8,128)(2,1)} %bitcast.8, f32[2048]{0:T(1024)S(1)} %copy-done.6, f32[512]{0:T(512)S(1)} %add_rsqrt_fusion), kind=kOutput, calls=%fused_computation.11 | convolution fusion | flops 2151677952 | bytes 8398848 | tf_op jit(solution)/shard_map/dot_general | solution.py:122
  228.9 4.7 %fusion.32 = f32[512,1024]{1,0:T(8,128)} fusion(bf16[2048,128]{1,0:T(8,128)(2,1)S(1)} %copy-done.4, bf16[1024,6272]{1,0:T(8,128)(2,1)} %all-gather.2.cloned.1.call-done, bf16[512,2048]{0,1:T(8,128)(2,1)} %bitcast.8, f32[2048]{0:T(1024)S(1)} %copy-done.6, f32[512]{0:T(512)S(1)} %add_rsqrt_fusion), kind=kOutput, calls=%fused_computation.36 | convolution fusion | flops 406913024 | bytes 4990976 | tf_op jit(solution)/shard_map/dot_general | solution.py:124
  233.6 12.0 %fusion.11 = bf16[512,2048]{1,0:T(8,128)(2,1)} fusion(bf16[1024,6272]{1,0:T(8,128)(2,1)} %all-gather.2.cloned.1.call-done, f32[512,1024]{1,0:T(8,128)} %fusion.8, f32[512,1024]{1,0:T(8,128)} %fusion.32, bf16[512,2048]{0,1:T(8,128)(2,1)} %bitcast.8, f32[2048]{0:T(1024)S(1)} %copy-done.6, f32[512]{0:T(512)S(1)} %add_rsqrt_fusion), kind=kOutput, calls=%fused_computation.18 | convolution fusion | flops 4305977344 | bytes 16787456 | tf_op jit(solution)/shard_map/dot_general | solution.py:129
  245.6 2.5 constant_dynamic-slice_fusion.2
  251.7 3.0 copy.45
  254.7 2.6 reshape.146
  257.3 3.9 %collective-permute-done.3 = bf16[512,512]{1,0:T(8,128)(2,1)} collective-permute-done((bf16[512,512]{1,0:T(8,128)(2,1)}, bf16[512,512]{1,0:T(8,128)(2,1)}, u32[]{:S(2)}, u32[]{:S(2)}) %collective-permute-start.3) | collective-permute-done | bytes 524320 | tf_op jit(solution)/shard_map/ppermute | solution.py:41
  261.2 32.7 %collective-permute-done.4 = bf16[512,512]{1,0:T(8,128)(2,1)} collective-permute-done((bf16[512,512]{1,0:T(8,128)(2,1)}, bf16[512,512]{1,0:T(8,128)(2,1)}, u32[]{:S(2)}, u32[]{:S(2)}) %collective-permute-start.4) | collective-permute-done | bytes 524320 | tf_op jit(solution)/shard_map/ppermute | solution.py:41
  293.8 3.0 collective-permute-done.5
  296.9 2.6 add_convert_fusion
  (49 shorter events, 25.0 us)
Async XLA Ops:
  7.2 9.2 %copy-start = (bf16[512,2048]{1,0:T(8,128)(2,1)S(1)}, bf16[512,2048]{1,0:T(8,128)(2,1)}, u32[]{:S(2)}) copy-start(bf16[512,2048]{1,0:T(8,128)(2,1)} %param.19) | copy-start | bytes 6291460
  7.2 5.6 %copy-start.3 = (bf16[512,512]{1,0:T(8,128)(2,1)S(1)}, bf16[512,512]{1,0:T(8,128)(2,1)}, u32[]{:S(2)}) copy-start(bf16[512,512]{1,0:T(8,128)(2,1)} %param.14) | copy-start | bytes 1572868
  7.2 5.6 %copy-start.1 = (bf16[512,512]{1,0:T(8,128)(2,1)S(1)}, bf16[512,512]{1,0:T(8,128)(2,1)}, u32[]{:S(2)}) copy-start(bf16[512,512]{1,0:T(8,128)(2,1)} %param.15) | copy-start | bytes 1572868
  7.2 214.7 %all-gather.2.cloned.1.call-start = ((), (), s32[]{:S(2)}) async-start(), calls=%async_computation.3 | async-start | bytes 13045760 | tf_op jit(solution)/shard_map/all_gather | solution.py:70
  13.5 2.4 copy-start.5
  17.7 1.3 copy-start.2
  19.0 6.1 %copy-start.7 = (s32[1,512]{1,0:T(1,128)S(1)}, s32[1,512]{1,0:T(1,128)}, u32[]{:S(2)}) copy-start(s32[1,512]{1,0:T(1,128)} %param.26) | copy-start | bytes 6148
  20.1 15.7 %collective-permute-start = (bf16[512,512]{1,0:T(8,128)(2,1)}, bf16[512,512]{1,0:T(8,128)(2,1)}, u32[]{:S(2)}, u32[]{:S(2)}) collective-permute-start(bf16[512,512]{1,0:T(8,128)(2,1)} %get-tuple-element.9), channel_id=1, source_target_pairs={{0,1},{1,2},{2,3},{3,0},{4,5},{5,6},{6,7},{7,4},{8,9},{9,10},{10,1... | collective-permute-start | bytes 1572872 | tf_op jit(solution)/shard_map/ppermute | solution.py:41
  21.8 54.1 %collective-permute-start.1 = (bf16[512,512]{1,0:T(8,128)(2,1)}, bf16[512,512]{1,0:T(8,128)(2,1)}, u32[]{:S(2)}, u32[]{:S(2)}) collective-permute-start(bf16[512,512]{1,0:T(8,128)(2,1)} %get-tuple-element.11), channel_id=1, source_target_pairs={{0,2},{1,3},{2,0},{3,1},{4,6},{5,7},{6,4},{7,5},{8,10},{9,11},{10,... | collective-permute-start | bytes 1572872 | tf_op jit(solution)/shard_map/ppermute | solution.py:41
  23.1 60.7 %collective-permute-start.2 = (bf16[512,512]{1,0:T(8,128)(2,1)S(1)}, bf16[512,512]{1,0:T(8,128)(2,1)}, u32[]{:S(2)}, u32[]{:S(2)}) collective-permute-start(bf16[512,512]{1,0:T(8,128)(2,1)S(1)} %get-tuple-element.10), channel_id=1, source_target_pairs={{0,3},{1,0},{2,1},{3,2},{4,7},{5,4},{6,5},{7,6},{8,11},{9,8},{10,9... | collective-permute-start | bytes 1572872 | tf_op jit(solution)/shard_map/ppermute | solution.py:41
  156.7 49.3 %all-to-all-start.1 = ((bf16[4,512,512]{1,2,0:T(8,128)(2,1)}), bf16[4,512,512]{1,2,0:T(8,128)(2,1)}, u32[]{:S(2)}, u32[]{:S(2)}) async-start(bf16[4,512,512]{1,2,0:T(8,128)(2,1)} %broadcast_in_dim.55), calls=%async_computation.1 | async-start | bytes 4194304 | tf_op jit(solution)/shard_map/all_to_all | solution.py:109
  161.2 1.7 copy-start.8
  208.9 13.0 %copy-start.6 = (f32[2048]{0:T(1024)S(1)}, f32[2048]{0:T(1024)}, u32[]{:S(2)}) copy-start(f32[2048]{0:T(1024)} %param.20) | copy-start | bytes 24580
  208.9 42.7 %all-to-all-start.2 = ((bf16[4,2,64,2,512]{4,1,3,2,0:T(2,128)(2,1)}), bf16[4,2,64,2,512]{4,1,3,2,0:T(2,128)(2,1)}, u32[]{:S(2)}, u32[]{:S(2)}) async-start(bf16[4,2,64,2,512]{4,1,3,2,0:T(2,128)(2,1)} %copy.44), calls=%async_computation.2 | async-start | bytes 2097152 | tf_op jit(solution)/shard_map/all_to_all | solution.py:112
  221.9 7.0 %copy-start.4 = (bf16[2048,128]{1,0:T(8,128)(2,1)S(1)}, bf16[2048,128]{1,0:T(8,128)(2,1)}, u32[]{:S(2)}) copy-start(bf16[2048,128]{1,0:T(8,128)(2,1)} %param.21) | copy-start | bytes 1572868
  248.1 13.0 %collective-permute-start.3 = (bf16[512,512]{1,0:T(8,128)(2,1)}, bf16[512,512]{1,0:T(8,128)(2,1)}, u32[]{:S(2)}, u32[]{:S(2)}) collective-permute-start(bf16[512,512]{1,0:T(8,128)(2,1)} %get-tuple-element.6), channel_id=1, source_target_pairs={{0,1},{1,2},{2,3},{3,0},{4,5},{5,6},{6,7},{7,4},{8,9},{9,10},{10,1... | collective-permute-start | bytes 1572872 | tf_op jit(solution)/shard_map/ppermute | solution.py:41
  249.3 44.5 %collective-permute-start.4 = (bf16[512,512]{1,0:T(8,128)(2,1)}, bf16[512,512]{1,0:T(8,128)(2,1)}, u32[]{:S(2)}, u32[]{:S(2)}) collective-permute-start(bf16[512,512]{1,0:T(8,128)(2,1)} %get-tuple-element.8), channel_id=1, source_target_pairs={{0,2},{1,3},{2,0},{3,1},{4,6},{5,7},{6,4},{7,5},{8,10},{9,11},{10,... | collective-permute-start | bytes 1572872 | tf_op jit(solution)/shard_map/ppermute | solution.py:41
  250.4 46.4 %collective-permute-start.5 = (bf16[512,512]{1,0:T(8,128)(2,1)S(1)}, bf16[512,512]{1,0:T(8,128)(2,1)}, u32[]{:S(2)}, u32[]{:S(2)}) collective-permute-start(bf16[512,512]{1,0:T(8,128)(2,1)S(1)} %get-tuple-element.7), channel_id=1, source_target_pairs={{0,3},{1,0},{2,1},{3,2},{4,7},{5,4},{6,5},{7,6},{8,11},{9,8},{10,9... | collective-permute-start | bytes 1572872 | tf_op jit(solution)/shard_map/ppermute | solution.py:41
Sparse Core Ops, SparseCore 0:
  11.7 185.1 all-gather.1

commit v7 on v5

--- a/solution.py
+++ b/solution.py
@@ -102,8 +102,6 @@
     ).astype(jnp.bfloat16)
     per_dev = block_count // dec_count
     ordered = ordered.reshape(dec_count, per_dev, block_slots, 2, features)
-    moved = lax.all_to_all(ordered, "dec", split_axis=0, concat_axis=0, tiled=True)
-    kv_cache = moved.transpose(1, 2, 3, 0, 4).reshape(per_dev, block_slots, 2 * dec_count * features)
 
     attn = attend(queries, keys, values, seg_ids)
     partial_value = jnp.dot(attn, out_weight, preferred_element_type=jnp.float32).astype(
@@ -120,6 +118,9 @@
         permuted.reshape(req_n, per_group, quarter), "req", split_axis=0, concat_axis=0, tiled=True
     ).reshape(cap, quarter)
     mixed_rows = gather_over_dec(column, dec_count)
+    mixed_rows, ordered = lax.optimization_barrier((mixed_rows, ordered))
+    moved = lax.all_to_all(ordered, "dec", split_axis=0, concat_axis=0, tiled=True)
+    kv_cache = moved.transpose(1, 2, 3, 0, 4).reshape(per_dev, block_slots, 2 * dec_count * features)
 
     values_f = mixed_rows.astype(jnp.float32)
     scale = lax.rsqrt(jnp.mean(values_f * values_f, axis=-1, keepdims=True) + 1e-05)

time: 317 us -> 321 us (1.013)
  waiting for transfers between devices: 196 us -> 185 us
  local copies, waits for them, and re-layouts: 24.6 us -> 31.3 us
  matrix products: 23.5 us -> 28.7 us
  starting transfers between devices: 34.7 us -> 39.1 us
    ppermute x3, waiting for transfers between devices: 59.7 us -> 41.7 us  [gather_over_dec(): arrived.append(lax.ppermute(column, 'dec', pairs))]
    all_to_all x1, starting transfers between devices: 5.39 us -> 16.2 us  [body(): lax.all_to_all(ordered, 'dec', split_axis=0, concat_axis=0, tiled=True)]
    all_to_all x1, waiting for transfers between devices: 39.8 us -> 46.2 us  [body(): lax.all_to_all(permuted.reshape(req_n, per_group, quarter), 'req', split_...]
    ppermute x6, starting transfers between devices: 14.4 us -> 8 us  [reduce_over_dec(): total = total + lax.ppermute(piece, 'dec', pairs).astype(jnp.float32)]
    convert_element_type x1 -> x0, local copies, waits for them, and re-layouts: 5.23 us -> none  [body(): values_f = mixed_rows.astype(jnp.float32)]
    convert_element_type x2 -> x0, other arithmetic: 4.89 us -> none  [the longest x1 2.62 us: body(): normed = (values_f * scale * norm_gain).astype(jnp.bfloat16)]
    select_n x0 -> x1, local copies, waits for them, and re-layouts: none -> 4.16 us  [gather_over_dec(): jnp.take(stacked, (here - jnp.arange(dec_count)) % dec_count, axis=0)]
  transfers between devices with their start and end apart: 12 -> 12, of which waited for: 9 -> 9; matrix products, arithmetic and copies ran while one was open for 20% -> 24% of each run, Pallas kernels for 0% -> 0%
where the time goes in v7:
time: 321 us; the launch traced here: 320 us
  waiting for transfers between devices  185 us (58%)
  starting transfers between devices  39.1 us (12%)
  local copies, waits for them, and re-layouts  31.3 us (10%)
  matrix products  28.7 us (9%)
  other arithmetic  21.4 us (7%)
  between operations  14.3 us (4%)
    ppermute x6, waiting for transfers between devices, reduce_over_dec(): total = total + lax.ppermute(piece, 'dec', pairs).astype(jnp.float32)  97.2 us
    all_to_all x1, waiting for transfers between devices, body(): lax.all_to_all(permuted.reshape(req_n, per_group, quarter), 'req', split_...  46.2 us
    ppermute x3, waiting for transfers between devices, gather_over_dec(): arrived.append(lax.ppermute(column, 'dec', pairs))  41.7 us
    all_to_all x1, starting transfers between devices, body(): lax.all_to_all(ordered, 'dec', split_axis=0, concat_axis=0, tiled=True)  16.2 us
    all_to_all x1, starting transfers between devices, body(): lax.all_to_all(permuted.reshape(req_n, per_group, quarter), 'req', split_...  13.4 us
    dot_general x1, matrix products, body(): jnp.dot(hidden_units, down_rows, preferred_element_type=jnp.float32)  12 us
    ppermute x6, starting transfers between devices, reduce_over_dec(): total = total + lax.ppermute(piece, 'dec', pairs).astype(jnp.float32)  8 us
    dot_general x1, matrix products, body(): lax.dot_general(normed, gate_rows, contract, preferred_element_type=jnp.f...  7.01 us
  transfers between devices with their start and end apart: 12, of which 9 were waited for; matrix products, arithmetic and copies ran while one was open for 24% of the time, Pallas kernels for 0%

profile of v7, /device:TPU:33, one launch (start us, length us, event | category | flops | bytes accessed | tf_op | source)
XLA Modules:
  0.0 319.9 jit_solution(5999234193388383677)
XLA Ops:
  26.0 9.8 %collective-permute-done = bf16[512,512]{1,0:T(8,128)(2,1)} collective-permute-done((bf16[512,512]{1,0:T(8,128)(2,1)}, bf16[512,512]{1,0:T(8,128)(2,1)}, u32[]{:S(2)}, u32[]{:S(2)}) %collective-permute-start) | collective-permute-done | bytes 524320 | tf_op jit(solution)/shard_map/ppermute | solution.py:41
  35.8 40.0 %collective-permute-done.1 = bf16[512,512]{1,0:T(8,128)(2,1)} collective-permute-done((bf16[512,512]{1,0:T(8,128)(2,1)}, bf16[512,512]{1,0:T(8,128)(2,1)}, u32[]{:S(2)}, u32[]{:S(2)}) %collective-permute-start.1) | collective-permute-done | bytes 524320 | tf_op jit(solution)/shard_map/ppermute | solution.py:41
  75.9 8.0 %collective-permute-done.2 = bf16[512,512]{1,0:T(8,128)(2,1)} collective-permute-done((bf16[512,512]{1,0:T(8,128)(2,1)S(1)}, bf16[512,512]{1,0:T(8,128)(2,1)}, u32[]{:S(2)}, u32[]{:S(2)}) %collective-permute-start.2) | collective-permute-done | bytes 524320 | tf_op jit(solution)/shard_map/ppermute | solution.py:41
  85.9 2.6 gather_fusion
  90.5 13.4 %all-to-all-start = ((bf16[64,8,512]{2,1,0:T(8,128)(2,1)}), bf16[64,8,512]{2,1,0:T(8,128)(2,1)S(1)}, u32[]{:S(2)}, u32[]{:S(2)}) async-start(bf16[64,8,512]{2,1,0:T(8,128)(2,1)} %bitcast_select_fusion), calls=%async_computation | async-start | bytes 1048576 | tf_op jit(solution)/shard_map/all_to_all | solution.py:117
  106.3 46.2 %all-to-all-done = bf16[64,8,512]{2,1,0:T(8,128)(2,1)S(1)} async-done(((bf16[64,8,512]{2,1,0:T(8,128)(2,1)}), bf16[64,8,512]{2,1,0:T(8,128)(2,1)S(1)}, u32[]{:S(2)}, u32[]{:S(2)}) %all-to-all-start) | async-done | bytes 524320 | tf_op jit(solution)/shard_map/all_to_all | solution.py:117
  154.0 2.4 convolution_convert_fusion.1
  158.7 41.1 %collective-permute-done.5 = bf16[512,512]{1,0:T(8,128)(2,1)} collective-permute-done((bf16[512,512]{1,0:T(8,128)(2,1)S(1)}, bf16[512,512]{1,0:T(8,128)(2,1)}, u32[]{:S(2)}, u32[]{:S(2)}) %collective-permute-start.5) | collective-permute-done | bytes 524320 | tf_op jit(solution)/shard_map/ppermute | solution.py:50
  200.4 2.9 pad_maximum_fusion
  203.4 3.6 %gather_fusion.1 = bf16[4,512,512]{2,1,0:T(8,128)(2,1)} fusion(bf16[4,512,512]{2,1,0:T(8,128)(2,1)} %pad_maximum_fusion, s32[1024]{0:T(1024)S(1)} %pad_clamp_fusion), kind=kCustom, calls=%fused_computation.1 | custom fusion | bytes 4194320 | tf_op jit(solution)/shard_map/jit(_take)/gather | solution.py:52
  207.0 3.2 %select_bitcast_fusion = bf16[512,4,512]{2,0,1:T(8,128)(2,1)} fusion(bf16[4,512,512]{2,1,0:T(8,128)(2,1)} %gather_fusion.1, pred[4]{0:T(512)(128)(4,1)S(1)} %compare_and_fusion.1), kind=kLoop, calls=%fused_computation.31 | loop fusion | flops 1048576 | bytes 4194308 | tf_op jit(solution)/shard_map/jit(_take)/select_n | solution.py:52
  210.2 4.2 %copy.41 = bf16[512,4,512]{0,2,1:T(8,128)(2,1)} copy(bf16[512,4,512]{2,0,1:T(8,128)(2,1)} %select_bitcast_fusion) | data formatting | bytes 4194304 | tf_op jit(solution)/shard_map/jit(_take)/select_n | solution.py:52
  214.4 2.9 copy.44
  217.3 16.2 %all-to-all-start.1 = ((bf16[4,2,64,2,512]{4,1,3,2,0:T(2,128)(2,1)}), bf16[4,2,64,2,512]{4,1,3,2,0:T(2,128)(2,1)}, u32[]{:S(2)}, u32[]{:S(2)}) async-start(bf16[4,2,64,2,512]{4,1,3,2,0:T(2,128)(2,1)} %copy.44), calls=%async_computation.1 | async-start | bytes 2097152 | tf_op jit(solution)/shard_map/all_to_all | solution.py:122
  235.6 7.0 %fusion.8 = f32[512,1024]{1,0:T(8,128)} fusion(bf16[1024,6272]{1,0:T(8,128)(2,1)} %all-gather.2.cloned.1.call-done, bf16[512,2048]{0,1:T(8,128)(2,1)} %bitcast.55, f32[2048]{0:T(1024)S(1)} %copy-done.6, f32[512]{0:T(512)S(1)} %add_rsqrt_fusion), kind=kOutput, calls=%fused_computation.12 | convolution fusion | flops 2151677952 | bytes 8398848 | tf_op jit(solution)/shard_map/dot_general | solution.py:132
  242.6 4.7 %fusion.32 = f32[512,1024]{1,0:T(8,128)} fusion(bf16[2048,128]{1,0:T(8,128)(2,1)S(1)} %copy-done.4, bf16[1024,6272]{1,0:T(8,128)(2,1)} %all-gather.2.cloned.1.call-done, bf16[512,2048]{0,1:T(8,128)(2,1)} %bitcast.56, f32[2048]{0:T(1024)S(1)} %copy-done.6, f32[512]{0:T(512)S(1)} %add_rsqrt_fusion), kind=kOutput, calls=%fused_computation.39 | convolution fusion | flops 406913024 | bytes 4990976 | tf_op jit(solution)/shard_map/dot_general | solution.py:134
  247.3 12.0 %fusion.11 = bf16[512,2048]{1,0:T(8,128)(2,1)} fusion(bf16[1024,6272]{1,0:T(8,128)(2,1)} %all-gather.2.cloned.1.call-done, f32[512,1024]{1,0:T(8,128)} %fusion.8, f32[512,1024]{1,0:T(8,128)} %fusion.32, bf16[512,2048]{0,1:T(8,128)(2,1)} %bitcast.57, f32[2048]{0:T(1024)S(1)} %copy-done.6, f32[512]{0:T(512)S(1)} %add_rsqrt_fusion), kind=kOutput, calls=%fused_computation.19 | convolution fusion | flops 4305977344 | bytes 16787456 | tf_op jit(solution)/shard_map/dot_general | solution.py:139
  259.4 2.5 constant_dynamic-slice_fusion.2
  265.4 3.0 copy.45
  268.5 2.6 reshape.199
  271.1 3.5 %collective-permute-done.6 = bf16[512,512]{1,0:T(8,128)(2,1)} collective-permute-done((bf16[512,512]{1,0:T(8,128)(2,1)}, bf16[512,512]{1,0:T(8,128)(2,1)}, u32[]{:S(2)}, u32[]{:S(2)}) %collective-permute-start.6) | collective-permute-done | bytes 524320 | tf_op jit(solution)/shard_map/ppermute | solution.py:41
  274.6 32.7 %collective-permute-done.7 = bf16[512,512]{1,0:T(8,128)(2,1)} collective-permute-done((bf16[512,512]{1,0:T(8,128)(2,1)}, bf16[512,512]{1,0:T(8,128)(2,1)}, u32[]{:S(2)}, u32[]{:S(2)}) %collective-permute-start.7) | collective-permute-done | bytes 524320 | tf_op jit(solution)/shard_map/ppermute | solution.py:41
  307.3 3.2 collective-permute-done.8
  310.5 2.6 add_convert_fusion
  (59 shorter events, 35.1 us)
Async XLA Ops:
  7.2 9.2 %copy-start = (bf16[512,2048]{1,0:T(8,128)(2,1)S(1)}, bf16[512,2048]{1,0:T(8,128)(2,1)}, u32[]{:S(2)}) copy-start(bf16[512,2048]{1,0:T(8,128)(2,1)} %param.19) | copy-start | bytes 6291460
  7.2 5.6 %copy-start.3 = (bf16[512,512]{1,0:T(8,128)(2,1)S(1)}, bf16[512,512]{1,0:T(8,128)(2,1)}, u32[]{:S(2)}) copy-start(bf16[512,512]{1,0:T(8,128)(2,1)} %param.14) | copy-start | bytes 1572868
  7.2 5.6 %copy-start.1 = (bf16[512,512]{1,0:T(8,128)(2,1)S(1)}, bf16[512,512]{1,0:T(8,128)(2,1)}, u32[]{:S(2)}) copy-start(bf16[512,512]{1,0:T(8,128)(2,1)} %param.15) | copy-start | bytes 1572868
  7.2 228.4 %all-gather.2.cloned.1.call-start = ((), (), s32[]{:S(2)}) async-start(), calls=%async_computation.2 | async-start | bytes 13045760 | tf_op jit(solution)/shard_map/all_gather | solution.py:82
  13.5 2.4 copy-start.5
  17.7 1.3 copy-start.2
  19.0 6.2 %copy-start.7 = (s32[1,512]{1,0:T(1,128)S(1)}, s32[1,512]{1,0:T(1,128)}, u32[]{:S(2)}) copy-start(s32[1,512]{1,0:T(1,128)} %param.26) | copy-start | bytes 6148
  20.1 15.7 %collective-permute-start = (bf16[512,512]{1,0:T(8,128)(2,1)}, bf16[512,512]{1,0:T(8,128)(2,1)}, u32[]{:S(2)}, u32[]{:S(2)}) collective-permute-start(bf16[512,512]{1,0:T(8,128)(2,1)} %get-tuple-element.9), channel_id=1, source_target_pairs={{0,1},{1,2},{2,3},{3,0},{4,5},{5,6},{6,7},{7,4},{8,9},{9,10},{10,1... | collective-permute-start | bytes 1572872 | tf_op jit(solution)/shard_map/ppermute | solution.py:41
  21.8 54.1 %collective-permute-start.1 = (bf16[512,512]{1,0:T(8,128)(2,1)}, bf16[512,512]{1,0:T(8,128)(2,1)}, u32[]{:S(2)}, u32[]{:S(2)}) collective-permute-start(bf16[512,512]{1,0:T(8,128)(2,1)} %get-tuple-element.11), channel_id=1, source_target_pairs={{0,2},{1,3},{2,0},{3,1},{4,6},{5,7},{6,4},{7,5},{8,10},{9,11},{10,... | collective-permute-start | bytes 1572872 | tf_op jit(solution)/shard_map/ppermute | solution.py:41
  23.1 60.7 %collective-permute-start.2 = (bf16[512,512]{1,0:T(8,128)(2,1)S(1)}, bf16[512,512]{1,0:T(8,128)(2,1)}, u32[]{:S(2)}, u32[]{:S(2)}) collective-permute-start(bf16[512,512]{1,0:T(8,128)(2,1)S(1)} %get-tuple-element.10), channel_id=1, source_target_pairs={{0,3},{1,0},{2,1},{3,2},{4,7},{5,4},{6,5},{7,6},{8,11},{9,8},{10,9... | collective-permute-start | bytes 1572872 | tf_op jit(solution)/shard_map/ppermute | solution.py:41
  88.5 65.5 %copy-start.8 = (s32[1,8]{1,0:T(1,128)S(1)}, s32[1,8]{1,0:T(1,128)}, u32[]{:S(2)}) copy-start(s32[1,8]{1,0:T(1,128)} %param.27) | copy-start | bytes 100
  90.5 62.1 %all-to-all-start = ((bf16[64,8,512]{2,1,0:T(8,128)(2,1)}), bf16[64,8,512]{2,1,0:T(8,128)(2,1)S(1)}, u32[]{:S(2)}, u32[]{:S(2)}) async-start(bf16[64,8,512]{2,1,0:T(8,128)(2,1)} %bitcast_select_fusion), calls=%async_computation | async-start | bytes 1048576 | tf_op jit(solution)/shard_map/all_to_all | solution.py:117
  152.5 47.3 %collective-permute-start.5 = (bf16[512,512]{1,0:T(8,128)(2,1)S(1)}, bf16[512,512]{1,0:T(8,128)(2,1)}, u32[]{:S(2)}, u32[]{:S(2)}) collective-permute-start(bf16[512,512]{1,0:T(8,128)(2,1)S(1)} %bitcast.58), channel_id=1, source_target_pairs={{0,3},{1,0},{2,1},{3,2},{4,7},{5,4},{6,5},{7,6},{8,11},{9,8},{10,9... | collective-permute-start | bytes 1572872 | tf_op jit(solution)/shard_map/ppermute | solution.py:50
  152.5 47.3 %collective-permute-start.3 = (bf16[512,512]{1,0:T(8,128)(2,1)S(1)}, bf16[512,512]{1,0:T(8,128)(2,1)}, u32[]{:S(2)}, u32[]{:S(2)}) collective-permute-start(bf16[512,512]{1,0:T(8,128)(2,1)S(1)} %bitcast.59), channel_id=1, source_target_pairs={{0,1},{1,2},{2,3},{3,0},{4,5},{5,6},{6,7},{7,4},{8,9},{9,10},{10,1... | collective-permute-start | bytes 1572872 | tf_op jit(solution)/shard_map/ppermute | solution.py:50
  154.0 46.4 %collective-permute-start.4 = (bf16[512,512]{1,0:T(8,128)(2,1)S(1)}, bf16[512,512]{1,0:T(8,128)(2,1)}, u32[]{:S(2)}, u32[]{:S(2)}) collective-permute-start(bf16[512,512]{1,0:T(8,128)(2,1)S(1)} %bitcast.60), channel_id=1, source_target_pairs={{0,2},{1,3},{2,0},{3,1},{4,6},{5,7},{6,4},{7,5},{8,10},{9,11},{10,... | collective-permute-start | bytes 1572872 | tf_op jit(solution)/shard_map/ppermute | solution.py:50
  217.3 18.3 %copy-start.6 = (f32[2048]{0:T(1024)S(1)}, f32[2048]{0:T(1024)}, u32[]{:S(2)}) copy-start(f32[2048]{0:T(1024)} %param.20) | copy-start | bytes 24580
  217.3 48.1 %all-to-all-start.1 = ((bf16[4,2,64,2,512]{4,1,3,2,0:T(2,128)(2,1)}), bf16[4,2,64,2,512]{4,1,3,2,0:T(2,128)(2,1)}, u32[]{:S(2)}, u32[]{:S(2)}) async-start(bf16[4,2,64,2,512]{4,1,3,2,0:T(2,128)(2,1)} %copy.44), calls=%async_computation.1 | async-start | bytes 2097152 | tf_op jit(solution)/shard_map/all_to_all | solution.py:122
  235.6 7.1 %copy-start.4 = (bf16[2048,128]{1,0:T(8,128)(2,1)S(1)}, bf16[2048,128]{1,0:T(8,128)(2,1)}, u32[]{:S(2)}) copy-start(bf16[2048,128]{1,0:T(8,128)(2,1)} %param.21) | copy-start | bytes 1572868
  261.9 12.7 %collective-permute-start.6 = (bf16[512,512]{1,0:T(8,128)(2,1)}, bf16[512,512]{1,0:T(8,128)(2,1)}, u32[]{:S(2)}, u32[]{:S(2)}) collective-permute-start(bf16[512,512]{1,0:T(8,128)(2,1)} %get-tuple-element.6), channel_id=1, source_target_pairs={{0,1},{1,2},{2,3},{3,0},{4,5},{5,6},{6,7},{7,4},{8,9},{9,10},{10,1... | collective-permute-start | bytes 1572872 | tf_op jit(solution)/shard_map/ppermute | solution.py:41
  263.1 44.2 %collective-permute-start.7 = (bf16[512,512]{1,0:T(8,128)(2,1)}, bf16[512,512]{1,0:T(8,128)(2,1)}, u32[]{:S(2)}, u32[]{:S(2)}) collective-permute-start(bf16[512,512]{1,0:T(8,128)(2,1)} %get-tuple-element.8), channel_id=1, source_target_pairs={{0,2},{1,3},{2,0},{3,1},{4,6},{5,7},{6,4},{7,5},{8,10},{9,11},{10,... | collective-permute-start | bytes 1572872 | tf_op jit(solution)/shard_map/ppermute | solution.py:41
  264.0 46.4 %collective-permute-start.8 = (bf16[512,512]{1,0:T(8,128)(2,1)S(1)}, bf16[512,512]{1,0:T(8,128)(2,1)}, u32[]{:S(2)}, u32[]{:S(2)}) collective-permute-start(bf16[512,512]{1,0:T(8,128)(2,1)S(1)} %get-tuple-element.7), channel_id=1, source_target_pairs={{0,3},{1,0},{2,1},{3,2},{4,7},{5,4},{6,5},{7,6},{8,11},{9,8},{10,9... | collective-permute-start | bytes 1572872 | tf_op jit(solution)/shard_map/ppermute | solution.py:41
Sparse Core Ops, SparseCore 0:
  11.7 178.4 all-gather.1

commit v8 on v6

--- a/solution.py
+++ b/solution.py
@@ -31,14 +31,22 @@
     return result.astype(jnp.bfloat16).reshape(row_count, head_count * HD)
 
 
-def reduce_over_dec(part, dec_count):
-    quarter = part.shape[1] // dec_count
+def project_reduce_over_dec(lhs, rhs, dec_count):
+    quarter = rhs.shape[1] // dec_count
     here = lax.axis_index("dec")
-    total = lax.dynamic_slice_in_dim(part, here * quarter, quarter, 1).astype(jnp.float32)
+
+    def quarter_of(index):
+        block = lax.dynamic_slice_in_dim(rhs, index * quarter, quarter, 1)
+        return jnp.dot(lhs, block, preferred_element_type=jnp.float32).astype(jnp.bfloat16)
+
+    arrived = []
     for shift in range(1, dec_count):
-        piece = lax.dynamic_slice_in_dim(part, ((here + shift) % dec_count) * quarter, quarter, 1)
+        piece = quarter_of((here + shift) % dec_count)
         pairs = [(i, (i + shift) % dec_count) for i in range(dec_count)]
-        total = total + lax.ppermute(piece, "dec", pairs).astype(jnp.float32)
+        arrived.append(lax.ppermute(piece, "dec", pairs))
+    total = quarter_of(here).astype(jnp.float32)
+    for piece in arrived:
+        total = total + piece.astype(jnp.float32)
     return total
 
 
@@ -92,10 +100,7 @@
     ordered = ordered.reshape(dec_count, per_dev, block_slots, 2, features)
 
     attn = attend(queries, keys, values, seg_ids)
-    partial_value = jnp.dot(attn, out_weight, preferred_element_type=jnp.float32).astype(
-        jnp.bfloat16
-    )
-    head_total = reduce_over_dec(partial_value, dec_count)
+    head_total = project_reduce_over_dec(attn, out_weight, dec_count)
     hidden = (resid.astype(jnp.float32) + head_total).astype(jnp.bfloat16)
 
     permuted = jnp.take(hidden, row_order[0], axis=0)
@@ -126,10 +131,7 @@
     )
     up = lax.dot_general(normed, up_rows, contract, preferred_element_type=jnp.float32)
     hidden_units = (jax.nn.gelu(gate) * up).astype(jnp.bfloat16)
-    down_part = jnp.dot(
-        hidden_units, down_rows, preferred_element_type=jnp.float32
-    ).astype(jnp.bfloat16)
-    mlp_total = reduce_over_dec(down_part, dec_count)
+    mlp_total = project_reduce_over_dec(hidden_units, down_rows, dec_count)
     block_out = (column.astype(jnp.float32) + mlp_total).astype(jnp.bfloat16)
     return (block_out, kv_cache)
 

time: 307 us -> 306 us (level)
  matrix products: 27.6 us -> 38.8 us
  local copies, waits for them, and re-layouts: 26.2 us -> 19.5 us
  other arithmetic: 14.4 us -> 8.71 us
    dot_general x2 -> x9, matrix products: 13.3 us -> 24.2 us  [the longest x8 16.9 us: quarter_of(): jnp.dot(lhs, block, preferred_element_type=jnp.float32).astype(jnp.bfloat16)]
    convert_element_type x2 -> x0, other arithmetic: 4.66 us -> none  [the longest x1 2.65 us: body(): block_out = (column.astype(jnp.float32) + mlp_total).astype(jnp.bfloat16)]
    dynamic_slice x2 -> x0, local copies, waits for them, and re-layouts: 3.62 us -> none  [reduce_over_dec(): lax.dynamic_slice_in_dim(part, (here + shift) % dec_count * quarter, quar...]
    ppermute x6, waiting for transfers between devices: 97.5 us -> 94.1 us  [project_reduce_over_dec(): arrived.append(lax.ppermute(piece, 'dec', pairs))]
    all_to_all x1, waiting for transfers between devices: 39.5 us -> 42.9 us  [body(): lax.all_to_all(spread, 'dec', split_axis=0, concat_axis=0, tiled=True)]
where the time goes in v8:
time: 306 us; the launch traced here: 305 us
  waiting for transfers between devices  137 us (45%)
  blocking collectives  64.1 us (21%)
  matrix products  38.8 us (13%)
  starting transfers between devices  22.8 us (7%)
  local copies, waits for them, and re-layouts  19.5 us (6%)
  between operations  14.3 us (5%)
  other arithmetic  8.71 us (3%)
    ppermute x6, waiting for transfers between devices, project_reduce_over_dec(): arrived.append(lax.ppermute(piece, 'dec', pairs))  94.1 us
    all_to_all x1, blocking collectives, body(): lax.all_to_all(permuted.reshape(req_n, per_group, quarter), 'req', split_...  64.1 us
    all_to_all x1, waiting for transfers between devices, body(): lax.all_to_all(spread, 'dec', split_axis=0, concat_axis=0, tiled=True)  42.9 us
    dot_general x8, matrix products, quarter_of(): jnp.dot(lhs, block, preferred_element_type=jnp.float32).astype(jnp.bfloat16)  16.9 us
    all_to_all x1, starting transfers between devices, body(): lax.all_to_all(ordered, 'dec', split_axis=0, concat_axis=0, tiled=True)  10.1 us
    ppermute x6, starting transfers between devices, project_reduce_over_dec(): arrived.append(lax.ppermute(piece, 'dec', pairs))  8.02 us
    dot_general x1, matrix products, body(): lax.dot_general(normed, up_rows, contract, preferred_element_type=jnp.flo...  7.31 us
    dot_general x1, matrix products, body(): lax.dot_general(normed, gate_rows, contract, preferred_element_type=jnp.f...  6.92 us
  transfers between devices with their start and end apart: 9, of which 7 were waited for; matrix products, arithmetic and copies ran while one was open for 20% of the time, Pallas kernels for 0%

profile of v8, /device:TPU:33, one launch (start us, length us, event | category | flops | bytes accessed | tf_op | source)
XLA Modules:
  0.0 305.2 jit_solution(5717509675800707133)
XLA Ops:
  13.9 2.4 fusion.69
  20.5 2.3 convolution_convert_fusion.2
  24.2 2.3 convolution_convert_fusion.1
  29.3 4.3 %collective-permute-done = bf16[512,512]{1,0:T(8,128)(2,1)} collective-permute-done((bf16[512,512]{1,0:T(8,128)(2,1)}, bf16[512,512]{1,0:T(8,128)(2,1)}, u32[]{:S(2)}, u32[]{:S(2)}) %collective-permute-start) | collective-permute-done | bytes 524320 | tf_op jit(solution)/shard_map/ppermute | solution.py:46
  33.5 41.2 %collective-permute-done.1 = bf16[512,512]{1,0:T(8,128)(2,1)} collective-permute-done((bf16[512,512]{1,0:T(8,128)(2,1)}, bf16[512,512]{1,0:T(8,128)(2,1)}, u32[]{:S(2)}, u32[]{:S(2)}) %collective-permute-start.1) | collective-permute-done | bytes 524320 | tf_op jit(solution)/shard_map/ppermute | solution.py:46
  74.8 7.8 %collective-permute-done.2 = bf16[512,512]{1,0:T(8,128)(2,1)} collective-permute-done((bf16[512,512]{1,0:T(8,128)(2,1)}, bf16[512,512]{1,0:T(8,128)(2,1)}, u32[]{:S(2)}, u32[]{:S(2)}) %collective-permute-start.2) | collective-permute-done | bytes 524320 | tf_op jit(solution)/shard_map/ppermute | solution.py:46
  82.6 2.1 add_convert_fusion.1
  84.7 2.0 gather_fusion
  86.8 64.1 %all_to_all.15 = bf16[64,8,512]{2,1,0:T(8,128)(2,1)} all-to-all(bf16[64,8,512]{2,1,0:T(8,128)(2,1)S(1)} %bitcast_select_fusion), channel_id=1, replica_groups=mesh['req'=64,'dec'=4] {'req'}, dimensions={0} | all-to-all | bytes 1048576 | tf_op jit(solution)/shard_map/all_to_all | solution.py:110
  153.8 4.6 %all-to-all-start.1 = ((bf16[4,512,512]{1,2,0:T(8,128)(2,1)}), bf16[4,512,512]{1,2,0:T(8,128)(2,1)}, u32[]{:S(2)}, u32[]{:S(2)}) async-start(bf16[4,512,512]{1,2,0:T(8,128)(2,1)} %broadcast_in_dim.55), calls=%async_computation.1 | async-start | bytes 4194304 | tf_op jit(solution)/shard_map/all_to_all | solution.py:114
  160.6 42.9 %all-to-all-done.1 = bf16[4,512,512]{1,2,0:T(8,128)(2,1)} async-done(((bf16[4,512,512]{1,2,0:T(8,128)(2,1)}), bf16[4,512,512]{1,2,0:T(8,128)(2,1)}, u32[]{:S(2)}, u32[]{:S(2)}) %all-to-all-start.1) | async-done | bytes 2097184 | tf_op jit(solution)/shard_map/all_to_all | solution.py:114
  203.5 2.9 copy.44
  206.4 10.1 %all-to-all-start.2 = ((bf16[4,2,64,2,512]{4,1,3,2,0:T(2,128)(2,1)}), bf16[4,2,64,2,512]{4,1,3,2,0:T(2,128)(2,1)S(1)}, u32[]{:S(2)}, u32[]{:S(2)}) async-start(bf16[4,2,64,2,512]{4,1,3,2,0:T(2,128)(2,1)} %copy.44), calls=%async_computation.2 | async-start | bytes 2097152 | tf_op jit(solution)/shard_map/all_to_all | solution.py:117
  216.6 2.1 fusion.1
  218.7 6.9 %fusion.6 = f32[512,1024]{1,0:T(8,128)} fusion(bf16[1024,6272]{1,0:T(8,128)(2,1)} %all-gather.2.cloned.1.call-done, bf16[512,2048]{0,1:T(8,128)(2,1)} %bitcast.9, f32[2048]{0:T(1024)S(1)} %copy-done.4, f32[512]{0:T(512)S(1)} %add_rsqrt_fusion), kind=kOutput, calls=%fused_computation.9 | convolution fusion | flops 2151677952 | bytes 8398848 | tf_op jit(solution)/shard_map/dot_general | solution.py:127
  225.6 4.9 %fusion.27 = f32[512,1024]{1,0:T(8,128)} fusion(bf16[2048,128]{1,0:T(8,128)(2,1)} %param.21, bf16[1024,6272]{1,0:T(8,128)(2,1)} %all-gather.2.cloned.1.call-done, bf16[512,2048]{0,1:T(8,128)(2,1)} %bitcast.9, f32[2048]{0:T(1024)S(1)} %copy-done.4, f32[512]{0:T(512)S(1)} %add_rsqrt_fusion), kind=kOutput, calls=%fused_computation.42 | convolution fusion | flops 406913024 | bytes 4990976 | tf_op jit(solution)/shard_map/dot_general | solution.py:129
  230.5 7.3 %fusion.17 = bf16[512,1024]{1,0:T(8,128)(2,1)S(1)} fusion(f32[512,1024]{1,0:T(8,128)} %fusion.6, f32[512,1024]{1,0:T(8,128)} %fusion.27, bf16[1024,6272]{1,0:T(8,128)(2,1)} %all-gather.2.cloned.1.call-done, bf16[512,2048]{0,1:T(8,128)(2,1)} %bitcast.9, f32[2048]{0:T(1024)S(1)} %copy-done.4, f32[512]{0:T(512)S(1)} %add_rsqrt_fusion), kind=kOutput, calls=%fused_computation.24 | convolution fusion | flops 2157445120 | bytes 11544576 | tf_op jit(solution)/shard_map/dot_general | solution.py:132
  237.9 2.9 slice.21
  240.7 2.0 convolution_convert_fusion.7
  251.1 2.6 reshape.146
  253.7 5.1 %collective-permute-done.3 = bf16[512,512]{1,0:T(8,128)(2,1)} collective-permute-done((bf16[512,512]{1,0:T(8,128)(2,1)}, bf16[512,512]{1,0:T(8,128)(2,1)}, u32[]{:S(2)}, u32[]{:S(2)}) %collective-permute-start.3) | collective-permute-done | bytes 524320 | tf_op jit(solution)/shard_map/ppermute | solution.py:46
  258.8 32.7 %collective-permute-done.4 = bf16[512,512]{1,0:T(8,128)(2,1)} collective-permute-done((bf16[512,512]{1,0:T(8,128)(2,1)}, bf16[512,512]{1,0:T(8,128)(2,1)}, u32[]{:S(2)}, u32[]{:S(2)}) %collective-permute-start.4) | collective-permute-done | bytes 524320 | tf_op jit(solution)/shard_map/ppermute | solution.py:46
  291.5 3.0 collective-permute-done.5
  294.5 3.8 %add_convert_fusion = bf16[512,512]{1,0:T(8,128)(2,1)} fusion(bf16[512,512]{1,0:T(8,128)(2,1)} %collective-permute-done.5, bf16[512,512]{1,0:T(8,128)(2,1)} %collective-permute-done.4, bf16[512,512]{1,0:T(8,128)(2,1)} %collective-permute-done.3, bf16[512,1024]{1,0:T(8,128)(2,1)} %copy-done.9, bf16[1024,2048]{1,0:T(8,128)(2,1)} %copy-done.1, ...), kind=kOutput, calls=%fused_computation.46 | convolution fusion | flops 539754496 | bytes 4718596 | tf_op jit(solution)/shard_map/dot_general | solution.py:40
  (55 shorter events, 28.6 us)
Async XLA Ops:
  7.2 10.4 %copy-start = (bf16[512,2048]{1,0:T(8,128)(2,1)S(1)}, bf16[512,2048]{1,0:T(8,128)(2,1)}, u32[]{:S(2)}) copy-start(bf16[512,2048]{1,0:T(8,128)(2,1)} %param.19) | copy-start | bytes 6291460
  7.2 211.5 %all-gather.2.cloned.1.call-start = ((), (), s32[]{:S(2)}) async-start(), calls=%async_computation.3 | async-start | bytes 13045760 | tf_op jit(solution)/shard_map/all_gather | solution.py:78
  16.8 0.8 copy-start.8
  16.8 11.7 %copy-start.5 = (s32[1,512]{1,0:T(1,128)S(1)}, s32[1,512]{1,0:T(1,128)}, u32[]{:S(2)}) copy-start(s32[1,512]{1,0:T(1,128)} %param.26) | copy-start | bytes 6148
  16.8 65.8 %copy-start.7 = (bf16[512,512]{1,0:T(8,128)(2,1)S(1)}, bf16[512,512]{1,0:T(8,128)(2,1)}, u32[]{:S(2)}) copy-start(bf16[512,512]{1,0:T(8,128)(2,1)} %param.17) | copy-start | bytes 1572868
  18.9 14.7 %collective-permute-start = (bf16[512,512]{1,0:T(8,128)(2,1)}, bf16[512,512]{1,0:T(8,128)(2,1)}, u32[]{:S(2)}, u32[]{:S(2)}) collective-permute-start(bf16[512,512]{1,0:T(8,128)(2,1)} %convolution_convert_fusion.3), channel_id=1, source_target_pairs={{0,1},{1,2},{2,3},{3,0},{4,5},{5,6},{6,7},{7,4},{8,9},{9,10},{10,1... | collective-permute-start | bytes 1572872 | tf_op jit(solution)/shard_map/ppermute | solution.py:46
  22.8 52.0 %collective-permute-start.1 = (bf16[512,512]{1,0:T(8,128)(2,1)}, bf16[512,512]{1,0:T(8,128)(2,1)}, u32[]{:S(2)}, u32[]{:S(2)}) collective-permute-start(bf16[512,512]{1,0:T(8,128)(2,1)} %convolution_convert_fusion.2), channel_id=1, source_target_pairs={{0,2},{1,3},{2,0},{3,1},{4,6},{5,7},{6,4},{7,5},{8,10},{9,11},{10,... | collective-permute-start | bytes 1572872 | tf_op jit(solution)/shard_map/ppermute | solution.py:46
  26.5 56.1 %collective-permute-start.2 = (bf16[512,512]{1,0:T(8,128)(2,1)}, bf16[512,512]{1,0:T(8,128)(2,1)}, u32[]{:S(2)}, u32[]{:S(2)}) collective-permute-start(bf16[512,512]{1,0:T(8,128)(2,1)} %convolution_convert_fusion.1), channel_id=1, source_target_pairs={{0,3},{1,0},{2,1},{3,2},{4,7},{5,4},{6,5},{7,6},{8,11},{9,8},{10,9... | collective-permute-start | bytes 1572872 | tf_op jit(solution)/shard_map/ppermute | solution.py:46
  150.9 7.4 %copy-start.2 = (bf16[512,512]{1,0:T(8,128)(2,1)S(1)}, bf16[512,512]{1,0:T(8,128)(2,1)}, u32[]{:S(2)}) copy-start(bf16[512,512]{1,0:T(8,128)(2,1)} %param.15) | copy-start | bytes 1572868
  152.3 6.7 %copy-start.6 = (s32[1,8]{1,0:T(1,128)S(1)}, s32[1,8]{1,0:T(1,128)}, u32[]{:S(2)}) copy-start(s32[1,8]{1,0:T(1,128)} %param.27) | copy-start | bytes 100
  153.8 4.9 %copy-start.3 = (bf16[512,512]{1,0:T(8,128)(2,1)S(1)}, bf16[512,512]{1,0:T(8,128)(2,1)}, u32[]{:S(2)}) copy-start(bf16[512,512]{1,0:T(8,128)(2,1)} %param.16) | copy-start | bytes 1572868
  153.8 49.7 %all-to-all-start.1 = ((bf16[4,512,512]{1,2,0:T(8,128)(2,1)}), bf16[4,512,512]{1,2,0:T(8,128)(2,1)}, u32[]{:S(2)}, u32[]{:S(2)}) async-start(bf16[4,512,512]{1,2,0:T(8,128)(2,1)} %broadcast_in_dim.55), calls=%async_computation.1 | async-start | bytes 4194304 | tf_op jit(solution)/shard_map/all_to_all | solution.py:114
  159.4 59.3 %copy-start.4 = (f32[2048]{0:T(1024)S(1)}, f32[2048]{0:T(1024)}, u32[]{:S(2)}) copy-start(f32[2048]{0:T(1024)} %param.20) | copy-start | bytes 24580
  206.4 42.9 %all-to-all-start.2 = ((bf16[4,2,64,2,512]{4,1,3,2,0:T(2,128)(2,1)}), bf16[4,2,64,2,512]{4,1,3,2,0:T(2,128)(2,1)S(1)}, u32[]{:S(2)}, u32[]{:S(2)}) async-start(bf16[4,2,64,2,512]{4,1,3,2,0:T(2,128)(2,1)} %copy.44), calls=%async_computation.2 | async-start | bytes 2097152 | tf_op jit(solution)/shard_map/all_to_all | solution.py:117
  237.8 6.4 %copy-start.9 = (bf16[512,1024]{1,0:T(8,128)(2,1)}, bf16[512,1024]{1,0:T(8,128)(2,1)S(1)}, u32[]{:S(2)}) copy-start(bf16[512,1024]{1,0:T(8,128)(2,1)S(1)} %fusion.17) | copy-start | bytes 3145732
  240.7 3.5 %copy-start.1 = (bf16[1024,2048]{1,0:T(8,128)(2,1)}, bf16[1024,2048]{1,0:T(8,128)(2,1)S(1)}, u32[]{:S(2)}) copy-start(bf16[1024,2048]{1,0:T(8,128)(2,1)S(1)} %slice.21) | copy-start | bytes 12582916
  245.8 13.0 %collective-permute-start.3 = (bf16[512,512]{1,0:T(8,128)(2,1)}, bf16[512,512]{1,0:T(8,128)(2,1)}, u32[]{:S(2)}, u32[]{:S(2)}) collective-permute-start(bf16[512,512]{1,0:T(8,128)(2,1)} %convolution_convert_fusion.7), channel_id=1, source_target_pairs={{0,1},{1,2},{2,3},{3,0},{4,5},{5,6},{6,7},{7,4},{8,9},{9,10},{10,1... | collective-permute-start | bytes 1572872 | tf_op jit(solution)/shard_map/ppermute | solution.py:46
  247.0 44.5 %collective-permute-start.4 = (bf16[512,512]{1,0:T(8,128)(2,1)}, bf16[512,512]{1,0:T(8,128)(2,1)}, u32[]{:S(2)}, u32[]{:S(2)}) collective-permute-start(bf16[512,512]{1,0:T(8,128)(2,1)} %convolution_convert_fusion.6), channel_id=1, source_target_pairs={{0,2},{1,3},{2,0},{3,1},{4,6},{5,7},{6,4},{7,5},{8,10},{9,11},{10,... | collective-permute-start | bytes 1572872 | tf_op jit(solution)/shard_map/ppermute | solution.py:46
  248.1 46.4 %collective-permute-start.5 = (bf16[512,512]{1,0:T(8,128)(2,1)}, bf16[512,512]{1,0:T(8,128)(2,1)}, u32[]{:S(2)}, u32[]{:S(2)}) collective-permute-start(bf16[512,512]{1,0:T(8,128)(2,1)} %convolution_convert_fusion.5), channel_id=1, source_target_pairs={{0,3},{1,0},{2,1},{3,2},{4,7},{5,4},{6,5},{7,6},{8,11},{9,8},{10,9... | collective-permute-start | bytes 1572872 | tf_op jit(solution)/shard_map/ppermute | solution.py:46
Sparse Core Ops, SparseCore 0:
  11.6 183.8 all-gather.1

commit v9 on v8

--- a/solution.py
+++ b/solution.py
@@ -47,6 +47,17 @@
     total = quarter_of(here).astype(jnp.float32)
     for piece in arrived:
         total = total + piece.astype(jnp.float32)
+    return total
+
+
+def reduce_over_dec(part, dec_count):
+    quarter = part.shape[1] // dec_count
+    here = lax.axis_index("dec")
+    total = lax.dynamic_slice_in_dim(part, here * quarter, quarter, 1).astype(jnp.float32)
+    for shift in range(1, dec_count):
+        piece = lax.dynamic_slice_in_dim(part, ((here + shift) % dec_count) * quarter, quarter, 1)
+        pairs = [(i, (i + shift) % dec_count) for i in range(dec_count)]
+        total = total + lax.ppermute(piece, "dec", pairs).astype(jnp.float32)
     return total
 
 
@@ -117,22 +128,29 @@
     moved = lax.all_to_all(ordered, "dec", split_axis=0, concat_axis=0, tiled=True)
     kv_cache = moved.transpose(1, 2, 3, 0, 4).reshape(per_dev, block_slots, 2 * dec_count * features)
 
-    values_f = mixed_rows.astype(jnp.float32)
-    scale = lax.rsqrt(jnp.mean(values_f * values_f, axis=-1, keepdims=True) + 1e-05)
-    normed = (values_f * scale * norm_gain).astype(jnp.bfloat16)
-    low_rank = jnp.dot(normed, adapter_down, preferred_element_type=jnp.float32).astype(
-        jnp.bfloat16
-    )
     contract = (((1,), (1,)), ((), ()))
-    gate = lax.dot_general(
-        normed, gate_rows, contract, preferred_element_type=jnp.float32
-    ) + lax.dot_general(
-        low_rank, adapter_rows, contract, preferred_element_type=jnp.float32
-    )
-    up = lax.dot_general(normed, up_rows, contract, preferred_element_type=jnp.float32)
-    hidden_units = (jax.nn.gelu(gate) * up).astype(jnp.bfloat16)
-    mlp_total = project_reduce_over_dec(hidden_units, down_rows, dec_count)
-    block_out = (column.astype(jnp.float32) + mlp_total).astype(jnp.bfloat16)
+    halves = 2
+    half = cap // halves
+    outs = []
+    for h in range(halves):
+        values_f = mixed_rows[h * half : (h + 1) * half].astype(jnp.float32)
+        scale = lax.rsqrt(jnp.mean(values_f * values_f, axis=-1, keepdims=True) + 1e-05)
+        normed = (values_f * scale * norm_gain).astype(jnp.bfloat16)
+        low_rank = jnp.dot(normed, adapter_down, preferred_element_type=jnp.float32).astype(
+            jnp.bfloat16
+        )
+        gate = lax.dot_general(
+            normed, gate_rows, contract, preferred_element_type=jnp.float32
+        ) + lax.dot_general(low_rank, adapter_rows, contract, preferred_element_type=jnp.float32)
+        up = lax.dot_general(normed, up_rows, contract, preferred_element_type=jnp.float32)
+        hidden_units = (jax.nn.gelu(gate) * up).astype(jnp.bfloat16)
+        down_part = jnp.dot(hidden_units, down_rows, preferred_element_type=jnp.float32).astype(
+            jnp.bfloat16
+        )
+        mlp_total = reduce_over_dec(down_part, dec_count)
+        own = column[h * half : (h + 1) * half].astype(jnp.float32)
+        outs.append((own + mlp_total).astype(jnp.bfloat16))
+    block_out = jnp.concatenate(outs, axis=0)
     return (block_out, kv_cache)
 
 

time: 306 us -> 299 us (0.977)
  waiting for transfers between devices: 137 us -> 110 us
  local copies, waits for them, and re-layouts: 19.5 us -> 25.9 us
  matrix products: 38.8 us -> 45.1 us
  other arithmetic: 8.71 us -> 12.3 us
    ppermute x6 -> x3, waiting for transfers between devices: 94.1 us -> 53.3 us  [project_reduce_over_dec(): arrived.append(lax.ppermute(piece, 'dec', pairs))]
    ppermute x0 -> x6, waiting for transfers between devices: none -> 17.1 us  [reduce_over_dec(): total = total + lax.ppermute(piece, 'dec', pairs).astype(jnp.float32)]
    dot_general x8 -> x4, matrix products: 16.9 us -> 8.22 us  [quarter_of(): jnp.dot(lhs, block, preferred_element_type=jnp.float32).astype(jnp.bfloat16)]
    dot_general x1 -> x2, matrix products: 7.31 us -> 15.9 us  [body(): jnp.dot(hidden_units, down_rows, preferred_element_type=jnp.float32)]
    ppermute x0 -> x6, starting transfers between devices: none -> 6.84 us  [reduce_over_dec(): total = total + lax.ppermute(piece, 'dec', pairs).astype(jnp.float32)]
    dynamic_slice x0 -> x2, local copies, waits for them, and re-layouts: none -> 3.84 us  [reduce_over_dec(): lax.dynamic_slice_in_dim(part, (here + shift) % dec_count * quarter, quar...]
    ppermute x6 -> x3, starting transfers between devices: 8.02 us -> 4.48 us  [project_reduce_over_dec(): arrived.append(lax.ppermute(piece, 'dec', pairs))]
    dot_general x1 -> x2, matrix products: 6.92 us -> 10.3 us  [body(): lax.dot_general(normed, gate_rows, contract, preferred_element_type=jnp.f...]
  transfers between devices with their start and end apart: 9 -> 12, of which waited for: 7 -> 6; matrix products, arithmetic and copies ran while one was open for 20% -> 26% of each run, Pallas kernels for 0% -> 0%
where the time goes in v9:
time: 299 us; the launch traced here: 297 us
  waiting for transfers between devices  110 us (37%)
  blocking collectives  63.7 us (21%)
  matrix products  45.1 us (15%)
  local copies, waits for them, and re-layouts  25.9 us (9%)
  starting transfers between devices  25.8 us (9%)
  between operations  14.3 us (5%)
  other arithmetic  12.3 us (4%)
    all_to_all x1, blocking collectives, body(): lax.all_to_all(permuted.reshape(req_n, per_group, quarter), 'req', split_...  63.7 us
    ppermute x3, waiting for transfers between devices, project_reduce_over_dec(): arrived.append(lax.ppermute(piece, 'dec', pairs))  53.3 us
    all_to_all x1, waiting for transfers between devices, body(): lax.all_to_all(spread, 'dec', split_axis=0, concat_axis=0, tiled=True)  39.8 us
    ppermute x6, waiting for transfers between devices, reduce_over_dec(): total = total + lax.ppermute(piece, 'dec', pairs).astype(jnp.float32)  17.1 us
    dot_general x2, matrix products, body(): jnp.dot(hidden_units, down_rows, preferred_element_type=jnp.float32)  15.9 us
    dot_general x2, matrix products, body(): lax.dot_general(normed, gate_rows, contract, preferred_element_type=jnp.f...  10.3 us
    all_to_all x1, starting transfers between devices, body(): lax.all_to_all(ordered, 'dec', split_axis=0, concat_axis=0, tiled=True)  10 us
    dot_general x4, matrix products, quarter_of(): jnp.dot(lhs, block, preferred_element_type=jnp.float32).astype(jnp.bfloat16)  8.22 us
  transfers between devices with their start and end apart: 12, of which 6 were waited for; matrix products, arithmetic and copies ran while one was open for 26% of the time, Pallas kernels for 0%

profile of v9, /device:TPU:33, one launch (start us, length us, event | category | flops | bytes accessed | tf_op | source)
XLA Modules:
  0.0 297.4 jit_solution(13239214364334172880)
XLA Ops:
  13.5 2.4 fusion.102
  20.1 2.3 convolution_convert_fusion.2
  23.8 2.3 convolution_convert_fusion.1
  28.9 4.1 %collective-permute-done = bf16[512,512]{1,0:T(8,128)(2,1)} collective-permute-done((bf16[512,512]{1,0:T(8,128)(2,1)}, bf16[512,512]{1,0:T(8,128)(2,1)}, u32[]{:S(2)}, u32[]{:S(2)}) %collective-permute-start) | collective-permute-done | bytes 524320 | tf_op jit(solution)/shard_map/ppermute | solution.py:46
  33.0 41.4 %collective-permute-done.1 = bf16[512,512]{1,0:T(8,128)(2,1)} collective-permute-done((bf16[512,512]{1,0:T(8,128)(2,1)}, bf16[512,512]{1,0:T(8,128)(2,1)}, u32[]{:S(2)}, u32[]{:S(2)}) %collective-permute-start.1) | collective-permute-done | bytes 524320 | tf_op jit(solution)/shard_map/ppermute | solution.py:46
  74.4 7.8 %collective-permute-done.2 = bf16[512,512]{1,0:T(8,128)(2,1)} collective-permute-done((bf16[512,512]{1,0:T(8,128)(2,1)}, bf16[512,512]{1,0:T(8,128)(2,1)}, u32[]{:S(2)}, u32[]{:S(2)}) %collective-permute-start.2) | collective-permute-done | bytes 524320 | tf_op jit(solution)/shard_map/ppermute | solution.py:46
  84.5 2.6 gather_fusion
  88.3 63.7 %all_to_all.15 = bf16[64,8,512]{2,1,0:T(8,128)(2,1)S(1)} all-to-all(bf16[64,8,512]{2,1,0:T(8,128)(2,1)S(1)} %bitcast_select_fusion), channel_id=1, replica_groups=mesh['req'=64,'dec'=4] {'req'}, dimensions={0} | all-to-all | bytes 1048576 | tf_op jit(solution)/shard_map/all_to_all | solution.py:121
  153.0 2.5 broadcast_in_dim.60
  155.5 4.4 %all-to-all-start.1 = ((bf16[4,512,512]{1,2,0:T(8,128)(2,1)}), bf16[4,512,512]{1,2,0:T(8,128)(2,1)}, u32[]{:S(2)}, u32[]{:S(2)}) async-start(bf16[4,512,512]{1,2,0:T(8,128)(2,1)} %broadcast_in_dim.60), calls=%async_computation.1 | async-start | bytes 4194304 | tf_op jit(solution)/shard_map/all_to_all | solution.py:125
  165.2 39.8 %all-to-all-done.1 = bf16[4,512,512]{1,2,0:T(8,128)(2,1)} async-done(((bf16[4,512,512]{1,2,0:T(8,128)(2,1)}), bf16[4,512,512]{1,2,0:T(8,128)(2,1)}, u32[]{:S(2)}, u32[]{:S(2)}) %all-to-all-start.1) | async-done | bytes 2097184 | tf_op jit(solution)/shard_map/all_to_all | solution.py:125
  205.1 2.9 copy.44
  208.0 10.0 %all-to-all-start.2 = ((bf16[4,2,64,2,512]{4,1,3,2,0:T(2,128)(2,1)}), bf16[4,2,64,2,512]{4,1,3,2,0:T(2,128)(2,1)}, u32[]{:S(2)}, u32[]{:S(2)}) async-start(bf16[4,2,64,2,512]{4,1,3,2,0:T(2,128)(2,1)} %copy.44), calls=%async_computation.2 | async-start | bytes 2097152 | tf_op jit(solution)/shard_map/all_to_all | solution.py:128
  220.1 5.1 %fusion.9 = f32[256,1024]{1,0:T(8,128)} fusion(bf16[1024,6272]{1,0:T(8,128)(2,1)} %all-gather.2.cloned.1.call-done, f32[256]{0:T(256)S(1)} %add_rsqrt_fusion, f32[2048]{0:T(1024)S(1)} %copy-done.6, bf16[512,2048]{0,1:T(8,128)(2,1)} %bitcast.10), kind=kOutput, calls=%fused_computation.13 | convolution fusion | flops 1075838976 | bytes 6300672 | tf_op jit(solution)/shard_map/dot_general | solution.py:142
  225.2 4.1 %fusion.61 = f32[256,1024]{1,0:T(8,128)} fusion(f32[256,1024]{1,0:T(8,128)} %fusion.9, bf16[2048,128]{1,0:T(8,128)(2,1)} %param.21, bf16[1024,6272]{1,0:T(8,128)(2,1)} %all-gather.2.cloned.1.call-done, f32[256]{0:T(256)S(1)} %add_rsqrt_fusion, f32[2048]{0:T(1024)S(1)} %copy-done.6, bf16[512,2048]{0,1:T(8,128)(2,1)} %bitcast.10), kind=kOutput, calls=%fused_computation.64 | convolution fusion | flops 205815808 | bytes 3941376 | tf_op jit(solution)/shard_map/dot_general | solution.py:144
  229.3 7.9 %fusion.17 = bf16[256,2048]{1,0:T(8,128)(2,1)} fusion(bf16[1024,6272]{1,0:T(8,128)(2,1)} %all-gather.2.cloned.1.call-done, f32[256,1024]{1,0:T(8,128)} %fusion.61, f32[256]{0:T(256)S(1)} %add_rsqrt_fusion, f32[2048]{0:T(1024)S(1)} %copy-done.6, bf16[512,2048]{0,1:T(8,128)(2,1)} %bitcast.10), kind=kOutput, calls=%fused_computation.23 | convolution fusion | flops 2150629376 | bytes 11543552 | tf_op jit(solution)/shard_map/dot_general | solution.py:147
  242.7 5.1 %fusion.11 = f32[256,1024]{1,0:T(8,128)} fusion(bf16[1024,6272]{1,0:T(8,128)(2,1)} %all-gather.2.cloned.1.call-done, f32[2048]{0:T(1024)S(1)} %copy-done.6, f32[256]{0:T(256)S(1)} %add_rsqrt_fusion.1, bf16[512,2048]{0,1:T(8,128)(2,1)} %bitcast.10), kind=kOutput, calls=%fused_computation.15 | convolution fusion | flops 1075838976 | bytes 6300672 | tf_op jit(solution)/shard_map/dot_general | solution.py:142
  247.8 4.1 %fusion.54 = f32[256,1024]{1,0:T(8,128)} fusion(f32[256,1024]{1,0:T(8,128)} %fusion.11, bf16[2048,128]{1,0:T(8,128)(2,1)} %param.21, bf16[1024,6272]{1,0:T(8,128)(2,1)} %all-gather.2.cloned.1.call-done, f32[2048]{0:T(1024)S(1)} %copy-done.6, f32[256]{0:T(256)S(1)} %add_rsqrt_fusion.1, bf16[512,2048]{0,1:T(8,128)(2,1)} %bitcast.10), kind=kOutput, calls=%fused_computation.57 | convolution fusion | flops 205815808 | bytes 3941376 | tf_op jit(solution)/shard_map/dot_general | solution.py:144
  252.0 7.9 %fusion.14 = bf16[256,2048]{1,0:T(8,128)(2,1)} fusion(bf16[1024,6272]{1,0:T(8,128)(2,1)} %all-gather.2.cloned.1.call-done, f32[256,1024]{1,0:T(8,128)} %fusion.54, f32[2048]{0:T(1024)S(1)} %copy-done.6, f32[256]{0:T(256)S(1)} %add_rsqrt_fusion.1, bf16[512,2048]{0,1:T(8,128)(2,1)} %bitcast.10), kind=kOutput, calls=%fused_computation.22 | convolution fusion | flops 2150629376 | bytes 11543552 | tf_op jit(solution)/shard_map/dot_general | solution.py:147
  262.1 3.0 %collective-permute-start.4 = (bf16[256,512]{1,0:T(8,128)(2,1)}, bf16[256,512]{1,0:T(8,128)(2,1)}, u32[]{:S(2)}, u32[]{:S(2)}) collective-permute-start(bf16[256,512]{1,0:T(8,128)(2,1)} %get-tuple-element.10), channel_id=1, source_target_pairs={{0,2},{1,3},{2,0},{3,1},{4,6},{5,7},{6,4},{7,5},{8,10},{9,11},{10,... | collective-permute-start | bytes 786440 | tf_op jit(solution)/shard_map/ppermute | solution.py:60
  265.1 3.0 %copy.45 = bf16[2,64,2,4,512]{4,3,2,1,0:T(4,128)(2,1)} copy(bf16[2,64,2,4,512]{4,0,2,1,3:T(2,128)(2,1)} %bitcast.20) | data formatting | bytes 2097152 | tf_op jit(solution)/shard_map/transpose | solution.py:129
  268.2 2.6 reshape.157
  270.8 14.6 %collective-permute-done.4 = bf16[256,512]{1,0:T(8,128)(2,1)} collective-permute-done((bf16[256,512]{1,0:T(8,128)(2,1)}, bf16[256,512]{1,0:T(8,128)(2,1)}, u32[]{:S(2)}, u32[]{:S(2)}) %collective-permute-start.4) | collective-permute-done | bytes 262176 | tf_op jit(solution)/shard_map/ppermute | solution.py:60
  285.4 2.5 collective-permute-done.5
  (60 shorter events, 36.7 us)
Async XLA Ops:
  7.2 10.0 %copy-start = (bf16[512,2048]{1,0:T(8,128)(2,1)S(1)}, bf16[512,2048]{1,0:T(8,128)(2,1)}, u32[]{:S(2)}) copy-start(bf16[512,2048]{1,0:T(8,128)(2,1)} %param.19) | copy-start | bytes 6291460
  7.2 5.6 %copy-start.2 = (bf16[512,512]{1,0:T(8,128)(2,1)S(1)}, bf16[512,512]{1,0:T(8,128)(2,1)}, u32[]{:S(2)}) copy-start(bf16[512,512]{1,0:T(8,128)(2,1)} %param.14) | copy-start | bytes 1572868
  7.2 5.6 %copy-start.1 = (bf16[512,512]{1,0:T(8,128)(2,1)S(1)}, bf16[512,512]{1,0:T(8,128)(2,1)}, u32[]{:S(2)}) copy-start(bf16[512,512]{1,0:T(8,128)(2,1)} %param.15) | copy-start | bytes 1572868
  7.2 212.9 %all-gather.2.cloned.1.call-start = ((), (), s32[]{:S(2)}) async-start(), calls=%async_computation.3 | async-start | bytes 13045760 | tf_op jit(solution)/shard_map/all_gather | solution.py:89
  13.5 2.4 copy-start.3
  16.4 0.8 copy-start.7
  18.5 9.6 %copy-start.4 = (s32[1,512]{1,0:T(1,128)S(1)}, s32[1,512]{1,0:T(1,128)}, u32[]{:S(2)}) copy-start(s32[1,512]{1,0:T(1,128)} %param.26) | copy-start | bytes 6148
  18.5 14.5 %collective-permute-start = (bf16[512,512]{1,0:T(8,128)(2,1)}, bf16[512,512]{1,0:T(8,128)(2,1)}, u32[]{:S(2)}, u32[]{:S(2)}) collective-permute-start(bf16[512,512]{1,0:T(8,128)(2,1)} %convolution_convert_fusion.3), channel_id=1, source_target_pairs={{0,1},{1,2},{2,3},{3,0},{4,5},{5,6},{6,7},{7,4},{8,9},{9,10},{10,1... | collective-permute-start | bytes 1572872 | tf_op jit(solution)/shard_map/ppermute | solution.py:46
  22.4 51.9 %collective-permute-start.1 = (bf16[512,512]{1,0:T(8,128)(2,1)}, bf16[512,512]{1,0:T(8,128)(2,1)}, u32[]{:S(2)}, u32[]{:S(2)}) collective-permute-start(bf16[512,512]{1,0:T(8,128)(2,1)} %convolution_convert_fusion.2), channel_id=1, source_target_pairs={{0,2},{1,3},{2,0},{3,1},{4,6},{5,7},{6,4},{7,5},{8,10},{9,11},{10,... | collective-permute-start | bytes 1572872 | tf_op jit(solution)/shard_map/ppermute | solution.py:46
  26.1 56.1 %collective-permute-start.2 = (bf16[512,512]{1,0:T(8,128)(2,1)}, bf16[512,512]{1,0:T(8,128)(2,1)}, u32[]{:S(2)}, u32[]{:S(2)}) collective-permute-start(bf16[512,512]{1,0:T(8,128)(2,1)} %convolution_convert_fusion.1), channel_id=1, source_target_pairs={{0,3},{1,0},{2,1},{3,2},{4,7},{5,4},{6,5},{7,6},{8,11},{9,8},{10,9... | collective-permute-start | bytes 1572872 | tf_op jit(solution)/shard_map/ppermute | solution.py:46
  155.5 49.6 %all-to-all-start.1 = ((bf16[4,512,512]{1,2,0:T(8,128)(2,1)}), bf16[4,512,512]{1,2,0:T(8,128)(2,1)}, u32[]{:S(2)}, u32[]{:S(2)}) async-start(bf16[4,512,512]{1,2,0:T(8,128)(2,1)} %broadcast_in_dim.60), calls=%async_computation.1 | async-start | bytes 4194304 | tf_op jit(solution)/shard_map/all_to_all | solution.py:125
  159.9 1.7 copy-start.5
  208.0 12.1 %copy-start.6 = (f32[2048]{0:T(1024)S(1)}, f32[2048]{0:T(1024)}, u32[]{:S(2)}) copy-start(f32[2048]{0:T(1024)} %param.20) | copy-start | bytes 24580
  208.0 57.1 %all-to-all-start.2 = ((bf16[4,2,64,2,512]{4,1,3,2,0:T(2,128)(2,1)}), bf16[4,2,64,2,512]{4,1,3,2,0:T(2,128)(2,1)}, u32[]{:S(2)}, u32[]{:S(2)}) async-start(bf16[4,2,64,2,512]{4,1,3,2,0:T(2,128)(2,1)} %copy.44), calls=%async_computation.2 | async-start | bytes 2097152 | tf_op jit(solution)/shard_map/all_to_all | solution.py:128
  239.1 26.0 %collective-permute-start.6 = (bf16[256,512]{1,0:T(8,128)(2,1)}, bf16[256,512]{1,0:T(8,128)(2,1)}, u32[]{:S(2)}, u32[]{:S(2)}) collective-permute-start(bf16[256,512]{1,0:T(8,128)(2,1)} %get-tuple-element.11), channel_id=1, source_target_pairs={{0,1},{1,2},{2,3},{3,0},{4,5},{5,6},{6,7},{7,4},{8,9},{9,10},{10,1... | collective-permute-start | bytes 786440 | tf_op jit(solution)/shard_map/ppermute | solution.py:60
  240.3 30.4 %collective-permute-start.7 = (bf16[256,512]{1,0:T(8,128)(2,1)S(1)}, bf16[256,512]{1,0:T(8,128)(2,1)}, u32[]{:S(2)}, u32[]{:S(2)}) collective-permute-start(bf16[256,512]{1,0:T(8,128)(2,1)S(1)} %get-tuple-element.13), channel_id=1, source_target_pairs={{0,2},{1,3},{2,0},{3,1},{4,6},{5,7},{6,4},{7,5},{8,10},{9,11},{10,... | collective-permute-start | bytes 786440 | tf_op jit(solution)/shard_map/ppermute | solution.py:60
  241.5 29.3 %collective-permute-start.8 = (bf16[256,512]{1,0:T(8,128)(2,1)S(1)}, bf16[256,512]{1,0:T(8,128)(2,1)}, u32[]{:S(2)}, u32[]{:S(2)}) collective-permute-start(bf16[256,512]{1,0:T(8,128)(2,1)S(1)} %get-tuple-element.12), channel_id=1, source_target_pairs={{0,3},{1,0},{2,1},{3,2},{4,7},{5,4},{6,5},{7,6},{8,11},{9,8},{10,9... | collective-permute-start | bytes 786440 | tf_op jit(solution)/shard_map/ppermute | solution.py:60
  261.9 8.9 %collective-permute-start.3 = (bf16[256,512]{1,0:T(8,128)(2,1)}, bf16[256,512]{1,0:T(8,128)(2,1)}, u32[]{:S(2)}, u32[]{:S(2)}) collective-permute-start(bf16[256,512]{1,0:T(8,128)(2,1)} %get-tuple-element.8), channel_id=1, source_target_pairs={{0,1},{1,2},{2,3},{3,0},{4,5},{5,6},{6,7},{7,4},{8,9},{9,10},{10,1... | collective-permute-start | bytes 786440 | tf_op jit(solution)/shard_map/ppermute | solution.py:60
  262.1 23.3 %collective-permute-start.4 = (bf16[256,512]{1,0:T(8,128)(2,1)}, bf16[256,512]{1,0:T(8,128)(2,1)}, u32[]{:S(2)}, u32[]{:S(2)}) collective-permute-start(bf16[256,512]{1,0:T(8,128)(2,1)} %get-tuple-element.10), channel_id=1, source_target_pairs={{0,2},{1,3},{2,0},{3,1},{4,6},{5,7},{6,4},{7,5},{8,10},{9,11},{10,... | collective-permute-start | bytes 786440 | tf_op jit(solution)/shard_map/ppermute | solution.py:60
  265.1 22.7 %collective-permute-start.5 = (bf16[256,512]{1,0:T(8,128)(2,1)S(1)}, bf16[256,512]{1,0:T(8,128)(2,1)}, u32[]{:S(2)}, u32[]{:S(2)}) collective-permute-start(bf16[256,512]{1,0:T(8,128)(2,1)S(1)} %get-tuple-element.9), channel_id=1, source_target_pairs={{0,3},{1,0},{2,1},{3,2},{4,7},{5,4},{6,5},{7,6},{8,11},{9,8},{10,9... | collective-permute-start | bytes 786440 | tf_op jit(solution)/shard_map/ppermute | solution.py:60
Sparse Core Ops, SparseCore 0:
  11.7 182.9 all-gather.1

commit v10 on v8

--- a/solution.py
+++ b/solution.py
@@ -47,6 +47,17 @@
     total = quarter_of(here).astype(jnp.float32)
     for piece in arrived:
         total = total + piece.astype(jnp.float32)
+    return total
+
+
+def reduce_over_dec(part, dec_count):
+    quarter = part.shape[1] // dec_count
+    here = lax.axis_index("dec")
+    total = lax.dynamic_slice_in_dim(part, here * quarter, quarter, 1).astype(jnp.float32)
+    for shift in range(1, dec_count):
+        piece = lax.dynamic_slice_in_dim(part, ((here + shift) % dec_count) * quarter, quarter, 1)
+        pairs = [(i, (i + shift) % dec_count) for i in range(dec_count)]
+        total = total + lax.ppermute(piece, "dec", pairs).astype(jnp.float32)
     return total
 
 
@@ -110,30 +121,46 @@
     column = lax.all_to_all(
         permuted.reshape(req_n, per_group, quarter), "req", split_axis=0, concat_axis=0, tiled=True
     ).reshape(cap, quarter)
-    spread = jnp.broadcast_to(column[None], (dec_count, cap, quarter))
-    quarters = lax.all_to_all(spread, "dec", split_axis=0, concat_axis=0, tiled=True)
-    mixed_rows = quarters.transpose(1, 0, 2).reshape(cap, dec_count * quarter)
-    mixed_rows, ordered = lax.optimization_barrier((mixed_rows, ordered))
+    halves = 2
+    half = cap // halves
+    mixed_halves = []
+    for h in range(halves):
+        rows_h = column[h * half : (h + 1) * half]
+        spread = jnp.broadcast_to(rows_h[None], (dec_count, half, quarter))
+        quarters = lax.all_to_all(spread, "dec", split_axis=0, concat_axis=0, tiled=True)
+        mixed_halves.append(quarters.transpose(1, 0, 2).reshape(half, dec_count * quarter))
+    mixed_halves[-1], ordered = lax.optimization_barrier((mixed_halves[-1], ordered))
     moved = lax.all_to_all(ordered, "dec", split_axis=0, concat_axis=0, tiled=True)
     kv_cache = moved.transpose(1, 2, 3, 0, 4).reshape(per_dev, block_slots, 2 * dec_count * features)
 
-    values_f = mixed_rows.astype(jnp.float32)
+    outs = []
+    for h in range(halves):
+        outs.append(mlp_half(h, mixed_halves[h], column, half, norm_gain, adapter_down, gate_rows,
+                             adapter_rows, up_rows, down_rows, dec_count))
+    block_out = jnp.concatenate(outs, axis=0)
+    return (block_out, kv_cache)
+
+
+def mlp_half(h, mixed, column, half, norm_gain, adapter_down, gate_rows, adapter_rows, up_rows,
+             down_rows, dec_count):
+    contract = (((1,), (1,)), ((), ()))
+    values_f = mixed.astype(jnp.float32)
     scale = lax.rsqrt(jnp.mean(values_f * values_f, axis=-1, keepdims=True) + 1e-05)
     normed = (values_f * scale * norm_gain).astype(jnp.bfloat16)
     low_rank = jnp.dot(normed, adapter_down, preferred_element_type=jnp.float32).astype(
         jnp.bfloat16
     )
-    contract = (((1,), (1,)), ((), ()))
     gate = lax.dot_general(
         normed, gate_rows, contract, preferred_element_type=jnp.float32
-    ) + lax.dot_general(
-        low_rank, adapter_rows, contract, preferred_element_type=jnp.float32
-    )
+    ) + lax.dot_general(low_rank, adapter_rows, contract, preferred_element_type=jnp.float32)
     up = lax.dot_general(normed, up_rows, contract, preferred_element_type=jnp.float32)
     hidden_units = (jax.nn.gelu(gate) * up).astype(jnp.bfloat16)
-    mlp_total = project_reduce_over_dec(hidden_units, down_rows, dec_count)
-    block_out = (column.astype(jnp.float32) + mlp_total).astype(jnp.bfloat16)
-    return (block_out, kv_cache)
+    down_part = jnp.dot(hidden_units, down_rows, preferred_element_type=jnp.float32).astype(
+        jnp.bfloat16
+    )
+    mlp_total = reduce_over_dec(down_part, dec_count)
+    own = column[h * half : (h + 1) * half].astype(jnp.float32)
+    return (own + mlp_total).astype(jnp.bfloat16)
 
 
 def solution(mesh):

time: 306 us -> 303 us (level)
  waiting for transfers between devices: 137 us -> 106 us
  starting transfers between devices: 22.8 us -> 32.3 us
  local copies, waits for them, and re-layouts: 19.5 us -> 27.2 us
  matrix products: 38.8 us -> 43.7 us
  other arithmetic: 8.71 us -> 12.5 us
    ppermute x6 -> x3, waiting for transfers between devices: 94.1 us -> 53.2 us  [project_reduce_over_dec(): arrived.append(lax.ppermute(piece, 'dec', pairs))]
    ppermute x0 -> x6, waiting for transfers between devices: none -> 19.4 us  [reduce_over_dec(): total = total + lax.ppermute(piece, 'dec', pairs).astype(jnp.float32)]
    dot_general x3 -> x6, matrix products: 19.1 us -> 31.8 us  [the longest x2 14.7 us: mlp_half(): jnp.dot(hidden_units, down_rows, preferred_element_type=jnp.float32)]
    all_to_all x1 -> x2, waiting for transfers between devices: 42.9 us -> 33.9 us  [body(): lax.all_to_all(spread, 'dec', split_axis=0, concat_axis=0, tiled=True)]
    all_to_all x1 -> x2, starting transfers between devices: 4.57 us -> 13.6 us  [body(): lax.all_to_all(spread, 'dec', split_axis=0, concat_axis=0, tiled=True)]
    dot_general x8 -> x4, matrix products: 16.9 us -> 8.07 us  [quarter_of(): jnp.dot(lhs, block, preferred_element_type=jnp.float32).astype(jnp.bfloat16)]
    ppermute x0 -> x6, starting transfers between devices: none -> 6.81 us  [reduce_over_dec(): total = total + lax.ppermute(piece, 'dec', pairs).astype(jnp.float32)]
    dynamic_slice x0 -> x2, local copies, waits for them, and re-layouts: none -> 3.93 us  [reduce_over_dec(): lax.dynamic_slice_in_dim(part, (here + shift) % dec_count * quarter, quar...]
  transfers between devices with their start and end apart: 9 -> 13, of which waited for: 7 -> 9; matrix products, arithmetic and copies ran while one was open for 20% -> 26% of each run, Pallas kernels for 0% -> 0%
where the time goes in v10:
time: 303 us; the launch traced here: 300 us
  waiting for transfers between devices  106 us (35%)
  blocking collectives  64 us (21%)
  matrix products  43.7 us (14%)
  starting transfers between devices  32.3 us (11%)
  local copies, waits for them, and re-layouts  27.2 us (9%)
  between operations  14.3 us (5%)
  other arithmetic  12.5 us (4%)
    all_to_all x1, blocking collectives, body(): lax.all_to_all(permuted.reshape(req_n, per_group, quarter), 'req', split_...  64 us
    ppermute x3, waiting for transfers between devices, project_reduce_over_dec(): arrived.append(lax.ppermute(piece, 'dec', pairs))  53.2 us
    all_to_all x2, waiting for transfers between devices, body(): lax.all_to_all(spread, 'dec', split_axis=0, concat_axis=0, tiled=True)  33.9 us
    ppermute x6, waiting for transfers between devices, reduce_over_dec(): total = total + lax.ppermute(piece, 'dec', pairs).astype(jnp.float32)  19.4 us
    dot_general x2, matrix products, mlp_half(): jnp.dot(hidden_units, down_rows, preferred_element_type=jnp.float32)  14.7 us
    all_to_all x2, starting transfers between devices, body(): lax.all_to_all(spread, 'dec', split_axis=0, concat_axis=0, tiled=True)  13.6 us
    dot_general x2, matrix products, mlp_half(): lax.dot_general(normed, gate_rows, contract, preferred_element_type=jnp.f...  10 us
    dot_general x4, matrix products, quarter_of(): jnp.dot(lhs, block, preferred_element_type=jnp.float32).astype(jnp.bfloat16)  8.07 us
  transfers between devices with their start and end apart: 13, of which 9 were waited for; matrix products, arithmetic and copies ran while one was open for 26% of the time, Pallas kernels for 0%

profile of v10, /device:TPU:33, one launch (start us, length us, event | category | flops | bytes accessed | tf_op | source)
XLA Modules:
  0.0 300.4 jit_solution(16508284982034594258)
XLA Ops:
  13.9 2.4 fusion.94
  20.5 2.3 convolution_convert_fusion.2
  29.4 4.2 %collective-permute-done = bf16[512,512]{1,0:T(8,128)(2,1)} collective-permute-done((bf16[512,512]{1,0:T(8,128)(2,1)}, bf16[512,512]{1,0:T(8,128)(2,1)}, u32[]{:S(2)}, u32[]{:S(2)}) %collective-permute-start) | collective-permute-done | bytes 524320 | tf_op jit(solution)/shard_map/ppermute | solution.py:46
  33.6 41.1 %collective-permute-done.1 = bf16[512,512]{1,0:T(8,128)(2,1)} collective-permute-done((bf16[512,512]{1,0:T(8,128)(2,1)}, bf16[512,512]{1,0:T(8,128)(2,1)}, u32[]{:S(2)}, u32[]{:S(2)}) %collective-permute-start.1) | collective-permute-done | bytes 524320 | tf_op jit(solution)/shard_map/ppermute | solution.py:46
  74.7 7.9 %collective-permute-done.2 = bf16[512,512]{1,0:T(8,128)(2,1)} collective-permute-done((bf16[512,512]{1,0:T(8,128)(2,1)}, bf16[512,512]{1,0:T(8,128)(2,1)}, u32[]{:S(2)}, u32[]{:S(2)}) %collective-permute-start.2) | collective-permute-done | bytes 524320 | tf_op jit(solution)/shard_map/ppermute | solution.py:46
  86.8 64.0 %all_to_all.20 = bf16[64,8,512]{2,1,0:T(8,128)(2,1)S(1)} all-to-all(bf16[64,8,512]{2,1,0:T(8,128)(2,1)S(1)} %bitcast_select_fusion), channel_id=1, replica_groups=mesh['req'=64,'dec'=4] {'req'}, dimensions={0} | all-to-all | bytes 1048576 | tf_op jit(solution)/shard_map/all_to_all | solution.py:121
  153.6 3.6 %all-to-all-start.2 = ((bf16[4,256,512]{1,2,0:T(8,128)(2,1)}), bf16[4,256,512]{1,2,0:T(8,128)(2,1)S(1)}, u32[]{:S(2)}, u32[]{:S(2)}) async-start(bf16[4,256,512]{1,2,0:T(8,128)(2,1)} %broadcast_in_dim.65), calls=%async_computation.2 | async-start | bytes 2097152 | tf_op jit(solution)/shard_map/all_to_all | solution.py:130
  158.3 22.6 %all-to-all-done.2 = bf16[4,256,512]{1,2,0:T(8,128)(2,1)S(1)} async-done(((bf16[4,256,512]{1,2,0:T(8,128)(2,1)}), bf16[4,256,512]{1,2,0:T(8,128)(2,1)S(1)}, u32[]{:S(2)}, u32[]{:S(2)}) %all-to-all-start.2) | async-done | bytes 1048608 | tf_op jit(solution)/shard_map/all_to_all | solution.py:130
  182.3 9.9 %all-to-all-start.1 = ((bf16[4,256,512]{1,2,0:T(8,128)(2,1)}), bf16[4,256,512]{1,2,0:T(8,128)(2,1)S(1)}, u32[]{:S(2)}, u32[]{:S(2)}) async-start(bf16[4,256,512]{1,2,0:T(8,128)(2,1)} %broadcast_in_dim.64), calls=%async_computation.1 | async-start | bytes 2097152 | tf_op jit(solution)/shard_map/all_to_all | solution.py:130
  198.5 2.9 copy.47
  203.0 11.3 %all-to-all-done.1 = bf16[4,256,512]{1,2,0:T(8,128)(2,1)S(1)} async-done(((bf16[4,256,512]{1,2,0:T(8,128)(2,1)}), bf16[4,256,512]{1,2,0:T(8,128)(2,1)S(1)}, u32[]{:S(2)}, u32[]{:S(2)}) %all-to-all-start.1) | async-done | bytes 1048608 | tf_op jit(solution)/shard_map/all_to_all | solution.py:130
  214.2 7.5 %all-to-all-start.3 = ((bf16[4,2,64,2,512]{4,1,3,2,0:T(2,128)(2,1)}), bf16[4,2,64,2,512]{4,1,3,2,0:T(2,128)(2,1)}, u32[]{:S(2)}, u32[]{:S(2)}) async-start(bf16[4,2,64,2,512]{4,1,3,2,0:T(2,128)(2,1)} %copy.47), calls=%async_computation.3 | async-start | bytes 2097152 | tf_op jit(solution)/shard_map/all_to_all | solution.py:133
  223.3 5.2 %fusion.9 = f32[256,1024]{1,0:T(8,128)} fusion(bf16[1024,6272]{1,0:T(8,128)(2,1)} %all-gather.2.cloned.1.call-done, bf16[256,2048]{0,1:T(8,128)(2,1)} %bitcast.69, f32[256]{0:T(256)S(1)} %add_rsqrt_fusion, f32[2048]{0:T(1024)S(1)} %copy-done.6), kind=kOutput, calls=%fused_computation.13 | convolution fusion | flops 1075838976 | bytes 6300672 | tf_op jit(solution)/shard_map/dot_general | solution.py:153
  228.6 3.7 %fusion.60 = f32[256,1024]{1,0:T(8,128)} fusion(f32[256,1024]{1,0:T(8,128)} %fusion.9, bf16[2048,128]{1,0:T(8,128)(2,1)} %param.21, bf16[1024,6272]{1,0:T(8,128)(2,1)} %all-gather.2.cloned.1.call-done, bf16[256,2048]{0,1:T(8,128)(2,1)S(1)} %bitcast.70, f32[256]{0:T(256)S(1)} %add_rsqrt_fusion, f32[2048]{0:T(1024)S(1)} %copy-done.6), kind=kOutput, calls=%fused_computation.63 | convolution fusion | flops 205815808 | bytes 3941376 | tf_op jit(solution)/shard_map/dot_general | solution.py:155
  232.3 7.6 %fusion.17 = bf16[256,2048]{1,0:T(8,128)(2,1)} fusion(bf16[1024,6272]{1,0:T(8,128)(2,1)} %all-gather.2.cloned.1.call-done, f32[256,1024]{1,0:T(8,128)} %fusion.60, bf16[256,2048]{0,1:T(8,128)(2,1)S(1)} %bitcast.71, f32[256]{0:T(256)S(1)} %add_rsqrt_fusion, f32[2048]{0:T(1024)S(1)} %copy-done.6), kind=kOutput, calls=%fused_computation.21 | convolution fusion | flops 2150629376 | bytes 11543552 | tf_op jit(solution)/shard_map/dot_general | solution.py:158
  245.5 4.8 %fusion.11 = f32[256,1024]{1,0:T(8,128)} fusion(bf16[256,2048]{0,1:T(8,128)(2,1)} %fusion.24, bf16[1024,6272]{1,0:T(8,128)(2,1)} %all-gather.2.cloned.1.call-done), kind=kOutput, calls=%fused_computation.15 | convolution fusion | flops 1073741824 | bytes 6291456 | tf_op jit(solution)/shard_map/dot_general | solution.py:153
  250.2 3.4 %fusion.53 = f32[256,1024]{1,0:T(8,128)} fusion(f32[256,1024]{1,0:T(8,128)} %fusion.11, bf16[256,2048]{0,1:T(8,128)(2,1)S(1)} %copy-done.5, bf16[2048,128]{1,0:T(8,128)(2,1)} %param.21, bf16[1024,6272]{1,0:T(8,128)(2,1)} %all-gather.2.cloned.1.call-done), kind=kOutput, calls=%fused_computation.56 | convolution fusion | flops 203718656 | bytes 3932160 | tf_op jit(solution)/shard_map/dot_general | solution.py:155
  253.6 7.1 %fusion.14 = bf16[256,2048]{1,0:T(8,128)(2,1)} fusion(bf16[1024,6272]{1,0:T(8,128)(2,1)} %all-gather.2.cloned.1.call-done, f32[256,1024]{1,0:T(8,128)} %fusion.53, bf16[256,2048]{0,1:T(8,128)(2,1)S(1)} %copy-done.5), kind=kOutput, calls=%fused_computation.20 | convolution fusion | flops 2148532224 | bytes 11534336 | tf_op jit(solution)/shard_map/dot_general | solution.py:158
  262.9 3.0 %collective-permute-start.4 = (bf16[256,512]{1,0:T(8,128)(2,1)S(1)}, bf16[256,512]{1,0:T(8,128)(2,1)}, u32[]{:S(2)}, u32[]{:S(2)}) collective-permute-start(bf16[256,512]{1,0:T(8,128)(2,1)S(1)} %get-tuple-element.8), channel_id=1, source_target_pairs={{0,2},{1,3},{2,0},{3,1},{4,6},{5,7},{6,4},{7,5},{8,10},{9,11},{10,... | collective-permute-start | bytes 786440 | tf_op jit(solution)/shard_map/ppermute | solution.py:60
  265.9 3.0 %copy.48 = bf16[2,64,2,4,512]{4,3,2,1,0:T(4,128)(2,1)} copy(bf16[2,64,2,4,512]{4,0,2,1,3:T(2,128)(2,1)} %bitcast.21) | data formatting | bytes 2097152 | tf_op jit(solution)/shard_map/transpose | solution.py:134
  268.9 2.6 reshape.159
  271.5 6.1 %collective-permute-done.8 = bf16[256,512]{1,0:T(8,128)(2,1)} collective-permute-done((bf16[256,512]{1,0:T(8,128)(2,1)S(1)}, bf16[256,512]{1,0:T(8,128)(2,1)}, u32[]{:S(2)}, u32[]{:S(2)}) %collective-permute-start.8) | collective-permute-done | bytes 262176 | tf_op jit(solution)/shard_map/ppermute | solution.py:60
  277.6 5.6 %collective-permute-done.3 = bf16[256,512]{1,0:T(8,128)(2,1)} collective-permute-done((bf16[256,512]{1,0:T(8,128)(2,1)}, bf16[256,512]{1,0:T(8,128)(2,1)}, u32[]{:S(2)}, u32[]{:S(2)}) %collective-permute-start.3) | collective-permute-done | bytes 262176 | tf_op jit(solution)/shard_map/ppermute | solution.py:60
  283.3 5.5 %collective-permute-done.4 = bf16[256,512]{1,0:T(8,128)(2,1)} collective-permute-done((bf16[256,512]{1,0:T(8,128)(2,1)S(1)}, bf16[256,512]{1,0:T(8,128)(2,1)}, u32[]{:S(2)}, u32[]{:S(2)}) %collective-permute-start.4) | collective-permute-done | bytes 262176 | tf_op jit(solution)/shard_map/ppermute | solution.py:60
  (73 shorter events, 48.8 us)
Async XLA Ops:
  7.2 10.4 %copy-start = (bf16[512,2048]{1,0:T(8,128)(2,1)S(1)}, bf16[512,2048]{1,0:T(8,128)(2,1)}, u32[]{:S(2)}) copy-start(bf16[512,2048]{1,0:T(8,128)(2,1)} %param.19) | copy-start | bytes 6291460
  7.2 216.2 %all-gather.2.cloned.1.call-start = ((), (), s32[]{:S(2)}) async-start(), calls=%async_computation.4 | async-start | bytes 13045760 | tf_op jit(solution)/shard_map/all_gather | solution.py:89
  16.8 0.8 copy-start.10
  16.8 11.8 %copy-start.7 = (s32[1,512]{1,0:T(1,128)S(1)}, s32[1,512]{1,0:T(1,128)}, u32[]{:S(2)}) copy-start(s32[1,512]{1,0:T(1,128)} %param.26) | copy-start | bytes 6148
  16.8 65.8 %copy-start.9 = (bf16[512,512]{1,0:T(8,128)(2,1)S(1)}, bf16[512,512]{1,0:T(8,128)(2,1)}, u32[]{:S(2)}) copy-start(bf16[512,512]{1,0:T(8,128)(2,1)} %param.17) | copy-start | bytes 1572868
  18.9 14.7 %collective-permute-start = (bf16[512,512]{1,0:T(8,128)(2,1)}, bf16[512,512]{1,0:T(8,128)(2,1)}, u32[]{:S(2)}, u32[]{:S(2)}) collective-permute-start(bf16[512,512]{1,0:T(8,128)(2,1)} %convolution_convert_fusion.3), channel_id=1, source_target_pairs={{0,1},{1,2},{2,3},{3,0},{4,5},{5,6},{6,7},{7,4},{8,9},{9,10},{10,1... | collective-permute-start | bytes 1572872 | tf_op jit(solution)/shard_map/ppermute | solution.py:46
  22.8 51.9 %collective-permute-start.1 = (bf16[512,512]{1,0:T(8,128)(2,1)}, bf16[512,512]{1,0:T(8,128)(2,1)}, u32[]{:S(2)}, u32[]{:S(2)}) collective-permute-start(bf16[512,512]{1,0:T(8,128)(2,1)} %convolution_convert_fusion.2), channel_id=1, source_target_pairs={{0,2},{1,3},{2,0},{3,1},{4,6},{5,7},{6,4},{7,5},{8,10},{9,11},{10,... | collective-permute-start | bytes 1572872 | tf_op jit(solution)/shard_map/ppermute | solution.py:46
  26.5 56.1 %collective-permute-start.2 = (bf16[512,512]{1,0:T(8,128)(2,1)}, bf16[512,512]{1,0:T(8,128)(2,1)}, u32[]{:S(2)}, u32[]{:S(2)}) collective-permute-start(bf16[512,512]{1,0:T(8,128)(2,1)} %convolution_convert_fusion.1), channel_id=1, source_target_pairs={{0,3},{1,0},{2,1},{3,2},{4,7},{5,4},{6,5},{7,6},{8,11},{9,8},{10,9... | collective-permute-start | bytes 1572872 | tf_op jit(solution)/shard_map/ppermute | solution.py:46
  150.8 0.8 copy-start.1
  153.5 41.3 %copy-start.8 = (s32[1,8]{1,0:T(1,128)S(1)}, s32[1,8]{1,0:T(1,128)}, u32[]{:S(2)}) copy-start(s32[1,8]{1,0:T(1,128)} %param.27) | copy-start | bytes 100
  153.6 27.3 %all-to-all-start.2 = ((bf16[4,256,512]{1,2,0:T(8,128)(2,1)}), bf16[4,256,512]{1,2,0:T(8,128)(2,1)S(1)}, u32[]{:S(2)}, u32[]{:S(2)}) async-start(bf16[4,256,512]{1,2,0:T(8,128)(2,1)} %broadcast_in_dim.65), calls=%async_computation.2 | async-start | bytes 2097152 | tf_op jit(solution)/shard_map/all_to_all | solution.py:130
  180.9 1.4 copy-start.3
  182.3 32.0 %all-to-all-start.1 = ((bf16[4,256,512]{1,2,0:T(8,128)(2,1)}), bf16[4,256,512]{1,2,0:T(8,128)(2,1)S(1)}, u32[]{:S(2)}, u32[]{:S(2)}) async-start(bf16[4,256,512]{1,2,0:T(8,128)(2,1)} %broadcast_in_dim.64), calls=%async_computation.1 | async-start | bytes 2097152 | tf_op jit(solution)/shard_map/all_to_all | solution.py:130
  196.3 25.7 %copy-start.6 = (f32[2048]{0:T(1024)S(1)}, f32[2048]{0:T(1024)}, u32[]{:S(2)}) copy-start(f32[2048]{0:T(1024)} %param.20) | copy-start | bytes 24580
  214.2 51.7 %all-to-all-start.3 = ((bf16[4,2,64,2,512]{4,1,3,2,0:T(2,128)(2,1)}), bf16[4,2,64,2,512]{4,1,3,2,0:T(2,128)(2,1)}, u32[]{:S(2)}, u32[]{:S(2)}) async-start(bf16[4,2,64,2,512]{4,1,3,2,0:T(2,128)(2,1)} %copy.47), calls=%async_computation.3 | async-start | bytes 2097152 | tf_op jit(solution)/shard_map/all_to_all | solution.py:133
  223.3 5.2 %copy-start.4 = (bf16[4,256,512]{1,2,0:T(8,128)(2,1)S(1)}, bf16[4,256,512]{1,2,0:T(8,128)(2,1)}, u32[]{:S(2)}) copy-start(bf16[4,256,512]{1,2,0:T(8,128)(2,1)} %copy-done.3) | copy-start | bytes 3145732
  241.9 24.0 %collective-permute-start.6 = (bf16[256,512]{1,0:T(8,128)(2,1)}, bf16[256,512]{1,0:T(8,128)(2,1)}, u32[]{:S(2)}, u32[]{:S(2)}) collective-permute-start(bf16[256,512]{1,0:T(8,128)(2,1)} %get-tuple-element.9), channel_id=1, source_target_pairs={{0,1},{1,2},{2,3},{3,0},{4,5},{5,6},{6,7},{7,4},{8,9},{9,10},{10,1... | collective-permute-start | bytes 786440 | tf_op jit(solution)/shard_map/ppermute | solution.py:60
  243.1 28.4 %collective-permute-start.7 = (bf16[256,512]{1,0:T(8,128)(2,1)}, bf16[256,512]{1,0:T(8,128)(2,1)}, u32[]{:S(2)}, u32[]{:S(2)}) collective-permute-start(bf16[256,512]{1,0:T(8,128)(2,1)} %get-tuple-element.11), channel_id=1, source_target_pairs={{0,2},{1,3},{2,0},{3,1},{4,6},{5,7},{6,4},{7,5},{8,10},{9,11},{10,... | collective-permute-start | bytes 786440 | tf_op jit(solution)/shard_map/ppermute | solution.py:60
  244.2 6.0 %copy-start.5 = (bf16[256,2048]{0,1:T(8,128)(2,1)S(1)}, bf16[256,2048]{0,1:T(8,128)(2,1)}, u32[]{:S(2)}) copy-start(bf16[256,2048]{0,1:T(8,128)(2,1)} %fusion.24) | copy-start | bytes 3145732
  244.2 33.4 %collective-permute-start.8 = (bf16[256,512]{1,0:T(8,128)(2,1)S(1)}, bf16[256,512]{1,0:T(8,128)(2,1)}, u32[]{:S(2)}, u32[]{:S(2)}) collective-permute-start(bf16[256,512]{1,0:T(8,128)(2,1)S(1)} %get-tuple-element.10), channel_id=1, source_target_pairs={{0,3},{1,0},{2,1},{3,2},{4,7},{5,4},{6,5},{7,6},{8,11},{9,8},{10,9... | collective-permute-start | bytes 786440 | tf_op jit(solution)/shard_map/ppermute | solution.py:60
  260.7 30.2 %copy-start.2 = (bf16[64,8,512]{2,1,0:T(8,128)(2,1)S(1)}, bf16[64,8,512]{2,1,0:T(8,128)(2,1)}, u32[]{:S(2)}) copy-start(bf16[64,8,512]{2,1,0:T(8,128)(2,1)} %copy-done.1) | copy-start | bytes 1572868
  262.6 20.6 %collective-permute-start.3 = (bf16[256,512]{1,0:T(8,128)(2,1)}, bf16[256,512]{1,0:T(8,128)(2,1)}, u32[]{:S(2)}, u32[]{:S(2)}) collective-permute-start(bf16[256,512]{1,0:T(8,128)(2,1)} %get-tuple-element.6), channel_id=1, source_target_pairs={{0,1},{1,2},{2,3},{3,0},{4,5},{5,6},{6,7},{7,4},{8,9},{9,10},{10,1... | collective-permute-start | bytes 786440 | tf_op jit(solution)/shard_map/ppermute | solution.py:60
  262.9 25.9 %collective-permute-start.4 = (bf16[256,512]{1,0:T(8,128)(2,1)S(1)}, bf16[256,512]{1,0:T(8,128)(2,1)}, u32[]{:S(2)}, u32[]{:S(2)}) collective-permute-start(bf16[256,512]{1,0:T(8,128)(2,1)S(1)} %get-tuple-element.8), channel_id=1, source_target_pairs={{0,2},{1,3},{2,0},{3,1},{4,6},{5,7},{6,4},{7,5},{8,10},{9,11},{10,... | collective-permute-start | bytes 786440 | tf_op jit(solution)/shard_map/ppermute | solution.py:60
  265.9 25.0 %collective-permute-start.5 = (bf16[256,512]{1,0:T(8,128)(2,1)S(1)}, bf16[256,512]{1,0:T(8,128)(2,1)}, u32[]{:S(2)}, u32[]{:S(2)}) collective-permute-start(bf16[256,512]{1,0:T(8,128)(2,1)S(1)} %get-tuple-element.7), channel_id=1, source_target_pairs={{0,3},{1,0},{2,1},{3,2},{4,7},{5,4},{6,5},{7,6},{8,11},{9,8},{10,9... | collective-permute-start | bytes 786440 | tf_op jit(solution)/shard_map/ppermute | solution.py:60
Sparse Core Ops, SparseCore 0:
  11.6 176.9 all-gather.1
